TPU v7x, 128 devices: a whole 4x4x4 slice. The times are simulated.
128 devices in a mesh: cam: 8 (over x, core), tile: 16 (over y, z).
Axes of the slice: x: 4, y: 4, z: 4, core: 2. Of those that a mesh axis runs over, the one named last changes fastest.
Arguments:
- depth_weights: bfloat16 [512, 16, 64, 128], P(('cam', 'tile')), may hold values from 0.049804688 to 1
- context: bfloat16 [512, 16, 128, 128], P(('cam', 'tile')), may hold values from -1.5 to 1.5
- block_owner: int32 [512, 16, 1], P(('cam', 'tile')), may hold values from 0 to 127; in each aligned block of 64 rows (0 to 63, 64 to 127, ..., all dimensions but the last counted through in order) at most 2 rows name the same one
- block_local: int32 [512, 16], P(('cam', 'tile')), may hold values from 0 to 15
- block_cell: int32 [512, 16, 64], P(('cam', 'tile')), may hold values from 0 to 255
- conv_weight: bfloat16 [4, 3, 3, 128, 128], replicated, may hold values from -0.25 to 0.25
- cotangent: bfloat16 [128, 4096, 128], P('cam', 'tile'), may hold values from -6 to 6
Outputs:
- bev_out: bfloat16 [128, 4096, 128], P('cam', 'tile')
- grad_depth: bfloat16 [512, 16, 64, 128], P(('cam', 'tile'))
- grad_context: bfloat16 [512, 16, 128, 128], P(('cam', 'tile'))
Inputs may be any that keep to these rules, and one draw needn't show every extreme that they name: `block_owner`: among the blocks of the cameras of one device (aligned groups of 4 cameras) no owner is named by more than 2 blocks, a bound that some block reaches.
All inputs are finite; a program needn't handle non-finite values.
Results may differ from a plain program's by a relative error of at most 0.02.
Values may be sent and summed in bfloat16 or wider, within the bound.
No kernel may reach another device: no remote copies, remote signals or barrier semaphores. Data moves between devices by JAX's collectives and lax.ppermute only.
A program may use at most 128 MiB of HBM per device.

v0:
```python
import jax
import jax.numpy as jnp
from jax import lax
from jax.sharding import PartitionSpec as P

TS = 16
LAYERS = 4


def extended(cells, sides, width):
    for axis, dim in sides:
        count = lax.axis_size(axis)
        ends = count - 1
        head = lax.slice_in_dim(cells, 0, width, axis=dim)
        tail = lax.slice_in_dim(cells, cells.shape[dim] - width, cells.shape[dim], axis=dim)
        cells = jnp.concatenate(
            [
                lax.ppermute(tail, axis, [(i, (i + 1) % count) for i in range(ends)]),
                cells,
                lax.ppermute(head, axis, [((i + 1) % count, i) for i in range(ends)]),
            ],
            axis=dim,
        )
    return cells


def silu_slope(preact):
    sigma = jax.nn.sigmoid(preact)
    return sigma * (1.0 + preact * (1.0 - sigma))


def conv_taps(padded, kernel, flipped):
    rows_out = padded.shape[0] - 2
    cols_out = padded.shape[1] - 2
    total = jnp.zeros((rows_out, cols_out, kernel.shape[3]), jnp.float32)
    for row_tap in range(3):
        for col_tap in range(3):
            window = padded[row_tap : row_tap + rows_out, col_tap : col_tap + cols_out]
            if flipped:
                total = total + jnp.einsum(
                    "xyo,io->xyi",
                    window,
                    kernel[2 - row_tap, 2 - col_tap],
                    preferred_element_type=jnp.float32,
                )
            else:
                total = total + jnp.einsum(
                    "xyi,io->xyo",
                    window,
                    kernel[row_tap, col_tap],
                    preferred_element_type=jnp.float32,
                )
    return total


def per_device(
    depth_weights, context, block_owner, block_local, block_cell, conv_weight, cotangent
):
    cams_here, blocks_cam, bins, pixels = depth_weights.shape
    channels = context.shape[3]
    rows_here = cotangent.shape[0]
    cols_here = cotangent.shape[1]
    cam_devices = lax.axis_size("cam")
    tile_devices = lax.axis_size("tile")
    owner_count = cam_devices * tile_devices
    blocks_here = cams_here * blocks_cam
    capacity = max(2, 2 * blocks_here // owner_count)
    slots_total = owner_count * capacity
    flat_depth = depth_weights.reshape(blocks_here, bins, pixels)
    flat_context = context.reshape(blocks_here, pixels, channels)
    lifted = jnp.einsum(
        "bdp,bpc->bdc", flat_depth, flat_context, preferred_element_type=jnp.float32
    ).astype(jnp.bfloat16)
    owner_ids = block_owner.reshape(blocks_here)
    positions = jnp.arange(blocks_here, dtype=jnp.int32)
    earlier_same = (owner_ids[:, None] == owner_ids[None, :]) & (
        positions[None, :] < positions[:, None]
    )
    rank_within = jnp.sum(earlier_same.astype(jnp.int32), axis=1)
    slot_index = owner_ids * capacity + rank_within
    tiles_across = cols_here // TS
    tiles_down = rows_here // TS
    tile_count = tiles_across * tiles_down
    tile_cells = TS * TS
    local_ids = block_local.reshape(blocks_here)
    cell_ids = block_cell.reshape(blocks_here, bins)
    row_start = local_ids // tiles_across * TS
    col_start = local_ids % tiles_across * TS
    region_cell = (
        (row_start[:, None] + cell_ids // TS) * cols_here + col_start[:, None] + cell_ids % TS
    )
    send_rows = jnp.zeros((slots_total, bins, channels), jnp.bfloat16).at[slot_index].set(lifted)
    send_cells = jnp.zeros((slots_total, bins), jnp.int32).at[slot_index].set(region_cell)
    recv_rows, recv_cells = (
        lax.all_to_all(send_rows, ("cam", "tile"), split_axis=0, concat_axis=0, tiled=True),
        lax.all_to_all(send_cells, ("cam", "tile"), split_axis=0, concat_axis=0, tiled=True),
    )
    cell_row = recv_cells // cols_here
    cell_col = recv_cells % cols_here
    within_tile = cell_row % TS * TS + cell_col % TS
    slot_tile = cell_row[:, 0] // TS * tiles_across + cell_col[:, 0] // TS
    cell_onehot = (
        jnp.arange(tile_cells, dtype=jnp.int32)[None, :, None] == within_tile[:, None, :]
    ).astype(jnp.bfloat16)
    tile_onehot = jnp.arange(tile_count, dtype=jnp.int32)[:, None] == slot_tile[None, :]
    slot_sums = jnp.einsum(
        "sed,sdc->sec", cell_onehot, recv_rows, preferred_element_type=jnp.float32
    )
    tile_sums = jnp.einsum(
        "ts,sec->tec", tile_onehot.astype(jnp.float32), slot_sums, precision=lax.Precision.HIGHEST
    )
    tile_grid = tile_sums.reshape(tiles_down, tiles_across, TS, TS, channels).transpose(
        0, 2, 1, 3, 4
    )
    activation = tile_grid.reshape(rows_here, cols_here, channels).astype(jnp.bfloat16)
    stored = []
    for layer in range(LAYERS):
        padded = extended(activation, (("cam", 0), ("tile", 1)), 1)
        preact = conv_taps(padded, conv_weight[layer], False)
        stored.append(preact)
        activation = jax.nn.silu(preact).astype(jnp.bfloat16)
    gradient = cotangent
    for layer in range(LAYERS - 1, -1, -1):
        grad_pre = (gradient.astype(jnp.float32) * silu_slope(stored[layer])).astype(jnp.bfloat16)
        padded_grad = extended(grad_pre, (("cam", 0), ("tile", 1)), 1)
        gradient = conv_taps(padded_grad, conv_weight[layer], True).astype(jnp.bfloat16)
    grad_tiles = (
        gradient.reshape(tiles_down, TS, tiles_across, TS, channels)
        .transpose(0, 2, 1, 3, 4)
        .reshape(tile_count, tile_cells, channels)
    )
    slot_grad = jnp.einsum(
        "ts,tec->sec",
        tile_onehot.astype(jnp.bfloat16),
        grad_tiles,
        preferred_element_type=jnp.float32,
    ).astype(jnp.bfloat16)
    grad_rows = jnp.einsum(
        "sed,sec->sdc", cell_onehot, slot_grad, preferred_element_type=jnp.float32
    ).astype(jnp.bfloat16)
    returned = lax.all_to_all(grad_rows, ("cam", "tile"), split_axis=0, concat_axis=0, tiled=True)
    block_grad = returned[slot_index]
    grad_context = jnp.einsum(
        "bdp,bdc->bpc", flat_depth, block_grad, preferred_element_type=jnp.float32
    ).astype(jnp.bfloat16)
    grad_depth = jnp.einsum(
        "bdc,bpc->bdp", block_grad, flat_context, preferred_element_type=jnp.float32
    ).astype(jnp.bfloat16)
    return (
        activation,
        grad_depth.reshape(depth_weights.shape),
        grad_context.reshape(context.shape),
    )


def solution(mesh):
    placed = (
        P(("cam", "tile"), None, None, None),
        P(("cam", "tile"), None, None, None),
        P(("cam", "tile"), None, None),
        P(("cam", "tile"), None),
        P(("cam", "tile"), None, None),
        P(),
        P("cam", "tile", None),
    )
    return jax.shard_map(
        per_device,
        mesh=mesh,
        in_specs=placed,
        out_specs=(
            P("cam", "tile", None),
            P(("cam", "tile"), None, None, None),
            P(("cam", "tile"), None, None, None),
        ),
        check_vma=False,
    )
```

profile of v0, /device:TPU:6, one launch (start us, length us, event | category | flops | bytes accessed | tf_op | source)
XLA Modules:
  0.0 445.4 jit_solution(17762314704547502250)
XLA Ops:
  7.0 10.5 %all-to-all-start = ((s32[128,1,128]{2,1,0:T(1,128)}), s32[128,1,128]{2,1,0:T(1,128)S(1)}, u32[]{:S(2)}, u32[]{:S(2)}) async-start(s32[128,1,128]{2,1,0:T(1,128)} %reshape.339), calls=%async_computation | async-start | bytes 131072 | tf_op jit(solution)/shard_map/all_to_all | solution.py:96
  22.5 8.1 %scatter_fusion = bf16[256,64,128]{2,1,0:T(8,128)(2,1)} fusion(bf16[256,64,128]{2,1,0:T(8,128)(2,1)} %broadcast_in_dim.5, s32[64]{0:T(128)S(1)} %fusion.235, bf16[64,64,128]{2,1,0:T(8,128)(2,1)S(1)} %convolution_convert_fusion.3), kind=kCustom, calls=%fused_computation.2 | custom fusion | bytes 3145984 | tf_op jit(solution)/shard_map/scatter | solution.py:92
  30.6 10.2 %all-to-all-start.1 = ((bf16[256,64,128]{2,1,0:T(8,128)(2,1)}), bf16[256,64,128]{2,1,0:T(8,128)(2,1)}, u32[]{:S(2)}, u32[]{:S(2)}) async-start(bf16[256,64,128]{2,1,0:T(8,128)(2,1)} %scatter_fusion), calls=%async_computation.1 | async-start | bytes 8388608 | tf_op jit(solution)/shard_map/all_to_all | solution.py:95
  44.9 49.1 %all-to-all-done.1 = bf16[256,64,128]{2,1,0:T(8,128)(2,1)} async-done(((bf16[256,64,128]{2,1,0:T(8,128)(2,1)}), bf16[256,64,128]{2,1,0:T(8,128)(2,1)}, u32[]{:S(2)}, u32[]{:S(2)}) %all-to-all-start.1) | async-done | bytes 4194336 | tf_op jit(solution)/shard_map/all_to_all | solution.py:95
  94.1 17.2 %fusion.4 = f32[256,256,128]{2,1,0:T(8,128)} fusion(bf16[256,64,128]{2,1,0:T(8,128)(2,1)} %all-to-all-done.1, s32[256,64]{1,0:T(8,128)S(1)} %get-tuple-element.72), kind=kOutput, calls=%fused_computation.8 | convolution fusion | flops 1077936128 | bytes 37814272 | tf_op jit(solution)/shard_map/sed,sdc->sec/dot_general | solution.py:106
  111.3 44.9 %fusion.10 = bf16[16,256,128]{2,0,1:T(8,128)(2,1)S(1)} fusion(f32[256,256,128]{2,1,0:T(8,128)} %fusion.4, s32[256]{0:T(256)S(1)} %fusion.233), kind=kOutput, calls=%fused_computation.34 | convolution fusion | flops 1611141120 | bytes 34604032 | tf_op jit(solution)/shard_map/ts,sec->tec/dot_general | solution.py:109
  158.5 3.6 collective-permute-start.1
  177.4 3.6 collective-permute-start.5
  196.6 3.6 collective-permute-start.9
  202.1 5.9 %collective-permute-start.10 = (bf16[18,1,128]{2,1,0:T(2,128)(2,1)S(1)}, bf16[18,1,128]{2,1,0:T(2,128)(2,1)S(1)}, u32[]{:S(2)}, u32[]{:S(2)}) collective-permute-start(bf16[18,1,128]{2,1,0:T(2,128)(2,1)S(1)} %get-tuple-element.46), channel_id=1, source_target_pairs={{0,1},{1,2},{2,3},{3,4},{4,5},{5,6},{6,7},{7,8},{8,9},{9,10},{10,1... | collective-permute-start | bytes 13832 | tf_op jit(solution)/shard_map/ppermute | solution.py:18
  219.7 3.6 collective-permute-start.13
  225.3 4.0 collective-permute-start.14
  243.0 3.6 collective-permute-start.17
  248.5 4.0 collective-permute-start.18
  264.5 3.6 collective-permute-start.21
  270.0 4.0 collective-permute-start.22
  286.0 3.6 collective-permute-start.25
  291.6 4.0 collective-permute-start.26
  313.1 4.0 collective-permute-start.30
  326.9 4.8 %convolution_convert_fusion = bf16[256,256,128]{2,0,1:T(8,128)(2,1)S(1)} fusion(bf16[16,256,128]{2,1,0:T(8,128)(2,1)S(1)} %bitcast.297, s32[256]{0:T(256)S(1)} %fusion.233), kind=kOutput, calls=%fused_computation.9 | convolution fusion | flops 276828160 | bytes 17826816 | tf_op jit(solution)/shard_map/ts,tec->sec/dot_general | solution.py:132
  331.7 37.0 %fusion.7 = bf16[256,64,128]{2,1,0:T(8,128)(2,1)} fusion(bf16[256,256,128]{2,0,1:T(8,128)(2,1)S(1)} %convolution_convert_fusion, s32[256,64]{1,0:T(8,128)S(1)} %copy-done.6), kind=kOutput, calls=%fused_computation.12 | convolution fusion | flops 1080033280 | bytes 21037056 | tf_op jit(solution)/shard_map/sed,sec->sdc/dot_general | solution.py:138
  368.6 10.6 %all-to-all-start.2 = ((bf16[256,64,128]{2,1,0:T(8,128)(2,1)}), bf16[256,64,128]{2,1,0:T(8,128)(2,1)}, u32[]{:S(2)}, u32[]{:S(2)}) async-start(bf16[256,64,128]{2,1,0:T(8,128)(2,1)} %fusion.7), calls=%async_computation.2 | async-start | bytes 8388608 | tf_op jit(solution)/shard_map/all_to_all | solution.py:141
  379.3 53.2 %all-to-all-done.2 = bf16[256,64,128]{2,1,0:T(8,128)(2,1)} async-done(((bf16[256,64,128]{2,1,0:T(8,128)(2,1)}), bf16[256,64,128]{2,1,0:T(8,128)(2,1)}, u32[]{:S(2)}, u32[]{:S(2)}) %all-to-all-start.2) | async-done | bytes 4194336 | tf_op jit(solution)/shard_map/all_to_all | solution.py:141
  441.3 3.9 copy.39
  (195 shorter events, 142.5 us)
Async XLA Ops:
  7.0 23.6 %all-to-all-start = ((s32[128,1,128]{2,1,0:T(1,128)}), s32[128,1,128]{2,1,0:T(1,128)S(1)}, u32[]{:S(2)}, u32[]{:S(2)}) async-start(s32[128,1,128]{2,1,0:T(1,128)} %reshape.339), calls=%async_computation | async-start | bytes 131072 | tf_op jit(solution)/shard_map/all_to_all | solution.py:96
  30.6 63.5 %all-to-all-start.1 = ((bf16[256,64,128]{2,1,0:T(8,128)(2,1)}), bf16[256,64,128]{2,1,0:T(8,128)(2,1)}, u32[]{:S(2)}, u32[]{:S(2)}) async-start(bf16[256,64,128]{2,1,0:T(8,128)(2,1)} %scatter_fusion), calls=%async_computation.1 | async-start | bytes 8388608 | tf_op jit(solution)/shard_map/all_to_all | solution.py:95
  156.5 6.0 %collective-permute-start = (bf16[1,256,128]{2,1,0:T(8,128)(2,1)S(1)}, bf16[1,256,128]{2,1,0:T(8,128)(2,1)S(1)}, u32[]{:S(2)}, u32[]{:S(2)}) collective-permute-start(bf16[1,256,128]{2,1,0:T(8,128)(2,1)S(1)} %bitcast.307), channel_id=1, source_target_pairs={{0,16},{16,32},{32,48},{48,64},{64,80},{80,96},{96,112},{1,17},{17... | collective-permute-start | bytes 196616 | tf_op jit(solution)/shard_map/ppermute | solution.py:18
  165.7 5.6 %collective-permute-start.3 = (bf16[18,1,128]{2,1,0:T(2,128)(2,1)S(1)}, bf16[18,1,128]{2,1,0:T(2,128)(2,1)S(1)}, u32[]{:S(2)}, u32[]{:S(2)}) collective-permute-start(bf16[18,1,128]{2,1,0:T(2,128)(2,1)S(1)} %get-tuple-element.53), channel_id=1, source_target_pairs={{1,0},{2,1},{3,2},{4,3},{5,4},{6,5},{7,6},{8,7},{9,8},{10,9},{11,1... | collective-permute-start | bytes 13832 | tf_op jit(solution)/shard_map/ppermute | solution.py:20
  175.4 6.0 %collective-permute-start.4 = (bf16[1,256,128]{2,1,0:T(8,128)(2,1)S(1)}, bf16[1,256,128]{2,1,0:T(8,128)(2,1)S(1)}, u32[]{:S(2)}, u32[]{:S(2)}) collective-permute-start(bf16[1,256,128]{2,1,0:T(8,128)(2,1)S(1)} %get-tuple-element.67), channel_id=1, source_target_pairs={{0,16},{16,32},{32,48},{48,64},{64,80},{80,96},{96,112},{1,17},{17... | collective-permute-start | bytes 196616 | tf_op jit(solution)/shard_map/ppermute | solution.py:18
  184.9 5.6 %collective-permute-start.7 = (bf16[18,1,128]{2,1,0:T(2,128)(2,1)S(1)}, bf16[18,1,128]{2,1,0:T(2,128)(2,1)S(1)}, u32[]{:S(2)}, u32[]{:S(2)}) collective-permute-start(bf16[18,1,128]{2,1,0:T(2,128)(2,1)S(1)} %get-tuple-element.49), channel_id=1, source_target_pairs={{1,0},{2,1},{3,2},{4,3},{5,4},{6,5},{7,6},{8,7},{9,8},{10,9},{11,1... | collective-permute-start | bytes 13832 | tf_op jit(solution)/shard_map/ppermute | solution.py:20
  194.6 6.0 %collective-permute-start.8 = (bf16[1,256,128]{2,1,0:T(8,128)(2,1)S(1)}, bf16[1,256,128]{2,1,0:T(8,128)(2,1)S(1)}, u32[]{:S(2)}, u32[]{:S(2)}) collective-permute-start(bf16[1,256,128]{2,1,0:T(8,128)(2,1)S(1)} %get-tuple-element.65), channel_id=1, source_target_pairs={{0,16},{16,32},{32,48},{48,64},{64,80},{80,96},{96,112},{1,17},{17... | collective-permute-start | bytes 196616 | tf_op jit(solution)/shard_map/ppermute | solution.py:18
  202.1 8.2 %collective-permute-start.10 = (bf16[18,1,128]{2,1,0:T(2,128)(2,1)S(1)}, bf16[18,1,128]{2,1,0:T(2,128)(2,1)S(1)}, u32[]{:S(2)}, u32[]{:S(2)}) collective-permute-start(bf16[18,1,128]{2,1,0:T(2,128)(2,1)S(1)} %get-tuple-element.46), channel_id=1, source_target_pairs={{0,1},{1,2},{2,3},{3,4},{4,5},{5,6},{6,7},{7,8},{8,9},{9,10},{10,1... | collective-permute-start | bytes 13832 | tf_op jit(solution)/shard_map/ppermute | solution.py:18
  208.0 5.6 %collective-permute-start.11 = (bf16[18,1,128]{2,1,0:T(2,128)(2,1)S(1)}, bf16[18,1,128]{2,1,0:T(2,128)(2,1)S(1)}, u32[]{:S(2)}, u32[]{:S(2)}) collective-permute-start(bf16[18,1,128]{2,1,0:T(2,128)(2,1)S(1)} %get-tuple-element.45), channel_id=1, source_target_pairs={{1,0},{2,1},{3,2},{4,3},{5,4},{6,5},{7,6},{8,7},{9,8},{10,9},{11,1... | collective-permute-start | bytes 13832 | tf_op jit(solution)/shard_map/ppermute | solution.py:20
  217.8 6.0 %collective-permute-start.12 = (bf16[1,256,128]{2,1,0:T(8,128)(2,1)S(1)}, bf16[1,256,128]{2,1,0:T(8,128)(2,1)S(1)}, u32[]{:S(2)}, u32[]{:S(2)}) collective-permute-start(bf16[1,256,128]{2,1,0:T(8,128)(2,1)S(1)} %get-tuple-element.63), channel_id=1, source_target_pairs={{0,16},{16,32},{32,48},{48,64},{64,80},{80,96},{96,112},{1,17},{17... | collective-permute-start | bytes 196616 | tf_op jit(solution)/shard_map/ppermute | solution.py:18
  225.3 6.2 %collective-permute-start.14 = (bf16[18,1,128]{2,1,0:T(2,128)(2,1)S(1)}, bf16[18,1,128]{2,1,0:T(2,128)(2,1)S(1)}, u32[]{:S(2)}, u32[]{:S(2)}) collective-permute-start(bf16[18,1,128]{2,1,0:T(2,128)(2,1)S(1)} %get-tuple-element.38), channel_id=1, source_target_pairs={{0,1},{1,2},{2,3},{3,4},{4,5},{5,6},{6,7},{7,8},{8,9},{9,10},{10,1... | collective-permute-start | bytes 13832 | tf_op jit(solution)/shard_map/ppermute | solution.py:18
  229.3 5.6 %collective-permute-start.15 = (bf16[18,1,128]{2,1,0:T(2,128)(2,1)S(1)}, bf16[18,1,128]{2,1,0:T(2,128)(2,1)S(1)}, u32[]{:S(2)}, u32[]{:S(2)}) collective-permute-start(bf16[18,1,128]{2,1,0:T(2,128)(2,1)S(1)} %get-tuple-element.37), channel_id=1, source_target_pairs={{1,0},{2,1},{3,2},{4,3},{5,4},{6,5},{7,6},{8,7},{9,8},{10,9},{11,1... | collective-permute-start | bytes 13832 | tf_op jit(solution)/shard_map/ppermute | solution.py:20
  241.1 6.0 %collective-permute-start.16 = (bf16[1,256,128]{2,1,0:T(8,128)(2,1)S(1)}, bf16[1,256,128]{2,1,0:T(8,128)(2,1)S(1)}, u32[]{:S(2)}, u32[]{:S(2)}) collective-permute-start(bf16[1,256,128]{2,1,0:T(8,128)(2,1)S(1)} %get-tuple-element.61), channel_id=1, source_target_pairs={{0,16},{16,32},{32,48},{48,64},{64,80},{80,96},{96,112},{1,17},{17... | collective-permute-start | bytes 196616 | tf_op jit(solution)/shard_map/ppermute | solution.py:18
  248.5 6.7 %collective-permute-start.18 = (bf16[18,1,128]{2,1,0:T(2,128)(2,1)S(1)}, bf16[18,1,128]{2,1,0:T(2,128)(2,1)S(1)}, u32[]{:S(2)}, u32[]{:S(2)}) collective-permute-start(bf16[18,1,128]{2,1,0:T(2,128)(2,1)S(1)} %get-tuple-element.34), channel_id=1, source_target_pairs={{0,1},{1,2},{2,3},{3,4},{4,5},{5,6},{6,7},{7,8},{8,9},{9,10},{10,1... | collective-permute-start | bytes 13832 | tf_op jit(solution)/shard_map/ppermute | solution.py:18
  262.6 6.0 %collective-permute-start.20 = (bf16[1,256,128]{2,1,0:T(8,128)(2,1)S(1)}, bf16[1,256,128]{2,1,0:T(8,128)(2,1)S(1)}, u32[]{:S(2)}, u32[]{:S(2)}) collective-permute-start(bf16[1,256,128]{2,1,0:T(8,128)(2,1)S(1)} %get-tuple-element.59), channel_id=1, source_target_pairs={{0,16},{16,32},{32,48},{48,64},{64,80},{80,96},{96,112},{1,17},{17... | collective-permute-start | bytes 196616 | tf_op jit(solution)/shard_map/ppermute | solution.py:18
  270.0 6.2 %collective-permute-start.22 = (bf16[18,1,128]{2,1,0:T(2,128)(2,1)S(1)}, bf16[18,1,128]{2,1,0:T(2,128)(2,1)S(1)}, u32[]{:S(2)}, u32[]{:S(2)}) collective-permute-start(bf16[18,1,128]{2,1,0:T(2,128)(2,1)S(1)} %get-tuple-element.30), channel_id=1, source_target_pairs={{0,1},{1,2},{2,3},{3,4},{4,5},{5,6},{6,7},{7,8},{8,9},{9,10},{10,1... | collective-permute-start | bytes 13832 | tf_op jit(solution)/shard_map/ppermute | solution.py:18
  274.1 5.6 %collective-permute-start.23 = (bf16[18,1,128]{2,1,0:T(2,128)(2,1)S(1)}, bf16[18,1,128]{2,1,0:T(2,128)(2,1)S(1)}, u32[]{:S(2)}, u32[]{:S(2)}) collective-permute-start(bf16[18,1,128]{2,1,0:T(2,128)(2,1)S(1)} %get-tuple-element.29), channel_id=1, source_target_pairs={{1,0},{2,1},{3,2},{4,3},{5,4},{6,5},{7,6},{8,7},{9,8},{10,9},{11,1... | collective-permute-start | bytes 13832 | tf_op jit(solution)/shard_map/ppermute | solution.py:20
  284.1 6.0 %collective-permute-start.24 = (bf16[1,256,128]{2,1,0:T(8,128)(2,1)S(1)}, bf16[1,256,128]{2,1,0:T(8,128)(2,1)S(1)}, u32[]{:S(2)}, u32[]{:S(2)}) collective-permute-start(bf16[1,256,128]{2,1,0:T(8,128)(2,1)S(1)} %get-tuple-element.57), channel_id=1, source_target_pairs={{0,16},{16,32},{32,48},{48,64},{64,80},{80,96},{96,112},{1,17},{17... | collective-permute-start | bytes 196616 | tf_op jit(solution)/shard_map/ppermute | solution.py:18
  291.6 6.2 %collective-permute-start.26 = (bf16[18,1,128]{2,1,0:T(2,128)(2,1)S(1)}, bf16[18,1,128]{2,1,0:T(2,128)(2,1)S(1)}, u32[]{:S(2)}, u32[]{:S(2)}) collective-permute-start(bf16[18,1,128]{2,1,0:T(2,128)(2,1)S(1)} %get-tuple-element.26), channel_id=1, source_target_pairs={{0,1},{1,2},{2,3},{3,4},{4,5},{5,6},{6,7},{7,8},{8,9},{9,10},{10,1... | collective-permute-start | bytes 13832 | tf_op jit(solution)/shard_map/ppermute | solution.py:18
  295.6 5.6 %collective-permute-start.27 = (bf16[18,1,128]{2,1,0:T(2,128)(2,1)S(1)}, bf16[18,1,128]{2,1,0:T(2,128)(2,1)S(1)}, u32[]{:S(2)}, u32[]{:S(2)}) collective-permute-start(bf16[18,1,128]{2,1,0:T(2,128)(2,1)S(1)} %get-tuple-element.25), channel_id=1, source_target_pairs={{1,0},{2,1},{3,2},{4,3},{5,4},{6,5},{7,6},{8,7},{9,8},{10,9},{11,1... | collective-permute-start | bytes 13832 | tf_op jit(solution)/shard_map/ppermute | solution.py:20
  305.6 6.0 %collective-permute-start.28 = (bf16[1,256,128]{2,1,0:T(8,128)(2,1)S(1)}, bf16[1,256,128]{2,1,0:T(8,128)(2,1)S(1)}, u32[]{:S(2)}, u32[]{:S(2)}) collective-permute-start(bf16[1,256,128]{2,1,0:T(8,128)(2,1)S(1)} %get-tuple-element.55), channel_id=1, source_target_pairs={{0,16},{16,32},{32,48},{48,64},{64,80},{80,96},{96,112},{1,17},{17... | collective-permute-start | bytes 196616 | tf_op jit(solution)/shard_map/ppermute | solution.py:18
  313.1 6.4 %collective-permute-start.30 = (bf16[18,1,128]{2,1,0:T(2,128)(2,1)S(1)}, bf16[18,1,128]{2,1,0:T(2,128)(2,1)S(1)}, u32[]{:S(2)}, u32[]{:S(2)}) collective-permute-start(bf16[18,1,128]{2,1,0:T(2,128)(2,1)S(1)} %get-tuple-element.22), channel_id=1, source_target_pairs={{0,1},{1,2},{2,3},{3,4},{4,5},{5,6},{6,7},{7,8},{8,9},{9,10},{10,1... | collective-permute-start | bytes 13832 | tf_op jit(solution)/shard_map/ppermute | solution.py:18
  317.1 5.6 %collective-permute-start.31 = (bf16[18,1,128]{2,1,0:T(2,128)(2,1)S(1)}, bf16[18,1,128]{2,1,0:T(2,128)(2,1)S(1)}, u32[]{:S(2)}, u32[]{:S(2)}) collective-permute-start(bf16[18,1,128]{2,1,0:T(2,128)(2,1)S(1)} %get-tuple-element.21), channel_id=1, source_target_pairs={{1,0},{2,1},{3,2},{4,3},{5,4},{6,5},{7,6},{8,7},{9,8},{10,9},{11,1... | collective-permute-start | bytes 13832 | tf_op jit(solution)/shard_map/ppermute | solution.py:20
  368.6 63.8 %all-to-all-start.2 = ((bf16[256,64,128]{2,1,0:T(8,128)(2,1)}), bf16[256,64,128]{2,1,0:T(8,128)(2,1)}, u32[]{:S(2)}, u32[]{:S(2)}) async-start(bf16[256,64,128]{2,1,0:T(8,128)(2,1)} %fusion.7), calls=%async_computation.2 | async-start | bytes 8388608 | tf_op jit(solution)/shard_map/all_to_all | solution.py:141
  (20 other events, 178.6 us)
where the time goes:
time: 452 us; the launch traced here: 445 us
  matrix products  152 us (34%)
  waiting for transfers between devices  140 us (31%)
  starting transfers between devices  117 us (26%)
  local copies, waits for them, and re-layouts  24.8 us (5%)
  other arithmetic  10.5 us (2%)
    all_to_all x1, waiting for transfers between devices, per_device(): lax.all_to_all(grad_rows, ('cam', 'tile'), split_axis=0, concat_axis=0, t...  53.2 us
    all_to_all x1, waiting for transfers between devices, per_device(): lax.all_to_all(send_rows, ('cam', 'tile'), split_axis=0, concat_axis=0, t...  49.1 us
    dot_general x1, matrix products, per_device(): jnp.einsum('ts,sec->tec', tile_onehot.astype(jnp.float32), slot_sums, pre...  44.9 us
    ppermute x16, starting transfers between devices, extended(): lax.ppermute(tail, axis, [(i, (i + 1) % count) for i in range(ends)])  44.9 us
    ppermute x16, starting transfers between devices, extended(): lax.ppermute(head, axis, [((i + 1) % count, i) for i in range(ends)])  40.3 us
    ppermute x16, waiting for transfers between devices, extended(): lax.ppermute(head, axis, [((i + 1) % count, i) for i in range(ends)])  37.9 us
    dot_general x1, matrix products, per_device(): jnp.einsum('sed,sec->sdc', cell_onehot, slot_grad, preferred_element_type...  37 us
    dot_general x36, matrix products, conv_taps(): jnp.einsum('xyi,io->xyo', window, kernel[row_tap, col_tap], preferred_ele...  20.2 us
  transfers between devices with their start and end apart: 35, of which 18 were waited for; matrix products, arithmetic and copies ran while one was open for 6% of the time, Pallas kernels for 0%

commit v1 on v0

v1 whole, which is shorter than its diff:
```python
import jax
import jax.numpy as jnp
from jax import lax
from jax.experimental import pallas as pl
from jax.experimental.pallas import tpu as pltpu
from jax.sharding import PartitionSpec as P

TS = 16
LAYERS = 4
EXT = 2 * LAYERS
EMPTY = 256.0
BF = jnp.bfloat16
F32 = jnp.float32


def ring(axis):
    count = lax.axis_size(axis)
    ends = count - 1
    down = [(i, i + 1) for i in range(ends)]
    up = [(i + 1, i) for i in range(ends)]
    return down, up


def with_sides(cells, axis, dim, width):
    down, up = ring(axis)
    size = cells.shape[dim]
    head = lax.slice_in_dim(cells, 0, width, axis=dim)
    tail = lax.slice_in_dim(cells, size - width, size, axis=dim)
    return jnp.concatenate(
        [lax.ppermute(tail, axis, down), cells, lax.ppermute(head, axis, up)], axis=dim
    )


def take_slot(owner, count):
    rank = count[owner]
    count[owner] = rank + 1
    return rank


def clear_counts(count, size):
    @pl.loop(0, size)
    def _(i):
        count[i] = 0


def pack_kernel(owner, local, cells, depth, context, out, count, meta):
    owners, rows, width = out.shape
    bins = depth.shape[1]
    clear_counts(count, owners)
    out[...] = jnp.zeros(out.shape, BF)
    kind = lax.broadcasted_iota(jnp.int32, meta.shape, 1)
    meta[...] = jnp.where(kind == 0, EMPTY, 0.0)
    lane = lax.broadcasted_iota(jnp.int32, (1, width), 1)

    def block(b, carry):
        to = owner[b]
        rank = take_slot(to, count)
        lifted = jnp.dot(depth[b], context[b], preferred_element_type=F32)
        out[to, pl.ds(pl.multiple_of(rank * bins, bins), bins), :] = lifted.astype(BF)
        mine = (lane // bins) == rank
        meta[to, pl.ds(0, 1), :] = jnp.where(mine, cells[b], meta[to, pl.ds(0, 1), :])
        tile = local[b].astype(F32)
        meta[to, pl.ds(1, 1), :] = jnp.where(mine, tile, meta[to, pl.ds(1, 1), :])
        return carry

    lax.fori_loop(0, depth.shape[0], block, 0, unroll=4)
    out[:, pl.ds(2 * bins, 8), :] = meta[...].astype(BF)


def pack(owner, local, cells, depth, context, owners):
    blocks, bins, pixels = depth.shape
    channels = context.shape[2]
    smem = pl.BlockSpec(memory_space=pltpu.SMEM)
    vmem = pl.BlockSpec(memory_space=pltpu.VMEM)
    return pl.pallas_call(
        pack_kernel,
        out_shape=jax.ShapeDtypeStruct((owners, 2 * bins + 8, channels), BF),
        in_specs=[smem, smem, vmem, vmem, vmem],
        out_specs=vmem,
        scratch_shapes=[pltpu.SMEM((owners,), jnp.int32), pltpu.VMEM((owners, 8, channels), F32)],
        compiler_params=pltpu.CompilerParams(vmem_limit_bytes=40 << 20),
        name="pack",
    )(owner, local, cells, depth, context)


def cell_onehot(cell_row, cells):
    number = lax.broadcasted_iota(jnp.int32, (cells, cell_row.shape[1]), 0)
    return jnp.where(number == cell_row, 1.0, 0.0).astype(BF)


def splat_kernel(tiles, message, out, acc):
    step = pl.program_id(0)
    sources, rows, channels = message.shape
    bins = (rows - 8) // 2
    cells = TS * TS

    @pl.when(step == 0)
    def _():
        acc[...] = jnp.zeros(acc.shape, F32)

    def source(s, carry):
        meta = message[s, pl.ds(2 * bins, 8), :].astype(jnp.int32)
        hot = cell_onehot(meta[0:1], cells)
        first = message[s, 0:bins, :]
        second = message[s, bins : 2 * bins, :]
        nothing = jnp.zeros((bins, channels), BF)
        both = jnp.concatenate(
            [
                jnp.concatenate([first, nothing], axis=0),
                jnp.concatenate([nothing, second], axis=0),
            ],
            axis=1,
        )
        sums = jnp.dot(hot, both, preferred_element_type=F32)
        for rank in range(2):
            tile = tiles[(step * sources + s) * 2 + rank]
            at = pl.ds(pl.multiple_of(tile * TS, TS), TS)
            part = sums[:, rank * channels : (rank + 1) * channels]
            acc[:, at, :] += part.reshape(TS, TS, channels)
        return carry

    lax.fori_loop(0, sources, source, 0, unroll=2)

    @pl.when(step == pl.num_programs(0) - 1)
    def _():
        out[...] = acc[...].astype(BF)


def splat(tiles, message, rows, cols):
    owners, height, channels = message.shape
    chunk = owners // 8
    return pl.pallas_call(
        splat_kernel,
        out_shape=jax.ShapeDtypeStruct((rows, cols, channels), BF),
        grid=(owners // chunk,),
        in_specs=[
            pl.BlockSpec(memory_space=pltpu.SMEM),
            pl.BlockSpec((chunk, height, channels), lambda i: (i, 0, 0)),
        ],
        out_specs=pl.BlockSpec((rows, cols, channels), lambda i: (0, 0, 0)),
        scratch_shapes=[pltpu.VMEM((rows, cols, channels), F32)],
        compiler_params=pltpu.CompilerParams(vmem_limit_bytes=40 << 20),
        name="splat",
    )(tiles, message)


def conv_kernel(
    edges, middle, above, below, left, right, corner_above, corner_below, cot, weights,
    bev, grad, ping, pong, slopes, half,
):
    rows, cols, channels = middle.shape
    wide = cols + 2 * EXT
    three = 3 * channels
    pairs = rows // 2 + EXT
    column = lax.broadcasted_iota(jnp.int32, (wide, channels), 0)
    gone = ((column < EXT) & (edges[2] == 1)) | ((column >= wide - EXT) & (edges[3] == 1))
    half[0] = jnp.zeros((wide, channels), F32)
    half[1] = jnp.where(gone, 0.0, 0.5)

    def put(ref, pair, side, value):
        base = side * three
        ref[pair, :, base : base + channels] = pltpu.roll(value, 1, 0).astype(BF)
        ref[pair, :, base + channels : base + 2 * channels] = value.astype(BF)
        ref[pair, :, base + 2 * channels : base + three] = pltpu.roll(value, wide - 1, 0).astype(BF)

    def load(pair, side, west, center, east):
        joined = jnp.concatenate(
            [west.astype(F32), center.astype(F32), east.astype(F32)], axis=0
        )
        put(ping, pair, side, joined)

    def load_outer(k, carry):
        for side in range(2):
            row = 2 * k + side
            for refs, base in (((corner_above, above), 0), ((corner_below, below), EXT + rows)):
                corner, field = refs
                load(
                    base // 2 + k, side, corner[row, 0:EXT, :], field[row], corner[row, EXT:, :]
                )
        return carry

    def load_inner(k, carry):
        for side in range(2):
            row = 2 * k + side
            load(EXT // 2 + k, side, left[row], middle[row], right[row])
        return carry

    lax.fori_loop(0, EXT // 2, load_outer, 0)
    lax.fori_loop(0, rows // 2, load_inner, 0)

    def conv(ref, k, layer):
        return jnp.dot(
            ref[k], weights[layer, 0 : 2 * three, :], preferred_element_type=F32
        ) + jnp.dot(ref[k + 1], weights[layer, 2 * three :, :], preferred_element_type=F32)

    source, target = ping, pong
    offset = 0
    offsets = []
    for layer in range(LAYERS):
        count = pairs - 1 - layer
        offsets.append(offset)

        def forward(k, carry, layer=layer, source=source, target=target, offset=offset):
            total = conv(source, k, layer)
            for side in range(2):
                row = layer + 1 + 2 * k + side
                inside = jnp.where(
                    ((row < EXT) & (edges[0] == 1)) | ((row >= EXT + rows) & (edges[1] == 1)), 0, 1
                )
                preact = total[:, side * channels : (side + 1) * channels]
                scale = half[inside]
                sigma = scale + scale * jnp.tanh(0.5 * preact)
                active = preact * sigma
                slope = sigma + (active - active * sigma)
                if layer < LAYERS - 1:
                    put(target, k, side, active)
                    slopes[offset + k, side] = slope
                else:
                    @pl.when((row >= EXT) & (row < EXT + rows))
                    def _(row=row, active=active):
                        bev[row - EXT] = active[EXT : EXT + cols].astype(BF)

                    put(target, k, side, cot[row - LAYERS].astype(F32) * slope)
            return carry

        lax.fori_loop(0, count, forward, 0)
        offset += count
        source, target = target, source

    for step in range(LAYERS):
        layer = LAYERS - 1 - step
        count = rows // 2 + layer

        def backward(k, carry, layer=layer, source=source, target=target, step=step):
            total = conv(source, k, LAYERS + layer)
            for side in range(2):
                value = total[:, side * channels : (side + 1) * channels]
                if layer > 0:
                    below_at = offsets[layer - 1] + k + step + 1
                    put(target, k, side, value * slopes[below_at, side])
                else:
                    grad[2 * k + side] = value[EXT : EXT + cols].astype(BF)
            return carry

        lax.fori_loop(0, count, backward, 0)
        source, target = target, source


def convs(edges, middle, above, below, left, right, corner_above, corner_below, cot, weights):
    rows, cols, channels = middle.shape
    wide = cols + 2 * EXT
    pairs = rows // 2 + EXT
    kept = sum(pairs - 1 - layer for layer in range(LAYERS - 1))
    vmem = pl.BlockSpec(memory_space=pltpu.VMEM)
    buffer = pltpu.VMEM((pairs, wide, 6 * channels), BF)
    return pl.pallas_call(
        conv_kernel,
        out_shape=(
            jax.ShapeDtypeStruct((rows, cols, channels), BF),
            jax.ShapeDtypeStruct((rows, cols, channels), BF),
        ),
        in_specs=[pl.BlockSpec(memory_space=pltpu.SMEM)] + [vmem] * 9,
        out_specs=(vmem, vmem),
        scratch_shapes=[
            buffer,
            buffer,
            pltpu.VMEM((kept, 2, wide, channels), F32),
            pltpu.VMEM((2, wide, channels), F32),
        ],
        compiler_params=pltpu.CompilerParams(vmem_limit_bytes=60 << 20),
        name="convs",
    )(edges, middle, above, below, left, right, corner_above, corner_below, cot, weights)


def gather_kernel(tiles, message, grad, out, turned):
    step = pl.program_id(0)
    sources, _, channels = message.shape
    rows, cols, _ = grad.shape
    cells = TS * TS

    @pl.when(step == 0)
    def _():
        for tile in range(cols // TS):
            piece = grad[:, tile * TS : (tile + 1) * TS, :].reshape(cells, channels)
            turned[tile] = piece.astype(F32).T.astype(BF)

    lane = lax.broadcasted_iota(jnp.int32, (channels, channels), 1)

    def source(s, carry):
        meta = message[s].astype(jnp.int32)
        hot = cell_onehot(meta[0:1], cells)
        at = (step * sources + s) * 2
        first = jnp.dot(turned[tiles[at]], hot, preferred_element_type=F32)
        second = jnp.dot(turned[tiles[at + 1]], hot, preferred_element_type=F32)
        out[s] = jnp.where(lane < channels // 2, first, second).astype(BF)
        return carry

    lax.fori_loop(0, sources, source, 0, unroll=2)


def gather(tiles, message, grad):
    owners, height, channels = message.shape
    rows, cols, _ = grad.shape
    chunk = owners // 8
    return pl.pallas_call(
        gather_kernel,
        out_shape=jax.ShapeDtypeStruct((owners, channels, height - 8), BF),
        grid=(owners // chunk,),
        in_specs=[
            pl.BlockSpec(memory_space=pltpu.SMEM),
            pl.BlockSpec((chunk, 8, channels), lambda i: (i, height // 8 - 1, 0)),
            pl.BlockSpec((rows, cols, channels), lambda i: (0, 0, 0)),
        ],
        out_specs=pl.BlockSpec((chunk, channels, height - 8), lambda i: (i, 0, 0)),
        scratch_shapes=[pltpu.VMEM((cols // TS, channels, TS * TS), BF)],
        compiler_params=pltpu.CompilerParams(vmem_limit_bytes=40 << 20),
        name="gather",
    )(tiles, message, grad)


def final_kernel(owner, returned, depth, context, grad_depth, grad_context, count):
    step = pl.program_id(0)
    blocks, bins, _ = depth.shape

    @pl.when(step == 0)
    def _():
        clear_counts(count, returned.shape[0])

    def block(b, carry):
        to = owner[step * blocks + b]
        rank = take_slot(to, count)
        turned = returned[to].astype(F32).T
        rows = jnp.where(rank == 0, turned[0:bins], turned[bins : 2 * bins]).astype(BF)
        grad_depth[b] = lax.dot_general(
            rows, context[b], (((1,), (1,)), ((), ())), preferred_element_type=F32
        ).astype(BF)
        grad_context[b] = lax.dot_general(
            depth[b], rows, (((0,), (0,)), ((), ())), preferred_element_type=F32
        ).astype(BF)
        return carry

    lax.fori_loop(0, blocks, block, 0, unroll=4)


def final(owner, returned, depth, context):
    blocks, bins, pixels = depth.shape
    channels = context.shape[2]
    chunk = blocks // 4
    whole = pl.BlockSpec(returned.shape, lambda i: (0, 0, 0))
    depth_block = pl.BlockSpec((chunk, bins, pixels), lambda i: (i, 0, 0))
    context_block = pl.BlockSpec((chunk, pixels, channels), lambda i: (i, 0, 0))
    return pl.pallas_call(
        final_kernel,
        out_shape=(
            jax.ShapeDtypeStruct(depth.shape, BF),
            jax.ShapeDtypeStruct(context.shape, BF),
        ),
        grid=(blocks // chunk,),
        in_specs=[pl.BlockSpec(memory_space=pltpu.SMEM), whole, depth_block, context_block],
        out_specs=(depth_block, context_block),
        scratch_shapes=[pltpu.SMEM((returned.shape[0],), jnp.int32)],
        compiler_params=pltpu.CompilerParams(vmem_limit_bytes=40 << 20),
        name="final",
    )(owner, returned, depth, context)


def paired_weights(kernel):
    layers, _, _, inner, outer = kernel.shape
    upper = jnp.pad(kernel, ((0, 0), (0, 1), (0, 0), (0, 0), (0, 0)))
    lower = jnp.pad(kernel, ((0, 0), (1, 0), (0, 0), (0, 0), (0, 0)))
    return jnp.concatenate([upper, lower], axis=4).reshape(layers, 12 * inner, 2 * outer)


def per_device(
    depth_weights, context, block_owner, block_local, block_cell, conv_weight, cotangent
):
    cams_here, blocks_cam, bins, pixels = depth_weights.shape
    channels = context.shape[3]
    rows, cols, _ = cotangent.shape
    axes = ("cam", "tile")
    owners = lax.axis_size(axes)
    blocks = cams_here * blocks_cam
    depth = depth_weights.reshape(blocks, bins, pixels)
    flat_context = context.reshape(blocks, pixels, channels)
    owner = block_owner.reshape(blocks)
    local = block_local.reshape(blocks)
    cells = block_cell.reshape(blocks, 1, bins).astype(F32)
    cells = jnp.concatenate([cells, cells], axis=2)

    sent = pack(owner, local, cells, depth, flat_context, owners)
    message = lax.all_to_all(sent, axes, split_axis=0, concat_axis=0, tiled=True)

    cot = with_sides(with_sides(cotangent, "tile", 1, EXT), "cam", 0, LAYERS)
    turned_weight = conv_weight[:, ::-1, ::-1].swapaxes(3, 4)
    weights = jnp.concatenate([paired_weights(conv_weight), paired_weights(turned_weight)], axis=0)
    cam = lax.axis_index("cam")
    tile = lax.axis_index("tile")
    edges = jnp.stack(
        [cam == 0, cam == lax.axis_size("cam") - 1, tile == 0, tile == lax.axis_size("tile") - 1]
    ).astype(jnp.int32)

    tiles = message[:, 2 * bins + 1, :: bins].astype(jnp.int32).reshape(2 * owners)
    middle = splat(tiles, message, rows, cols)

    down, up = ring("cam")
    east, west = ring("tile")
    above = lax.ppermute(middle[rows - EXT :], "cam", down)
    below = lax.ppermute(middle[:EXT], "cam", up)
    left = lax.ppermute(middle[:, cols - EXT :], "tile", east)
    right = lax.ppermute(middle[:, :EXT], "tile", west)
    sides = jnp.concatenate([left, right], axis=1)
    corner_above = lax.ppermute(sides[rows - EXT :], "cam", down)
    corner_below = lax.ppermute(sides[:EXT], "cam", up)

    bev, grad = convs(
        edges, middle, above, below, left, right, corner_above, corner_below, cot, weights
    )
    rows_back = gather(tiles, message, grad)
    returned = lax.all_to_all(rows_back, axes, split_axis=0, concat_axis=0, tiled=True)
    grad_depth, grad_context = final(owner, returned, depth, flat_context)
    return (
        bev,
        grad_depth.reshape(depth_weights.shape),
        grad_context.reshape(context.shape),
    )


def solution(mesh):
    placed = (
        P(("cam", "tile"), None, None, None),
        P(("cam", "tile"), None, None, None),
        P(("cam", "tile"), None, None),
        P(("cam", "tile"), None),
        P(("cam", "tile"), None, None),
        P(),
        P("cam", "tile", None),
    )
    return jax.shard_map(
        per_device,
        mesh=mesh,
        in_specs=placed,
        out_specs=(
            P("cam", "tile", None),
            P(("cam", "tile"), None, None, None),
            P(("cam", "tile"), None, None, None),
        ),
        check_vma=False,
    )
```

time: 452 us -> 263 us (0.58); the launches traced: 445 us -> 262 us
  matrix products: 152 us -> 0 us
  waiting for transfers between devices: 140 us -> 35.5 us
  Pallas kernels: 0 us -> 93.7 us
  starting transfers between devices: 117 us -> 34.3 us
  blocking collectives: 0 us -> 69.6 us
  local copies, waits for them, and re-layouts: 24.8 us -> 17.8 us
    dot_general x79 -> x0, matrix products: 152 us -> none  [the longest x1 44.9 us: per_device(): jnp.einsum('ts,sec->tec', tile_onehot.astype(jnp.float32), slot_sums, pre...]
    all_to_all x3 -> x1, waiting for transfers between devices: 102 us -> 7.7 us  [per_device(): lax.all_to_all(sent, axes, split_axis=0, concat_axis=0, tiled=True)]
    pallas_call x0 -> x5, Pallas kernels: none -> 93.7 us  [the longest x1 48 us: convs(): pl.pallas_call(conv_kernel, out_shape=(jax.ShapeDtypeStruct((rows, cols,...]
    all_to_all x0 -> x1, blocking collectives: none -> 69.6 us  [per_device(): lax.all_to_all(rows_back, axes, split_axis=0, concat_axis=0, tiled=True)]
    ppermute x32 -> x10, starting transfers between devices: 85.2 us -> 23.4 us  [the longest x2 6.71 us: with_sides(): lax.ppermute(tail, axis, down)]
    all_to_all x3 -> x1, starting transfers between devices: 31.3 us -> 10.9 us  [per_device(): lax.all_to_all(sent, axes, split_axis=0, concat_axis=0, tiled=True)]
    ppermute x32 -> x10, waiting for transfers between devices: 37.9 us -> 27.8 us  [the longest x2 25.7 us: with_sides(): lax.ppermute(tail, axis, down)]
    scatter x1 -> x0, local copies, waits for them, and re-layouts: 8.14 us -> none  [per_device(): jnp.zeros((slots_total, bins, channels), jnp.bfloat16).at[slot_index]]
  transfers between devices with their start and end apart: 35 -> 11, of which waited for: 18 -> 4; matrix products, arithmetic and copies ran while one was open for 6% -> 6% of each run, Pallas kernels for 0% -> 7%
where the time goes in v1:
time: 263 us; the launch traced here: 262 us
  Pallas kernels  93.7 us (36%)
  blocking collectives  69.6 us (26%)
  waiting for transfers between devices  35.5 us (13%)
  starting transfers between devices  34.3 us (13%)
  local copies, waits for them, and re-layouts  17.8 us (7%)
  other arithmetic  10.2 us (4%)
    all_to_all x1, blocking collectives, per_device(): lax.all_to_all(rows_back, axes, split_axis=0, concat_axis=0, tiled=True)  69.6 us
    pallas_call x1, Pallas kernels, convs(): pl.pallas_call(conv_kernel, out_shape=(jax.ShapeDtypeStruct((rows, cols,...  48 us
    ppermute x2, waiting for transfers between devices, with_sides(): lax.ppermute(tail, axis, down)  25.7 us
    pallas_call x1, Pallas kernels, splat(): pl.pallas_call(splat_kernel, out_shape=jax.ShapeDtypeStruct((rows, cols,...  18.3 us
    pallas_call x1, Pallas kernels, gather(): pl.pallas_call(gather_kernel, out_shape=jax.ShapeDtypeStruct((owners, cha...  15.5 us
    all_to_all x1, starting transfers between devices, per_device(): lax.all_to_all(sent, axes, split_axis=0, concat_axis=0, tiled=True)  10.9 us
    unnamed x36, local copies, waits for them, and re-layouts  9.46 us
    all_to_all x1, waiting for transfers between devices, per_device(): lax.all_to_all(sent, axes, split_axis=0, concat_axis=0, tiled=True)  7.7 us
  transfers between devices with their start and end apart: 11, of which 4 were waited for; matrix products, arithmetic and copies ran while one was open for 6% of the time, Pallas kernels for 7%

profile of v1, /device:TPU:6, one launch (start us, length us, event | category | flops | bytes accessed | tf_op | source)
XLA Modules:
  0.0 262.1 jit_solution(16158496956263425104)
XLA Ops:
  4.3 1.6 copy-done.2
  7.1 4.7 %pack.1 = bf16[128,136,128]{2,1,0:T(8,128)(2,1)S(1)} custom-call(s32[64]{0:T(128)S(1)} %reshape.48.owner, s32[64]{0:T(128)S(1)} %reshape.49.local, f32[64,1,128]{2,1,0:T(1,128)S(1)} %pad_maximum_fusion.2.cells, bf16[64,64,128]{2,1,0:T(8,128)(2,1)S(1)} %bitcast.16, bf16[64,128,128]{2,1,0:T(8,128)(2,1)S(1)} %bitcast.14), custom_call_target="tpu_custom_call" | custom-call | tf_op jit(solution)/shard_map/pack/pallas_call | solution.py:75
  11.7 2.1 copy-done
  13.9 10.9 %all-to-all-start = ((bf16[128,136,128]{2,1,0:T(8,128)(2,1)}), bf16[128,136,128]{2,1,0:T(8,128)(2,1)}, u32[]{:S(2)}, u32[]{:S(2)}) async-start(bf16[128,136,128]{2,1,0:T(8,128)(2,1)} %copy-done), calls=%async_computation | async-start | bytes 8912896 | tf_op jit(solution)/shard_map/all_to_all | solution.py:391
  26.8 4.5 %collective-permute-start.6 = (bf16[16,8,128]{2,1,0:T(8,128)(2,1)S(1)}, bf16[16,8,128]{2,1,0:T(8,128)(2,1)S(1)}, u32[]{:S(2)}, u32[]{:S(2)}) collective-permute-start(bf16[16,8,128]{2,1,0:T(8,128)(2,1)S(1)} %get-tuple-element.14), channel_id=1, source_target_pairs={{0,1},{1,2},{2,3},{3,4},{4,5},{5,6},{6,7},{7,8},{8,9},{9,10},{10,1... | collective-permute-start | bytes 98312 | tf_op jit(solution)/shard_map/ppermute | solution.py:30
  31.9 2.8 %copy.11 = bf16[4,4,3,128,256]{4,3,2,1,0:T(8,128)(2,1)} copy(bf16[4,4,3,128,256]{3,4,2,1,0:T(8,128)(2,1)S(1)} %fusion.4) | data formatting | bytes 6291456 | tf_op jit(solution)/shard_map/concatenate | solution.py:371
  34.7 2.2 fusion.5
  37.3 3.2 %pad_maximum_fusion.weights = bf16[8,1536,256]{2,1,0:T(8,128)(2,1)} fusion(bf16[4,1536,256]{2,1,0:T(8,128)(2,1)S(1)} %bitcast.18, bf16[4,1536,256]{2,1,0:T(8,128)(2,1)S(1)} %bitcast.19), kind=kLoop, calls=%fused_computation.4 | loop fusion | flops 3145728 | bytes 12582912 | tf_op jit(solution)/shard_map/concatenate | solution.py:395
  41.1 25.7 %collective-permute-done.6 = bf16[16,8,128]{2,1,0:T(8,128)(2,1)S(1)} collective-permute-done((bf16[16,8,128]{2,1,0:T(8,128)(2,1)S(1)}, bf16[16,8,128]{2,1,0:T(8,128)(2,1)S(1)}, u32[]{:S(2)}, u32[]{:S(2)}) %collective-permute-start.6) | collective-permute-done | bytes 32800 | tf_op jit(solution)/shard_map/ppermute | solution.py:30
  67.8 2.2 collective-permute-start.8
  70.0 3.4 %collective-permute-start.9 = (bf16[4,272,128]{2,1,0:T(8,128)(2,1)S(1)}, bf16[4,272,128]{2,1,0:T(8,128)(2,1)S(1)}, u32[]{:S(2)}, u32[]{:S(2)}) collective-permute-start(bf16[4,272,128]{2,1,0:T(8,128)(2,1)S(1)} %get-tuple-element.12), channel_id=1, source_target_pairs={{16,0},{32,16},{48,32},{64,48},{80,64},{96,80},{112,96},{17,1},{33... | collective-permute-start | bytes 835592 | tf_op jit(solution)/shard_map/ppermute | solution.py:30
  73.4 7.7 %all-to-all-done.message = bf16[128,136,128]{2,1,0:T(8,128)(2,1)} async-done(((bf16[128,136,128]{2,1,0:T(8,128)(2,1)}), bf16[128,136,128]{2,1,0:T(8,128)(2,1)}, u32[]{:S(2)}, u32[]{:S(2)}) %all-to-all-start) | async-done | bytes 4456480 | tf_op jit(solution)/shard_map/all_to_all | solution.py:391
  81.1 2.8 %slice.33 = bf16[128,1,2]{2,1,0:T(2,128)(2,1)S(1)} slice(bf16[128,136,128]{2,1,0:T(8,128)(2,1)} %all-to-all-done.message), slice={[0:128:1], [129:130:1], [0:128:64]} | slice | bytes 1024 | tf_op jit(solution)/shard_map/slice | solution.py:402
  84.3 18.3 %splat.1.middle = bf16[16,256,128]{2,1,0:T(8,128)(2,1)S(1)} custom-call(s32[256]{0:T(256)S(1)} %reshape.56.tiles, bf16[128,136,128]{2,1,0:T(8,128)(2,1)} %all-to-all-done.message), custom_call_target="tpu_custom_call" | custom-call | tf_op jit(solution)/shard_map/splat/pallas_call | solution.py:132
  102.6 1.4 collective-permute-start.2
  105.4 1.9 collective-permute-start.1
  107.3 2.4 collective-permute-start
  109.9 3.0 %collective-permute-start.5 = (bf16[8,16,128]{2,1,0:T(8,128)(2,1)S(1)}, bf16[8,16,128]{2,1,0:T(8,128)(2,1)S(1)}, u32[]{:S(2)}, u32[]{:S(2)}) collective-permute-start(bf16[8,16,128]{2,1,0:T(8,128)(2,1)S(1)} %get-tuple-element.19), channel_id=1, source_target_pairs={{16,0},{32,16},{48,32},{64,48},{80,64},{96,80},{112,96},{17,1},{33... | collective-permute-start | bytes 98312 | tf_op jit(solution)/shard_map/ppermute | solution.py:413
  113.0 1.9 collective-permute-start.4
  116.3 1.9 collective-permute-done.4.corner_above
  120.5 48.0 %convs.1 = (bf16[16,256,128]{2,1,0:T(8,128)(2,1)}, bf16[16,256,128]{2,1,0:T(8,128)(2,1)}) custom-call(s32[4]{0:T(128)} %add_convert_fusion.edges, bf16[16,256,128]{2,1,0:T(8,128)(2,1)} %copy-done.1, bf16[8,256,128]{2,1,0:T(8,128)(2,1)} %copy-done.11, bf16[8,256,128]{2,1,0:T(8,128)(2,1)} %copy-done.10, bf16[16,8,128]{2,1,0:T(8,128)(2,1)} %copy-done.12, ...), custom_call_target="tpu_custom_call" | custom-call | tf_op jit(solution)/shard_map/convs/pallas_call | solution.py:256
  169.7 15.5 %gather.1 = bf16[128,128,128]{2,1,0:T(8,128)(2,1)S(1)} custom-call(s32[256]{0:T(256)S(1)} %reshape.56.tiles, bf16[128,136,128]{2,1,0:T(8,128)(2,1)} %all-to-all-done.message, bf16[16,256,128]{2,1,0:T(8,128)(2,1)S(1)} %copy-done.6), custom_call_target="tpu_custom_call" | custom-call | tf_op jit(solution)/shard_map/gather/pallas_call | solution.py:305
  185.2 69.6 %all_to_all.10.returned = bf16[128,128,128]{2,1,0:T(8,128)(2,1)S(1)} all-to-all(bf16[128,128,128]{2,1,0:T(8,128)(2,1)S(1)} %gather.1), channel_id=1, replica_groups=mesh['cam'=8,'tile'=16] {'cam','tile'}, dimensions={0} | all-to-all | bytes 8388608 | tf_op jit(solution)/shard_map/all_to_all | solution.py:419
  254.8 7.3 %final.1 = (bf16[64,64,128]{2,1,0:T(8,128)(2,1)}, bf16[64,128,128]{2,1,0:T(8,128)(2,1)}) custom-call(s32[64]{0:T(128)S(1)} %reshape.48.owner, bf16[128,128,128]{2,1,0:T(8,128)(2,1)S(1)} %all_to_all.10.returned, bf16[64,64,128]{2,1,0:T(8,128)(2,1)S(1)} %bitcast.17, bf16[64,128,128]{2,1,0:T(8,128)(2,1)S(1)} %bitcast.15), custom_call_target="tpu_custom_call" | custom-call | tf_op jit(solution)/shard_map/final/pallas_call | solution.py:352
  (62 shorter events, 16.0 us)
Async XLA Ops:
  4.2 1.6 copy-start.2
  5.8 1.2 copy-start.4
  11.7 2.1 copy-start
  13.9 17.5 %copy-start.8 = (bf16[4,3,3,128,128]{4,3,2,1,0:T(8,128)(2,1)S(1)}, bf16[4,3,3,128,128]{4,3,2,1,0:T(8,128)(2,1)}, u32[]{:S(2)}) copy-start(bf16[4,3,3,128,128]{4,3,2,1,0:T(8,128)(2,1)} %param.12) | copy-start | bytes 3538948
  13.9 67.2 %all-to-all-start = ((bf16[128,136,128]{2,1,0:T(8,128)(2,1)}), bf16[128,136,128]{2,1,0:T(8,128)(2,1)}, u32[]{:S(2)}, u32[]{:S(2)}) async-start(bf16[128,136,128]{2,1,0:T(8,128)(2,1)} %copy-done), calls=%async_computation | async-start | bytes 8912896 | tf_op jit(solution)/shard_map/all_to_all | solution.py:391
  25.5 41.5 %collective-permute-start.7 = (bf16[16,8,128]{2,1,0:T(8,128)(2,1)S(1)}, bf16[16,8,128]{2,1,0:T(8,128)(2,1)S(1)}, u32[]{:S(2)}, u32[]{:S(2)}) collective-permute-start(bf16[16,8,128]{2,1,0:T(8,128)(2,1)S(1)} %get-tuple-element.13), channel_id=1, source_target_pairs={{1,0},{2,1},{3,2},{4,3},{5,4},{6,5},{7,6},{8,7},{9,8},{10,9},{11,1... | collective-permute-start | bytes 98312 | tf_op jit(solution)/shard_map/ppermute | solution.py:30
  26.8 40.0 %collective-permute-start.6 = (bf16[16,8,128]{2,1,0:T(8,128)(2,1)S(1)}, bf16[16,8,128]{2,1,0:T(8,128)(2,1)S(1)}, u32[]{:S(2)}, u32[]{:S(2)}) collective-permute-start(bf16[16,8,128]{2,1,0:T(8,128)(2,1)S(1)} %get-tuple-element.14), channel_id=1, source_target_pairs={{0,1},{1,2},{2,3},{3,4},{4,5},{5,6},{6,7},{7,8},{8,9},{9,10},{10,1... | collective-permute-start | bytes 98312 | tf_op jit(solution)/shard_map/ppermute | solution.py:30
  34.7 2.6 copy-start.7
  37.3 29.6 %copy-start.9 = (bf16[16,256,128]{2,1,0:T(8,128)(2,1)S(1)}, bf16[16,256,128]{2,1,0:T(8,128)(2,1)}, u32[]{:S(2)}) copy-start(bf16[16,256,128]{2,1,0:T(8,128)(2,1)} %param.13) | copy-start | bytes 3145732
  67.8 45.2 %collective-permute-start.8 = (bf16[4,272,128]{2,1,0:T(8,128)(2,1)}, bf16[4,272,128]{2,1,0:T(8,128)(2,1)S(1)}, u32[]{:S(2)}, u32[]{:S(2)}) collective-permute-start(bf16[4,272,128]{2,1,0:T(8,128)(2,1)} %get-tuple-element.11), channel_id=1, source_target_pairs={{0,16},{16,32},{32,48},{48,64},{64,80},{80,96},{96,112},{1,17},{17... | collective-permute-start | bytes 835592 | tf_op jit(solution)/shard_map/ppermute | solution.py:30
  70.0 45.0 %collective-permute-start.9 = (bf16[4,272,128]{2,1,0:T(8,128)(2,1)S(1)}, bf16[4,272,128]{2,1,0:T(8,128)(2,1)S(1)}, u32[]{:S(2)}, u32[]{:S(2)}) collective-permute-start(bf16[4,272,128]{2,1,0:T(8,128)(2,1)S(1)} %get-tuple-element.12), channel_id=1, source_target_pairs={{16,0},{32,16},{48,32},{64,48},{80,64},{96,80},{112,96},{17,1},{33... | collective-permute-start | bytes 835592 | tf_op jit(solution)/shard_map/ppermute | solution.py:30
  102.5 16.3 %copy-start.1 = (bf16[16,256,128]{2,1,0:T(8,128)(2,1)}, bf16[16,256,128]{2,1,0:T(8,128)(2,1)S(1)}, u32[]{:S(2)}) copy-start(bf16[16,256,128]{2,1,0:T(8,128)(2,1)S(1)} %splat.1.middle) | copy-start | bytes 3145732
  102.6 4.8 %collective-permute-start.2 = (bf16[16,8,128]{2,1,0:T(8,128)(2,1)S(1)}, bf16[16,8,128]{2,1,0:T(8,128)(2,1)S(1)}, u32[]{:S(2)}, u32[]{:S(2)}) collective-permute-start(bf16[16,8,128]{2,1,0:T(8,128)(2,1)S(1)} %get-tuple-element.16), channel_id=1, source_target_pairs={{0,1},{1,2},{2,3},{3,4},{4,5},{5,6},{6,7},{7,8},{8,9},{9,10},{10,1... | collective-permute-start | bytes 98312 | tf_op jit(solution)/shard_map/ppermute | solution.py:409
  104.1 5.8 %collective-permute-start.3 = (bf16[16,8,128]{2,1,0:T(8,128)(2,1)S(1)}, bf16[16,8,128]{2,1,0:T(8,128)(2,1)S(1)}, u32[]{:S(2)}, u32[]{:S(2)}) collective-permute-start(bf16[16,8,128]{2,1,0:T(8,128)(2,1)S(1)} %get-tuple-element.15), channel_id=1, source_target_pairs={{1,0},{2,1},{3,2},{4,3},{5,4},{6,5},{7,6},{8,7},{9,8},{10,9},{11,1... | collective-permute-start | bytes 98312 | tf_op jit(solution)/shard_map/ppermute | solution.py:410
  105.4 12.9 %collective-permute-start.1 = (bf16[8,256,128]{2,1,0:T(8,128)(2,1)S(1)}, bf16[8,256,128]{2,1,0:T(8,128)(2,1)S(1)}, u32[]{:S(2)}, u32[]{:S(2)}) collective-permute-start(bf16[8,256,128]{2,1,0:T(8,128)(2,1)S(1)} %get-tuple-element.17), channel_id=1, source_target_pairs={{16,0},{32,16},{48,32},{64,48},{80,64},{96,80},{112,96},{17,1},{33... | collective-permute-start | bytes 1572872 | tf_op jit(solution)/shard_map/ppermute | solution.py:408
  107.3 11.5 %copy-start.12 = (bf16[16,8,128]{2,1,0:T(8,128)(2,1)}, bf16[16,8,128]{2,1,0:T(8,128)(2,1)S(1)}, u32[]{:S(2)}) copy-start(bf16[16,8,128]{2,1,0:T(8,128)(2,1)S(1)} %collective-permute-done.2.left) | copy-start | bytes 98308
  107.3 11.5 %collective-permute-start = (bf16[8,256,128]{2,1,0:T(8,128)(2,1)S(1)}, bf16[8,256,128]{2,1,0:T(8,128)(2,1)S(1)}, u32[]{:S(2)}, u32[]{:S(2)}) collective-permute-start(bf16[8,256,128]{2,1,0:T(8,128)(2,1)S(1)} %get-tuple-element.18), channel_id=1, source_target_pairs={{0,16},{16,32},{32,48},{48,64},{64,80},{80,96},{96,112},{1,17},{17... | collective-permute-start | bytes 1572872 | tf_op jit(solution)/shard_map/ppermute | solution.py:407
  109.9 3.1 %copy-start.13 = (bf16[16,8,128]{2,1,0:T(8,128)(2,1)}, bf16[16,8,128]{2,1,0:T(8,128)(2,1)S(1)}, u32[]{:S(2)}) copy-start(bf16[16,8,128]{2,1,0:T(8,128)(2,1)S(1)} %collective-permute-done.3.right) | copy-start | bytes 98308
  109.9 6.4 %collective-permute-start.5 = (bf16[8,16,128]{2,1,0:T(8,128)(2,1)S(1)}, bf16[8,16,128]{2,1,0:T(8,128)(2,1)S(1)}, u32[]{:S(2)}, u32[]{:S(2)}) collective-permute-start(bf16[8,16,128]{2,1,0:T(8,128)(2,1)S(1)} %get-tuple-element.19), channel_id=1, source_target_pairs={{16,0},{32,16},{48,32},{64,48},{80,64},{96,80},{112,96},{17,1},{33... | collective-permute-start | bytes 98312 | tf_op jit(solution)/shard_map/ppermute | solution.py:413
  113.0 5.2 %collective-permute-start.4 = (bf16[8,16,128]{2,1,0:T(8,128)(2,1)S(1)}, bf16[8,16,128]{2,1,0:T(8,128)(2,1)S(1)}, u32[]{:S(2)}, u32[]{:S(2)}) collective-permute-start(bf16[8,16,128]{2,1,0:T(8,128)(2,1)S(1)} %get-tuple-element.20), channel_id=1, source_target_pairs={{0,16},{16,32},{32,48},{48,64},{64,80},{80,96},{96,112},{1,17},{17... | collective-permute-start | bytes 98312 | tf_op jit(solution)/shard_map/ppermute | solution.py:412
  116.3 1.9 copy-start.14
  168.5 1.2 copy-start.6
  185.2 69.6 %copy-start.3 = (bf16[4,16,128,128]{3,2,1,0:T(8,128)(2,1)S(1)}, bf16[4,16,128,128]{3,2,1,0:T(8,128)(2,1)}, u32[]{:S(2)}) copy-start(bf16[4,16,128,128]{3,2,1,0:T(8,128)(2,1)} %param.8) | copy-start | bytes 6291460
  185.2 69.6 %copy-start.5 = (bf16[4,16,64,128]{3,2,1,0:T(8,128)(2,1)S(1)}, bf16[4,16,64,128]{3,2,1,0:T(8,128)(2,1)}, u32[]{:S(2)}) copy-start(bf16[4,16,64,128]{3,2,1,0:T(8,128)(2,1)} %param.7) | copy-start | bytes 3145732
  (3 other events, 2.2 us)

commit v2 on v1

v2 whole, which is shorter than its diff:
```python
import jax
import jax.numpy as jnp
from jax import lax
from jax.experimental import pallas as pl
from jax.experimental.pallas import tpu as pltpu
from jax.sharding import PartitionSpec as P

TS = 16
LAYERS = 4
EXT = 2 * LAYERS
PAIRS = 8
CHUNK = 4
EMPTY = 256.0
ABSENT = 255
BF = jnp.bfloat16
F32 = jnp.float32


def ring(axis):
    count = lax.axis_size(axis)
    ends = count - 1
    down = [(i, i + 1) for i in range(ends)]
    up = [(i + 1, i) for i in range(ends)]
    return down, up


def with_sides(cells, axis, dim, width):
    down, up = ring(axis)
    size = cells.shape[dim]
    head = lax.slice_in_dim(cells, 0, width, axis=dim)
    tail = lax.slice_in_dim(cells, size - width, size, axis=dim)
    return jnp.concatenate(
        [lax.ppermute(tail, axis, down), cells, lax.ppermute(head, axis, up)], axis=dim
    )


def take_slot(owner, count):
    rank = count[owner]
    count[owner] = rank + 1
    return rank


def clear_counts(count, size):
    @pl.loop(0, size)
    def _(i):
        count[i] = 0


def pair_cells(cells):
    return (cells // TS) * TS + (cells % 2) * (TS // 2) + (cells % TS) // 2


def pack_kernel(owner, local, cells, depth, context, out, count, wide, lifted, meta, sems):
    step = pl.program_id(0)
    blocks, bins, _ = depth.shape
    owners = out.shape[0]
    channels = context.shape[2]

    @pl.when(step == 0)
    def _():
        clear_counts(count, owners)
        kind = lax.broadcasted_iota(jnp.int32, meta.shape, 1)
        meta[...] = jnp.where(kind == 0, EMPTY, ABSENT)
        numbers = pair_cells(cells[...]).astype(F32)
        wide[...] = jnp.concatenate([numbers, numbers], axis=1)

    lane = lax.broadcasted_iota(jnp.int32, (1, 2 * bins), 1)

    def block(b, carry):
        at = step * blocks + b
        to = owner[at]
        rank = take_slot(to, count)
        product = jnp.dot(depth[b], context[b], preferred_element_type=F32)
        lifted[at // 2, pl.ds(pl.multiple_of((at % 2) * bins, bins), bins), :] = product.astype(BF)
        mine = (lane // bins) == rank
        row = wide[pl.ds(at, 1), :]
        meta[to, pl.ds(0, 1), :] = jnp.where(mine, row, meta[to, pl.ds(0, 1), :])
        tile = local[at].astype(F32)
        meta[to, pl.ds(1, 1), :] = jnp.where(mine, tile, meta[to, pl.ds(1, 1), :])
        pltpu.make_async_copy(
            lifted.at[at // 2, pl.ds(pl.multiple_of((at % 2) * bins, bins), bins), :],
            out.at[to, pl.ds(pl.multiple_of(rank * bins, bins), bins), :],
            sems.at[0],
        ).start()
        return carry

    lax.fori_loop(0, blocks, block, 0, unroll=4)

    @pl.when(step == pl.num_programs(0) - 1)
    def _():
        wide_meta = lifted.shape[0]
        def put_meta(small):
            small[...] = meta[...].astype(BF)
            copy = pltpu.make_async_copy(
                small, out.at[:, pl.ds(2 * bins, 8), :], sems.at[1]
            )
            copy.start()
            copy.wait()
        pl.run_scoped(put_meta, pltpu.VMEM(meta.shape, BF))
        pltpu.make_async_copy(
            lifted, out.at[pl.ds(0, wide_meta), pl.ds(0, 2 * bins), :], sems.at[0]
        ).wait()


def pack(owner, local, cells, depth, context, owners):
    blocks, bins, pixels = depth.shape
    channels = context.shape[2]
    chunk = blocks // 4
    smem = pl.BlockSpec(memory_space=pltpu.SMEM)
    return pl.pallas_call(
        pack_kernel,
        out_shape=jax.ShapeDtypeStruct((owners, 2 * bins + 8, channels), BF),
        grid=(blocks // chunk,),
        in_specs=[
            smem,
            smem,
            pl.BlockSpec(cells.shape, lambda i: (0, 0)),
            pl.BlockSpec((chunk, bins, pixels), lambda i: (i, 0, 0)),
            pl.BlockSpec((chunk, pixels, channels), lambda i: (i, 0, 0)),
        ],
        out_specs=pl.BlockSpec(memory_space=pltpu.HBM),
        scratch_shapes=[
            pltpu.SMEM((owners,), jnp.int32),
            pltpu.VMEM((blocks, 2 * bins), F32),
            pltpu.VMEM((blocks // 2, 2 * bins, channels), BF),
            pltpu.VMEM((owners, 8, 2 * bins), F32),
            pltpu.SemaphoreType.DMA((2,)),
        ],
        compiler_params=pltpu.CompilerParams(vmem_limit_bytes=40 << 20),
        name="pack",
    )(owner, local, cells, depth, context)


def cell_onehot(cell_row, cells):
    number = lax.broadcasted_iota(jnp.int32, (cells, cell_row.shape[1]), 0)
    return jnp.where(number == cell_row, 1.0, 0.0).astype(BF)


def splat_kernel(meta_all, message, out, tiles_out, even, odd, turned, tiles, sem):
    step = pl.program_id(0)
    sources, rows, channels = message.shape
    bins = (rows - 8) // 2
    cells = TS * TS

    @pl.when(step == 0)
    def _():
        numbers = meta_all[:, 0:8, :].astype(F32)
        flat = numbers[:, 1, :].T
        turned[0:1, :] = flat[0:1].astype(jnp.int32)
        turned[1:2, :] = flat[bins : bins + 1].astype(jnp.int32)
        copy = pltpu.make_async_copy(turned, tiles, sem)
        copy.start()
        even[...] = jnp.zeros(even.shape, F32)
        odd[...] = jnp.zeros(odd.shape, F32)
        copy.wait()

    def source(s, carry):
        meta = message[s, pl.ds(2 * bins, 8), :].astype(jnp.int32)
        hot = cell_onehot(meta[0:1], cells)
        tile = [tiles[rank, step * sources + s] for rank in range(2)]
        nothing = jnp.zeros((bins, channels), BF)
        first = jnp.where(tile[0] < ABSENT, message[s, 0:bins, :], nothing)
        second = jnp.where(tile[1] < ABSENT, message[s, bins : 2 * bins, :], nothing)
        both = jnp.concatenate(
            [
                jnp.concatenate([first, nothing], axis=0),
                jnp.concatenate([nothing, second], axis=0),
            ],
            axis=1,
        )
        sums = jnp.dot(hot, both, preferred_element_type=F32)
        for rank, acc in enumerate((even, odd)):
            here = jnp.minimum(tile[rank], acc.shape[1] // 8 - 1)
            at = pl.ds(pl.multiple_of(here * 8, 8), 8)
            part = sums[:, rank * channels : (rank + 1) * channels].reshape(TS, 2, 8, channels)
            for side in range(2):
                lanes = slice(side * channels, (side + 1) * channels)
                acc[:, at, lanes] += part[:, side]
        return carry

    lax.fori_loop(0, sources, source, 0, unroll=4)

    @pl.when(step == pl.num_programs(0) - 1)
    def _():
        out[...] = (even[...] + odd[...]).astype(BF)
        tiles_out[...] = turned[...]


def splat(message, rows, cols):
    owners, height, channels = message.shape
    chunk = owners // 8
    shape = (rows, cols // 2, 2 * channels)
    return pl.pallas_call(
        splat_kernel,
        out_shape=(
            jax.ShapeDtypeStruct(shape, BF),
            jax.ShapeDtypeStruct((2, owners), jnp.int32),
        ),
        grid=(owners // chunk,),
        in_specs=[
            pl.BlockSpec((owners, 8, channels), lambda i: (0, height // 8 - 1, 0)),
            pl.BlockSpec((chunk, height, channels), lambda i: (i, 0, 0)),
        ],
        out_specs=(
            pl.BlockSpec(shape, lambda i: (0, 0, 0)),
            pl.BlockSpec((2, owners), lambda i: (0, 0)),
        ),
        scratch_shapes=[
            pltpu.VMEM(shape, F32),
            pltpu.VMEM(shape, F32),
            pltpu.VMEM((2, owners), jnp.int32),
            pltpu.SMEM((2, owners), jnp.int32),
            pltpu.SemaphoreType.DMA,
        ],
        compiler_params=pltpu.CompilerParams(vmem_limit_bytes=40 << 20),
        name="splat",
    )(message, message)


def conv_kernel(
    edges, middle, above, below, left, right, corner_above, corner_below, cot, weights,
    bev, grad, ping, pong, slopes, half,
):
    rows, mid, double = middle.shape
    channels = double // 2
    wide = mid + 2 * PAIRS
    tall = rows + 2 * EXT
    column = lax.broadcasted_iota(jnp.int32, (wide, double), 0)
    gone = ((column < PAIRS) & (edges[2] == 1)) | ((column >= wide - PAIRS) & (edges[3] == 1))
    half[0] = jnp.zeros((wide, double), F32)
    half[1] = jnp.where(gone, 0.0, 0.5)

    def put(ref, row, value):
        first = value[:, :channels]
        second = value[:, channels:]
        ref[row, :, 0:channels] = pltpu.roll(second, 1, 0).astype(BF)
        ref[row, :, channels : 3 * channels] = value.astype(BF)
        ref[row, :, 3 * channels :] = pltpu.roll(first, wide - 1, 0).astype(BF)

    def load(row, west, center, east):
        put(
            ping, row,
            jnp.concatenate([west.astype(F32), center.astype(F32), east.astype(F32)], axis=0),
        )

    def load_outer(k, carry):
        load(k, corner_above[k, 0:PAIRS], above[k], corner_above[k, PAIRS:])
        load(EXT + rows + k, corner_below[k, 0:PAIRS], below[k], corner_below[k, PAIRS:])
        return carry

    def load_inner(k, carry):
        load(EXT + k, left[k], middle[k], right[k])
        return carry

    lax.fori_loop(0, EXT, load_outer, 0)
    lax.fori_loop(0, rows, load_inner, 0)

    def conv(ref, row, layer, chunk):
        taps = [
            ref[pl.ds(row + tap, chunk)].reshape(chunk * wide, 2 * double) for tap in range(3)
        ]
        return jnp.dot(
            jnp.concatenate(taps, axis=1), weights[layer], preferred_element_type=F32
        ).reshape(chunk, wide, double)

    source, target = ping, pong
    offset = 0
    offsets = []
    for layer in range(LAYERS):
        count = tall - 2 - 2 * layer
        offsets.append(offset)

        def forward(k, carry, layer=layer, source=source, target=target, offset=offset, count=count):
            start = jnp.minimum(k * CHUNK, count - CHUNK)
            total = conv(source, start, layer, CHUNK)
            for side in range(CHUNK):
                here = start + side
                row = layer + 1 + here
                inside = jnp.where(
                    ((row < EXT) & (edges[0] == 1)) | ((row >= EXT + rows) & (edges[1] == 1)), 0, 1
                )
                preact = total[side]
                scale = half[inside]
                sigma = scale + scale * jnp.tanh(0.5 * preact)
                active = preact * sigma
                slope = sigma + (active - active * sigma)
                if layer < LAYERS - 1:
                    put(target, here, active)
                    slopes[offset + here] = slope
                else:
                    @pl.when((row >= EXT) & (row < EXT + rows))
                    def _(row=row, active=active):
                        bev[row - EXT] = active[PAIRS : PAIRS + mid].astype(BF)

                    put(target, here, cot[here].astype(F32) * slope)
            return carry

        lax.fori_loop(0, -(-count // CHUNK), forward, 0)
        offset += count
        source, target = target, source

    for step in range(LAYERS):
        layer = LAYERS - 1 - step
        count = rows + 2 * layer

        def backward(k, carry, layer=layer, source=source, target=target, step=step, count=count):
            start = jnp.minimum(k * CHUNK, count - CHUNK)
            total = conv(source, start, LAYERS + layer, CHUNK)
            for side in range(CHUNK):
                here = start + side
                if layer > 0:
                    put(target, here, total[side] * slopes[offsets[layer - 1] + here + 2 * (step + 1)])
                else:
                    grad[here] = total[side, PAIRS : PAIRS + mid].astype(BF)
            return carry

        lax.fori_loop(0, -(-count // CHUNK), backward, 0)
        source, target = target, source


def convs(edges, middle, above, below, left, right, corner_above, corner_below, cot, weights):
    rows, mid, double = middle.shape
    wide = mid + 2 * PAIRS
    tall = rows + 2 * EXT
    kept = sum(tall - 2 - 2 * layer for layer in range(LAYERS - 1))
    vmem = pl.BlockSpec(memory_space=pltpu.VMEM)
    buffer = pltpu.VMEM((tall, wide, 2 * double), BF)
    return pl.pallas_call(
        conv_kernel,
        out_shape=(
            jax.ShapeDtypeStruct(middle.shape, BF),
            jax.ShapeDtypeStruct(middle.shape, BF),
        ),
        in_specs=[pl.BlockSpec(memory_space=pltpu.SMEM)] + [vmem] * 9,
        out_specs=(vmem, vmem),
        scratch_shapes=[
            buffer,
            buffer,
            pltpu.VMEM((kept, wide, double), F32),
            pltpu.VMEM((2, wide, double), F32),
        ],
        compiler_params=pltpu.CompilerParams(vmem_limit_bytes=60 << 20),
        name="convs",
    )(edges, middle, above, below, left, right, corner_above, corner_below, cot, weights)


def gather_kernel(tiles, message, grad, out, turned):
    step = pl.program_id(0)
    sources, _, channels = message.shape
    rows, mid, double = grad.shape
    cells = TS * TS
    bins = out.shape[2] // 2

    @pl.when(step == 0)
    def _():
        for tile in range(mid // 8):
            piece = grad[:, tile * 8 : (tile + 1) * 8, :].astype(F32)
            piece = jnp.stack([piece[:, :, :channels], piece[:, :, channels:]], axis=1)
            turned[tile] = piece.reshape(cells, channels).T.astype(BF)

    lane = lax.broadcasted_iota(jnp.int32, (1, 2 * bins), 1)
    lift = (lane // bins) * cells

    def source(s, carry):
        meta = message[s].astype(jnp.int32)[0:1]
        hot = cell_onehot(jnp.where(meta < cells, meta + lift, 2 * cells), 2 * cells)
        at = step * sources + s
        here = [jnp.minimum(tiles[rank, at], mid // 8 - 1) for rank in range(2)]
        both = jnp.concatenate([turned[here[0]], turned[here[1]]], axis=1)
        out[s] = jnp.dot(both, hot, preferred_element_type=F32).astype(BF)
        return carry

    lax.fori_loop(0, sources, source, 0, unroll=4)


def gather(tiles, message, grad):
    owners, height, channels = message.shape
    chunk = owners // 8
    return pl.pallas_call(
        gather_kernel,
        out_shape=jax.ShapeDtypeStruct((owners, channels, height - 8), BF),
        grid=(owners // chunk,),
        in_specs=[
            pl.BlockSpec(memory_space=pltpu.SMEM),
            pl.BlockSpec((chunk, 8, channels), lambda i: (i, height // 8 - 1, 0)),
            pl.BlockSpec(grad.shape, lambda i: (0, 0, 0)),
        ],
        out_specs=pl.BlockSpec((chunk, channels, height - 8), lambda i: (i, 0, 0)),
        scratch_shapes=[pltpu.VMEM((grad.shape[1] // 8, channels, TS * TS), BF)],
        compiler_params=pltpu.CompilerParams(vmem_limit_bytes=40 << 20),
        name="gather",
    )(tiles, message, grad)


def final_kernel(owner, returned, depth, context, grad_depth, grad_context, count):
    step = pl.program_id(0)
    blocks, bins, _ = depth.shape

    @pl.when(step == 0)
    def _():
        clear_counts(count, returned.shape[0])

    def block(b, carry):
        to = owner[step * blocks + b]
        rank = take_slot(to, count)
        turned = returned[to].astype(F32).T
        rows = jnp.where(rank == 0, turned[0:bins], turned[bins : 2 * bins]).astype(BF)
        grad_depth[b] = lax.dot_general(
            rows, context[b], (((1,), (1,)), ((), ())), preferred_element_type=F32
        ).astype(BF)
        grad_context[b] = lax.dot_general(
            depth[b], rows, (((0,), (0,)), ((), ())), preferred_element_type=F32
        ).astype(BF)
        return carry

    lax.fori_loop(0, blocks, block, 0, unroll=4)


def final(owner, returned, depth, context):
    blocks, bins, pixels = depth.shape
    channels = context.shape[2]
    chunk = blocks // 4
    whole = pl.BlockSpec(returned.shape, lambda i: (0, 0, 0))
    depth_block = pl.BlockSpec((chunk, bins, pixels), lambda i: (i, 0, 0))
    context_block = pl.BlockSpec((chunk, pixels, channels), lambda i: (i, 0, 0))
    return pl.pallas_call(
        final_kernel,
        out_shape=(
            jax.ShapeDtypeStruct(depth.shape, BF),
            jax.ShapeDtypeStruct(context.shape, BF),
        ),
        grid=(blocks // chunk,),
        in_specs=[pl.BlockSpec(memory_space=pltpu.SMEM), whole, depth_block, context_block],
        out_specs=(depth_block, context_block),
        scratch_shapes=[pltpu.SMEM((returned.shape[0],), jnp.int32)],
        compiler_params=pltpu.CompilerParams(vmem_limit_bytes=40 << 20),
        name="final",
    )(owner, returned, depth, context)


def paired_weights(kernel):
    layers, taps, _, inner, outer = kernel.shape
    first = jnp.pad(kernel, ((0, 0), (0, 0), (0, 1), (0, 0), (0, 0)))
    second = jnp.pad(kernel, ((0, 0), (0, 0), (1, 0), (0, 0), (0, 0)))
    return jnp.concatenate([first, second], axis=4).reshape(layers, 4 * taps * inner, 2 * outer)


def per_device(
    depth_weights, context, block_owner, block_local, block_cell, conv_weight, cotangent
):
    cams_here, blocks_cam, bins, pixels = depth_weights.shape
    channels = context.shape[3]
    rows, cols, _ = cotangent.shape
    mid = cols // 2
    axes = ("cam", "tile")
    owners = lax.axis_size(axes)
    blocks = cams_here * blocks_cam
    depth = depth_weights.reshape(blocks, bins, pixels)
    flat_context = context.reshape(blocks, pixels, channels)
    owner = block_owner.reshape(blocks)
    local = block_local.reshape(blocks)

    sent = pack(owner, local, block_cell.reshape(blocks, bins), depth, flat_context, owners)
    message = lax.all_to_all(sent, axes, split_axis=0, concat_axis=0, tiled=True)

    cot = cotangent.reshape(rows, mid, 2 * channels)
    cot = with_sides(with_sides(cot, "tile", 1, PAIRS), "cam", 0, LAYERS)
    turned_weight = conv_weight[:, ::-1, ::-1].swapaxes(3, 4)
    weights = jnp.concatenate([paired_weights(conv_weight), paired_weights(turned_weight)], axis=0)
    cam = lax.axis_index("cam")
    tile = lax.axis_index("tile")
    edges = jnp.stack(
        [cam == 0, cam == lax.axis_size("cam") - 1, tile == 0, tile == lax.axis_size("tile") - 1]
    ).astype(jnp.int32)

    middle, tiles = splat(message, rows, cols)

    down, up = ring("cam")
    east, west = ring("tile")
    above = lax.ppermute(middle[rows - EXT :], "cam", down)
    below = lax.ppermute(middle[:EXT], "cam", up)
    left = lax.ppermute(middle[:, mid - PAIRS :], "tile", east)
    right = lax.ppermute(middle[:, :PAIRS], "tile", west)
    sides = jnp.concatenate([left, right], axis=1)
    corner_above = lax.ppermute(sides[rows - EXT :], "cam", down)
    corner_below = lax.ppermute(sides[:EXT], "cam", up)

    bev, grad = convs(
        edges, middle, above, below, left, right, corner_above, corner_below, cot, weights
    )
    rows_back = gather(tiles, message, grad)
    returned = lax.all_to_all(rows_back, axes, split_axis=0, concat_axis=0, tiled=True)
    grad_depth, grad_context = final(owner, returned, depth, flat_context)
    return (
        bev.reshape(cotangent.shape),
        grad_depth.reshape(depth_weights.shape),
        grad_context.reshape(context.shape),
    )


def solution(mesh):
    placed = (
        P(("cam", "tile"), None, None, None),
        P(("cam", "tile"), None, None, None),
        P(("cam", "tile"), None, None),
        P(("cam", "tile"), None),
        P(("cam", "tile"), None, None),
        P(),
        P("cam", "tile", None),
    )
    return jax.shard_map(
        per_device,
        mesh=mesh,
        in_specs=placed,
        out_specs=(
            P("cam", "tile", None),
            P(("cam", "tile"), None, None, None),
            P(("cam", "tile"), None, None, None),
        ),
        check_vma=False,
    )
```

time: 263 us -> 252 us (0.958)
  blocking collectives: 69.6 us -> 0 us
  waiting for transfers between devices: 35.5 us -> 88.1 us
  starting transfers between devices: 34.3 us -> 50.6 us
  Pallas kernels: 93.7 us -> 84 us
    all_to_all x1 -> x0, blocking collectives: 69.6 us -> none  [per_device(): lax.all_to_all(rows_back, axes, split_axis=0, concat_axis=0, tiled=True)]
    all_to_all x0 -> x1, waiting for transfers between devices: none -> 50.9 us  [per_device(): lax.all_to_all(rows_back, axes, split_axis=0, concat_axis=0, tiled=True)]
    all_to_all x0 -> x1, starting transfers between devices: none -> 16.8 us  [per_device(): lax.all_to_all(rows_back, axes, split_axis=0, concat_axis=0, tiled=True)]
    pallas_call x2, Pallas kernels: 66.3 us -> 53.1 us  [the longest x1 39.9 us: convs(): pl.pallas_call(conv_kernel, out_shape=(jax.ShapeDtypeStruct(middle.shape,...]
    pallas_call x1, Pallas kernels: 4.67 us -> 11 us  [pack(): pl.pallas_call(pack_kernel, out_shape=jax.ShapeDtypeStruct((owners, 2 * b...]
    pallas_call x1, Pallas kernels: 15.5 us -> 10.8 us  [gather(): pl.pallas_call(gather_kernel, out_shape=jax.ShapeDtypeStruct((owners, cha...]
    slice x2 -> x1, local copies, waits for them, and re-layouts: 2.84 us -> 0.01 us  [per_device(): right = lax.ppermute(middle[:, :PAIRS], 'tile', west)]
    reshape x0 -> x2, local copies, waits for them, and re-layouts: none -> 2.74 us  [the longest x1 2.35 us: per_device(): bev.reshape(cotangent.shape)]
  transfers between devices with their start and end apart: 11 -> 12, of which waited for: 4 -> 5; matrix products, arithmetic and copies ran while one was open for 6% -> 5% of each run, Pallas kernels for 7% -> 5%
where the time goes in v2:
time: 252 us; the launch traced here: 251 us
  waiting for transfers between devices  88.1 us (35%)
  Pallas kernels  84 us (33%)
  starting transfers between devices  50.6 us (20%)
  local copies, waits for them, and re-layouts  18.2 us (7%)
  other arithmetic  9.12 us (4%)
    all_to_all x1, waiting for transfers between devices, per_device(): lax.all_to_all(rows_back, axes, split_axis=0, concat_axis=0, tiled=True)  50.9 us
    pallas_call x1, Pallas kernels, convs(): pl.pallas_call(conv_kernel, out_shape=(jax.ShapeDtypeStruct(middle.shape,...  39.9 us
    ppermute x2, waiting for transfers between devices, with_sides(): lax.ppermute(tail, axis, down)  28.1 us
    all_to_all x1, starting transfers between devices, per_device(): lax.all_to_all(rows_back, axes, split_axis=0, concat_axis=0, tiled=True)  16.8 us
    pallas_call x1, Pallas kernels, splat(): pl.pallas_call(splat_kernel, out_shape=(jax.ShapeDtypeStruct(shape, BF),...  13.2 us
    unnamed x44, local copies, waits for them, and re-layouts  11.6 us
    pallas_call x1, Pallas kernels, pack(): pl.pallas_call(pack_kernel, out_shape=jax.ShapeDtypeStruct((owners, 2 * b...  11 us
    all_to_all x1, starting transfers between devices, per_device(): lax.all_to_all(sent, axes, split_axis=0, concat_axis=0, tiled=True)  10.9 us
  transfers between devices with their start and end apart: 12, of which 5 were waited for; matrix products, arithmetic and copies ran while one was open for 5% of the time, Pallas kernels for 5%

profile of v2, /device:TPU:6, one launch (start us, length us, event | category | flops | bytes accessed | tf_op | source)
XLA Modules:
  0.0 251.1 jit_solution(11397126790505380975)
XLA Ops:
  6.9 11.0 %pack.1 = bf16[128,136,128]{2,1,0:T(8,128)(2,1)S(1)} custom-call(s32[64]{0:T(128)S(1)} %reshape.39.owner, s32[64]{0:T(128)S(1)} %reshape.40.local, s32[64,64]{1,0:T(8,128)S(1)} %bitcast.18, bf16[64,64,128]{2,1,0:T(8,128)(2,1)S(1)} %bitcast.16, bf16[64,128,128]{2,1,0:T(8,128)(2,1)S(1)} %bitcast.14), custom_call_target="tpu_custom_call" | custom-call | tf_op jit(solution)/shard_map/pack/pallas_call | solution.py:110
  17.9 2.1 copy-done
  20.0 10.9 %all-to-all-start = ((bf16[128,136,128]{2,1,0:T(8,128)(2,1)}), bf16[128,136,128]{2,1,0:T(8,128)(2,1)}, u32[]{:S(2)}, u32[]{:S(2)}) async-start(bf16[128,136,128]{2,1,0:T(8,128)(2,1)} %copy-done), calls=%async_computation | async-start | bytes 8912896 | tf_op jit(solution)/shard_map/all_to_all | solution.py:464
  32.7 4.5 %collective-permute-start.6 = (bf16[16,8,256]{2,1,0:T(8,128)(2,1)S(1)}, bf16[16,8,256]{2,1,0:T(8,128)(2,1)S(1)}, u32[]{:S(2)}, u32[]{:S(2)}) collective-permute-start(bf16[16,8,256]{2,1,0:T(8,128)(2,1)S(1)} %get-tuple-element.18), channel_id=1, source_target_pairs={{0,1},{1,2},{2,3},{3,4},{4,5},{5,6},{6,7},{7,8},{8,9},{9,10},{10,1... | collective-permute-start | bytes 196616 | tf_op jit(solution)/shard_map/ppermute | solution.py:33
  37.7 2.8 %copy.10 = bf16[4,3,4,128,256]{4,3,2,1,0:T(8,128)(2,1)} copy(bf16[4,3,4,128,256]{3,4,2,1,0:T(8,128)(2,1)S(1)} %fusion.4) | data formatting | bytes 6291456 | tf_op jit(solution)/shard_map/concatenate | solution.py:445
  40.5 2.2 fusion.5
  43.1 3.2 %pad_maximum_fusion.weights = bf16[8,1536,256]{2,1,0:T(8,128)(2,1)} fusion(bf16[4,1536,256]{2,1,0:T(8,128)(2,1)S(1)} %bitcast.19, bf16[4,1536,256]{2,1,0:T(8,128)(2,1)S(1)} %bitcast.20), kind=kLoop, calls=%fused_computation.4 | loop fusion | flops 3145728 | bytes 12582912 | tf_op jit(solution)/shard_map/concatenate | solution.py:469
  46.9 28.1 %collective-permute-done.6 = bf16[16,8,256]{2,1,0:T(8,128)(2,1)S(1)} collective-permute-done((bf16[16,8,256]{2,1,0:T(8,128)(2,1)S(1)}, bf16[16,8,256]{2,1,0:T(8,128)(2,1)S(1)}, u32[]{:S(2)}, u32[]{:S(2)}) %collective-permute-start.6) | collective-permute-done | bytes 65568 | tf_op jit(solution)/shard_map/ppermute | solution.py:33
  75.1 2.8 %collective-permute-start.8 = (bf16[4,144,256]{2,1,0:T(8,128)(2,1)S(1)}, bf16[4,144,256]{2,1,0:T(8,128)(2,1)S(1)}, u32[]{:S(2)}, u32[]{:S(2)}) collective-permute-start(bf16[4,144,256]{2,1,0:T(8,128)(2,1)S(1)} %get-tuple-element.15), channel_id=1, source_target_pairs={{0,16},{16,32},{32,48},{48,64},{64,80},{80,96},{96,112},{1,17},{17... | collective-permute-start | bytes 884744 | tf_op jit(solution)/shard_map/ppermute | solution.py:33
  78.0 2.8 %collective-permute-start.9 = (bf16[4,144,256]{2,1,0:T(8,128)(2,1)S(1)}, bf16[4,144,256]{2,1,0:T(8,128)(2,1)S(1)}, u32[]{:S(2)}, u32[]{:S(2)}) collective-permute-start(bf16[4,144,256]{2,1,0:T(8,128)(2,1)S(1)} %get-tuple-element.16), channel_id=1, source_target_pairs={{16,0},{32,16},{48,32},{64,48},{80,64},{96,80},{112,96},{17,1},{33... | collective-permute-start | bytes 884744 | tf_op jit(solution)/shard_map/ppermute | solution.py:33
  80.7 6.5 %all-to-all-done.meta_all.message = bf16[128,136,128]{2,1,0:T(8,128)(2,1)} async-done(((bf16[128,136,128]{2,1,0:T(8,128)(2,1)}), bf16[128,136,128]{2,1,0:T(8,128)(2,1)}, u32[]{:S(2)}, u32[]{:S(2)}) %all-to-all-start) | async-done | bytes 4456480 | tf_op jit(solution)/shard_map/all_to_all | solution.py:464
  87.2 13.2 %splat.1 = (bf16[16,128,256]{2,1,0:T(8,128)(2,1)S(1)}, s32[2,128]{1,0:T(2,128)S(1)}) custom-call(bf16[128,136,128]{2,1,0:T(8,128)(2,1)} %all-to-all-done.meta_all.message, bf16[128,136,128]{2,1,0:T(8,128)(2,1)} %all-to-all-done.meta_all.message), custom_call_target="tpu_custom_call" | custom-call | tf_op jit(solution)/shard_map/splat/pallas_call | solution.py:193
  103.2 1.9 collective-permute-start.1
  105.1 2.4 collective-permute-start
  108.1 2.7 %collective-permute-start.5 = (bf16[8,16,256]{2,1,0:T(8,128)(2,1)S(1)}, bf16[8,16,256]{2,1,0:T(8,128)(2,1)S(1)}, u32[]{:S(2)}, u32[]{:S(2)}) collective-permute-start(bf16[8,16,256]{2,1,0:T(8,128)(2,1)S(1)} %get-tuple-element.23), channel_id=1, source_target_pairs={{16,0},{32,16},{48,32},{64,48},{80,64},{96,80},{112,96},{17,1},{33... | collective-permute-start | bytes 196616 | tf_op jit(solution)/shard_map/ppermute | solution.py:486
  110.8 1.9 collective-permute-start.4
  114.2 2.2 collective-permute-done.4.corner_above
  118.1 39.9 %convs.1 = (bf16[16,128,256]{2,1,0:T(8,128)(2,1)}, bf16[16,128,256]{2,1,0:T(8,128)(2,1)}) custom-call(s32[4]{0:T(128)} %add_convert_fusion.edges, bf16[16,128,256]{2,1,0:T(8,128)(2,1)} %copy-done.4, bf16[8,128,256]{2,1,0:T(8,128)(2,1)} %copy-done.15, bf16[8,128,256]{2,1,0:T(8,128)(2,1)} %copy-done.14, bf16[16,8,256]{2,1,0:T(8,128)(2,1)} %copy-done.16, ...), custom_call_target="tpu_custom_call" | custom-call | tf_op jit(solution)/shard_map/convs/pallas_call | solution.py:328
  159.2 10.8 %gather.1 = bf16[128,128,128]{2,1,0:T(8,128)(2,1)S(1)} custom-call(s32[2,128]{1,0:T(2,128)S(1)} %get-tuple-element.11.tiles, bf16[128,136,128]{2,1,0:T(8,128)(2,1)} %all-to-all-done.meta_all.message, bf16[16,128,256]{2,1,0:T(8,128)(2,1)S(1)} %copy-done.7), custom_call_target="tpu_custom_call" | custom-call | tf_op jit(solution)/shard_map/gather/pallas_call | solution.py:379
  170.0 2.0 copy-done.1
  172.0 16.8 %all-to-all-start.1 = ((bf16[128,128,128]{2,1,0:T(8,128)(2,1)}), bf16[128,128,128]{2,1,0:T(8,128)(2,1)}, u32[]{:S(2)}, u32[]{:S(2)}) async-start(bf16[128,128,128]{2,1,0:T(8,128)(2,1)} %copy-done.1), calls=%async_computation.1 | async-start | bytes 8388608 | tf_op jit(solution)/shard_map/all_to_all | solution.py:492
  188.8 2.3 reshape.47
  191.2 50.9 %all-to-all-done.1.returned = bf16[128,128,128]{2,1,0:T(8,128)(2,1)} async-done(((bf16[128,128,128]{2,1,0:T(8,128)(2,1)}), bf16[128,128,128]{2,1,0:T(8,128)(2,1)}, u32[]{:S(2)}, u32[]{:S(2)}) %all-to-all-start.1) | async-done | bytes 4194336 | tf_op jit(solution)/shard_map/all_to_all | solution.py:492
  242.0 9.0 %final.1 = (bf16[64,64,128]{2,1,0:T(8,128)(2,1)}, bf16[64,128,128]{2,1,0:T(8,128)(2,1)}) custom-call(s32[64]{0:T(128)S(1)} %reshape.39.owner, bf16[128,128,128]{2,1,0:T(8,128)(2,1)} %all-to-all-done.1.returned, bf16[64,64,128]{2,1,0:T(8,128)(2,1)S(1)} %bitcast.17, bf16[64,128,128]{2,1,0:T(8,128)(2,1)S(1)} %bitcast.15), custom_call_target="tpu_custom_call" | custom-call | tf_op jit(solution)/shard_map/final/pallas_call | solution.py:426
  (68 shorter events, 17.0 us)
Async XLA Ops:
  17.9 2.1 copy-start
  20.0 10.9 %copy-start.13 = (bf16[16,256,128]{2,1,0:T(8,128)(2,1)S(1)}, bf16[16,256,128]{2,1,0:T(8,128)(2,1)}, u32[]{:S(2)}) copy-start(bf16[16,256,128]{2,1,0:T(8,128)(2,1)} %param.13) | copy-start | bytes 3145732
  20.0 67.2 %all-to-all-start = ((bf16[128,136,128]{2,1,0:T(8,128)(2,1)}), bf16[128,136,128]{2,1,0:T(8,128)(2,1)}, u32[]{:S(2)}, u32[]{:S(2)}) async-start(bf16[128,136,128]{2,1,0:T(8,128)(2,1)} %copy-done), calls=%async_computation | async-start | bytes 8912896 | tf_op jit(solution)/shard_map/all_to_all | solution.py:464
  30.9 6.3 %copy-start.12 = (bf16[4,3,3,128,128]{4,3,2,1,0:T(8,128)(2,1)S(1)}, bf16[4,3,3,128,128]{4,3,2,1,0:T(8,128)(2,1)}, u32[]{:S(2)}) copy-start(bf16[4,3,3,128,128]{4,3,2,1,0:T(8,128)(2,1)} %param.12) | copy-start | bytes 3538948
  31.3 5.9 %copy-start.10 = (bf16[16,128,256]{2,1,0:T(8,128)(2,1)}, bf16[16,128,256]{2,1,0:T(8,128)(2,1)S(1)}, u32[]{:S(2)}) copy-start(bf16[16,128,256]{2,1,0:T(8,128)(2,1)S(1)} %reshape.44) | copy-start | bytes 3145732
  31.4 43.7 %collective-permute-start.7 = (bf16[16,8,256]{2,1,0:T(8,128)(2,1)S(1)}, bf16[16,8,256]{2,1,0:T(8,128)(2,1)S(1)}, u32[]{:S(2)}, u32[]{:S(2)}) collective-permute-start(bf16[16,8,256]{2,1,0:T(8,128)(2,1)S(1)} %get-tuple-element.17), channel_id=1, source_target_pairs={{1,0},{2,1},{3,2},{4,3},{5,4},{6,5},{7,6},{8,7},{9,8},{10,9},{11,1... | collective-permute-start | bytes 196616 | tf_op jit(solution)/shard_map/ppermute | solution.py:33
  32.7 42.3 %collective-permute-start.6 = (bf16[16,8,256]{2,1,0:T(8,128)(2,1)S(1)}, bf16[16,8,256]{2,1,0:T(8,128)(2,1)S(1)}, u32[]{:S(2)}, u32[]{:S(2)}) collective-permute-start(bf16[16,8,256]{2,1,0:T(8,128)(2,1)S(1)} %get-tuple-element.18), channel_id=1, source_target_pairs={{0,1},{1,2},{2,3},{3,4},{4,5},{5,6},{6,7},{7,8},{8,9},{9,10},{10,1... | collective-permute-start | bytes 196616 | tf_op jit(solution)/shard_map/ppermute | solution.py:33
  40.5 2.6 %copy-start.9 = (bf16[4,3,4,128,256]{4,3,2,1,0:T(8,128)(2,1)S(1)}, bf16[4,3,4,128,256]{4,3,2,1,0:T(8,128)(2,1)}, u32[]{:S(2)}) copy-start(bf16[4,3,4,128,256]{4,3,2,1,0:T(8,128)(2,1)} %copy.10) | copy-start | bytes 9437188
  43.1 31.9 %copy-start.11 = (bf16[16,128,256]{2,1,0:T(8,128)(2,1)S(1)}, bf16[16,128,256]{2,1,0:T(8,128)(2,1)}, u32[]{:S(2)}) copy-start(bf16[16,128,256]{2,1,0:T(8,128)(2,1)} %copy-done.10) | copy-start | bytes 3145732
  75.1 35.6 %collective-permute-start.8 = (bf16[4,144,256]{2,1,0:T(8,128)(2,1)S(1)}, bf16[4,144,256]{2,1,0:T(8,128)(2,1)S(1)}, u32[]{:S(2)}, u32[]{:S(2)}) collective-permute-start(bf16[4,144,256]{2,1,0:T(8,128)(2,1)S(1)} %get-tuple-element.15), channel_id=1, source_target_pairs={{0,16},{16,32},{32,48},{48,64},{64,80},{80,96},{96,112},{1,17},{17... | collective-permute-start | bytes 884744 | tf_op jit(solution)/shard_map/ppermute | solution.py:33
  78.0 34.8 %collective-permute-start.9 = (bf16[4,144,256]{2,1,0:T(8,128)(2,1)S(1)}, bf16[4,144,256]{2,1,0:T(8,128)(2,1)S(1)}, u32[]{:S(2)}, u32[]{:S(2)}) collective-permute-start(bf16[4,144,256]{2,1,0:T(8,128)(2,1)S(1)} %get-tuple-element.16), channel_id=1, source_target_pairs={{16,0},{32,16},{48,32},{64,48},{80,64},{96,80},{112,96},{17,1},{33... | collective-permute-start | bytes 884744 | tf_op jit(solution)/shard_map/ppermute | solution.py:33
  100.5 13.7 %copy-start.4 = (bf16[16,128,256]{2,1,0:T(8,128)(2,1)}, bf16[16,128,256]{2,1,0:T(8,128)(2,1)S(1)}, u32[]{:S(2)}) copy-start(bf16[16,128,256]{2,1,0:T(8,128)(2,1)S(1)} %get-tuple-element.9.middle) | copy-start | bytes 3145732
  100.5 4.6 %collective-permute-start.2 = (bf16[16,8,256]{2,1,0:T(8,128)(2,1)S(1)}, bf16[16,8,256]{2,1,0:T(8,128)(2,1)S(1)}, u32[]{:S(2)}, u32[]{:S(2)}) collective-permute-start(bf16[16,8,256]{2,1,0:T(8,128)(2,1)S(1)} %get-tuple-element.20), channel_id=1, source_target_pairs={{0,1},{1,2},{2,3},{3,4},{4,5},{5,6},{6,7},{7,8},{8,9},{9,10},{10,1... | collective-permute-start | bytes 196616 | tf_op jit(solution)/shard_map/ppermute | solution.py:482
  101.9 6.2 %collective-permute-start.3 = (bf16[16,8,256]{2,1,0:T(8,128)(2,1)S(1)}, bf16[16,8,256]{2,1,0:T(8,128)(2,1)S(1)}, u32[]{:S(2)}, u32[]{:S(2)}) collective-permute-start(bf16[16,8,256]{2,1,0:T(8,128)(2,1)S(1)} %get-tuple-element.19), channel_id=1, source_target_pairs={{1,0},{2,1},{3,2},{4,3},{5,4},{6,5},{7,6},{8,7},{9,8},{10,9},{11,1... | collective-permute-start | bytes 196616 | tf_op jit(solution)/shard_map/ppermute | solution.py:483
  103.2 13.2 %collective-permute-start.1 = (bf16[8,128,256]{2,1,0:T(8,128)(2,1)S(1)}, bf16[8,128,256]{2,1,0:T(8,128)(2,1)S(1)}, u32[]{:S(2)}, u32[]{:S(2)}) collective-permute-start(bf16[8,128,256]{2,1,0:T(8,128)(2,1)S(1)} %get-tuple-element.21), channel_id=1, source_target_pairs={{16,0},{32,16},{48,32},{64,48},{80,64},{96,80},{112,96},{17,1},{33... | collective-permute-start | bytes 1572872 | tf_op jit(solution)/shard_map/ppermute | solution.py:481
  105.1 11.3 %copy-start.16 = (bf16[16,8,256]{2,1,0:T(8,128)(2,1)}, bf16[16,8,256]{2,1,0:T(8,128)(2,1)S(1)}, u32[]{:S(2)}) copy-start(bf16[16,8,256]{2,1,0:T(8,128)(2,1)S(1)} %collective-permute-done.2.left) | copy-start | bytes 196612
  105.1 11.3 %collective-permute-start = (bf16[8,128,256]{2,1,0:T(8,128)(2,1)S(1)}, bf16[8,128,256]{2,1,0:T(8,128)(2,1)S(1)}, u32[]{:S(2)}, u32[]{:S(2)}) collective-permute-start(bf16[8,128,256]{2,1,0:T(8,128)(2,1)S(1)} %get-tuple-element.22), channel_id=1, source_target_pairs={{0,16},{16,32},{32,48},{48,64},{64,80},{80,96},{96,112},{1,17},{17... | collective-permute-start | bytes 1572872 | tf_op jit(solution)/shard_map/ppermute | solution.py:480
  108.0 8.4 %copy-start.17 = (bf16[16,8,256]{2,1,0:T(8,128)(2,1)}, bf16[16,8,256]{2,1,0:T(8,128)(2,1)S(1)}, u32[]{:S(2)}) copy-start(bf16[16,8,256]{2,1,0:T(8,128)(2,1)S(1)} %collective-permute-done.3.right) | copy-start | bytes 196612
  108.1 6.1 %collective-permute-start.5 = (bf16[8,16,256]{2,1,0:T(8,128)(2,1)S(1)}, bf16[8,16,256]{2,1,0:T(8,128)(2,1)S(1)}, u32[]{:S(2)}, u32[]{:S(2)}) collective-permute-start(bf16[8,16,256]{2,1,0:T(8,128)(2,1)S(1)} %get-tuple-element.23), channel_id=1, source_target_pairs={{16,0},{32,16},{48,32},{64,48},{80,64},{96,80},{112,96},{17,1},{33... | collective-permute-start | bytes 196616 | tf_op jit(solution)/shard_map/ppermute | solution.py:486
  110.8 5.6 %collective-permute-start.4 = (bf16[8,16,256]{2,1,0:T(8,128)(2,1)S(1)}, bf16[8,16,256]{2,1,0:T(8,128)(2,1)S(1)}, u32[]{:S(2)}, u32[]{:S(2)}) collective-permute-start(bf16[8,16,256]{2,1,0:T(8,128)(2,1)S(1)} %get-tuple-element.24), channel_id=1, source_target_pairs={{0,16},{16,32},{32,48},{48,64},{64,80},{80,96},{96,112},{1,17},{17... | collective-permute-start | bytes 196616 | tf_op jit(solution)/shard_map/ppermute | solution.py:485
  114.2 2.2 copy-start.18
  172.0 70.0 %copy-start.6 = (bf16[4,16,64,128]{3,2,1,0:T(8,128)(2,1)S(1)}, bf16[4,16,64,128]{3,2,1,0:T(8,128)(2,1)}, u32[]{:S(2)}) copy-start(bf16[4,16,64,128]{3,2,1,0:T(8,128)(2,1)} %param.7) | copy-start | bytes 3145732
  172.0 70.0 %all-to-all-start.1 = ((bf16[128,128,128]{2,1,0:T(8,128)(2,1)}), bf16[128,128,128]{2,1,0:T(8,128)(2,1)}, u32[]{:S(2)}, u32[]{:S(2)}) async-start(bf16[128,128,128]{2,1,0:T(8,128)(2,1)} %copy-done.1), calls=%async_computation.1 | async-start | bytes 8388608 | tf_op jit(solution)/shard_map/all_to_all | solution.py:492
  188.8 53.2 %copy-start.3 = (bf16[4,16,128,128]{3,2,1,0:T(8,128)(2,1)S(1)}, bf16[4,16,128,128]{3,2,1,0:T(8,128)(2,1)}, u32[]{:S(2)}) copy-start(bf16[4,16,128,128]{3,2,1,0:T(8,128)(2,1)} %param.8) | copy-start | bytes 6291460
  (8 other events, 9.1 us)

commit v3 on v2

--- a/solution.py
+++ b/solution.py
@@ -1,3 +1,5 @@
+import functools
+
 import jax
 import jax.numpy as jnp
 from jax import lax
@@ -9,7 +11,6 @@
 LAYERS = 4
 EXT = 2 * LAYERS
 PAIRS = 8
-CHUNK = 4
 EMPTY = 256.0
 ABSENT = 255
 BF = jnp.bfloat16
@@ -41,16 +42,24 @@
 
 
 def clear_counts(count, size):
-    @pl.loop(0, size)
-    def _(i):
+    for i in range(size):
         count[i] = 0
+
+
+def in_hbm(x):
+    return pltpu.with_memory_space_constraint(x, pltpu.HBM)
+
+
+def spot_of(spots, at, tiles):
+    value = spots[at // spots.shape[1], at % spots.shape[1]]
+    return value // tiles, value % tiles
 
 
 def pair_cells(cells):
     return (cells // TS) * TS + (cells % 2) * (TS // 2) + (cells % TS) // 2
 
 
-def pack_kernel(owner, local, cells, depth, context, out, count, wide, lifted, meta, sems):
+def pack_kernel(tile_count, spots, cells, depth, context, out, count, wide, lifted, meta, sems):
     step = pl.program_id(0)
     blocks, bins, _ = depth.shape
     owners = out.shape[0]
@@ -68,14 +77,14 @@
 
     def block(b, carry):
         at = step * blocks + b
-        to = owner[at]
+        to, local = spot_of(spots, at, tile_count)
         rank = take_slot(to, count)
         product = jnp.dot(depth[b], context[b], preferred_element_type=F32)
         lifted[at // 2, pl.ds(pl.multiple_of((at % 2) * bins, bins), bins), :] = product.astype(BF)
         mine = (lane // bins) == rank
         row = wide[pl.ds(at, 1), :]
         meta[to, pl.ds(0, 1), :] = jnp.where(mine, row, meta[to, pl.ds(0, 1), :])
-        tile = local[at].astype(F32)
+        tile = local.astype(F32)
         meta[to, pl.ds(1, 1), :] = jnp.where(mine, tile, meta[to, pl.ds(1, 1), :])
         pltpu.make_async_copy(
             lifted.at[at // 2, pl.ds(pl.multiple_of((at % 2) * bins, bins), bins), :],
@@ -102,18 +111,16 @@
         ).wait()
 
 
-def pack(owner, local, cells, depth, context, owners):
+def pack(spots, cells, depth, context, owners, tile_count):
     blocks, bins, pixels = depth.shape
     channels = context.shape[2]
     chunk = blocks // 4
-    smem = pl.BlockSpec(memory_space=pltpu.SMEM)
     return pl.pallas_call(
-        pack_kernel,
-        out_shape=jax.ShapeDtypeStruct((owners, 2 * bins + 8, channels), BF),
+        functools.partial(pack_kernel, tile_count),
+        out_shape=pltpu.HBM((owners, 2 * bins + 8, channels), BF),
         grid=(blocks // chunk,),
         in_specs=[
-            smem,
-            smem,
+            pl.BlockSpec(memory_space=pltpu.SMEM),
             pl.BlockSpec(cells.shape, lambda i: (0, 0)),
             pl.BlockSpec((chunk, bins, pixels), lambda i: (i, 0, 0)),
             pl.BlockSpec((chunk, pixels, channels), lambda i: (i, 0, 0)),
@@ -126,9 +133,9 @@
             pltpu.VMEM((owners, 8, 2 * bins), F32),
             pltpu.SemaphoreType.DMA((2,)),
         ],
-        compiler_params=pltpu.CompilerParams(vmem_limit_bytes=40 << 20),
+        compiler_params=pltpu.CompilerParams(vmem_limit_bytes=24 << 20),
         name="pack",
-    )(owner, local, cells, depth, context)
+    )(spots, cells, depth, context)
 
 
 def cell_onehot(cell_row, cells):
@@ -217,18 +224,34 @@
     )(message, message)
 
 
+def chunks_of(count):
+    parts = -(-count // 7)
+    size = -(-count // parts)
+    return size, [min(i * size, count - size) for i in range(parts)]
+
+
 def conv_kernel(
-    edges, middle, above, below, left, right, corner_above, corner_below, cot, weights,
-    bev, grad, ping, pong, slopes, half,
+    edges, middle, above, below, left, right, corner_above, corner_below, cot_far, weights_far,
+    bev, grad, ping, pong, slopes, mask, sums, weights, cot, sems,
 ):
     rows, mid, double = middle.shape
     channels = double // 2
     wide = mid + 2 * PAIRS
     tall = rows + 2 * EXT
+    arrivals = [
+        pltpu.make_async_copy(weights_far.at[i], weights.at[i], sems.at[i])
+        for i in range(2 * LAYERS)
+    ]
+    cot_arrival = pltpu.make_async_copy(cot_far, cot, sems.at[2 * LAYERS])
+    for copy in arrivals[:LAYERS]:
+        copy.start()
+    cot_arrival.start()
+    for copy in arrivals[: LAYERS - 1 : -1]:
+        copy.start()
     column = lax.broadcasted_iota(jnp.int32, (wide, double), 0)
     gone = ((column < PAIRS) & (edges[2] == 1)) | ((column >= wide - PAIRS) & (edges[3] == 1))
-    half[0] = jnp.zeros((wide, double), F32)
-    half[1] = jnp.where(gone, 0.0, 0.5)
+    mask[0] = jnp.zeros((wide, double), F32)
+    mask[1] = jnp.where(gone, 0.0, 1.0)
 
     def put(ref, row, value):
         first = value[:, :channels]
@@ -255,67 +278,72 @@
     lax.fori_loop(0, EXT, load_outer, 0)
     lax.fori_loop(0, rows, load_inner, 0)
 
-    def conv(ref, row, layer, chunk):
-        taps = [
-            ref[pl.ds(row + tap, chunk)].reshape(chunk * wide, 2 * double) for tap in range(3)
-        ]
-        return jnp.dot(
-            jnp.concatenate(taps, axis=1), weights[layer], preferred_element_type=F32
-        ).reshape(chunk, wide, double)
-
-    source, target = ping, pong
-    offset = 0
-    offsets = []
+    def matmul(ref, index, start, size):
+        taps = [ref[pl.ds(start + tap, size)].reshape(size * wide, 2 * double) for tap in range(3)]
+        total = jnp.dot(
+            jnp.concatenate(taps, axis=1), weights[index], preferred_element_type=F32
+        )
+        sums[0:size] = total.reshape(size, wide, double)
+
+    kept = [tall - 2 - 2 * layer for layer in range(LAYERS)]
+    offsets = [sum(kept[:layer]) for layer in range(LAYERS)]
+
+    def forward(layer, target, start, size):
+        for side in range(size):
+            here = start + side
+            row = layer + 1 + here
+            inside = jnp.where(
+                ((row < EXT) & (edges[0] == 1)) | ((row >= EXT + rows) & (edges[1] == 1)), 0, 1
+            )
+            part = sums[side]
+            flag = mask[inside]
+            twice = flag + flag * jnp.tanh(part)
+            active = part * twice
+            slope = twice + active * (2.0 - twice)
+            if layer < LAYERS - 1:
+                put(target, here, active)
+                slopes[offsets[layer] + here] = slope.astype(slopes.dtype)
+            else:
+                bev[here] = active[PAIRS : PAIRS + mid].astype(BF)
+                put(target, here, cot[here].astype(F32) * slope)
+
+    def backward(step, target, start, size):
+        layer = LAYERS - 1 - step
+        for side in range(size):
+            here = start + side
+            if layer > 0:
+                slope = slopes[offsets[layer - 1] + here + 2 * (step + 1)].astype(F32)
+                put(target, here, sums[side] * slope)
+            else:
+                grad[here] = sums[side, PAIRS : PAIRS + mid].astype(BF)
+
+    stages = []
     for layer in range(LAYERS):
-        count = tall - 2 - 2 * layer
-        offsets.append(offset)
-
-        def forward(k, carry, layer=layer, source=source, target=target, offset=offset, count=count):
-            start = jnp.minimum(k * CHUNK, count - CHUNK)
-            total = conv(source, start, layer, CHUNK)
-            for side in range(CHUNK):
-                here = start + side
-                row = layer + 1 + here
-                inside = jnp.where(
-                    ((row < EXT) & (edges[0] == 1)) | ((row >= EXT + rows) & (edges[1] == 1)), 0, 1
-                )
-                preact = total[side]
-                scale = half[inside]
-                sigma = scale + scale * jnp.tanh(0.5 * preact)
-                active = preact * sigma
-                slope = sigma + (active - active * sigma)
-                if layer < LAYERS - 1:
-                    put(target, here, active)
-                    slopes[offset + here] = slope
-                else:
-                    @pl.when((row >= EXT) & (row < EXT + rows))
-                    def _(row=row, active=active):
-                        bev[row - EXT] = active[PAIRS : PAIRS + mid].astype(BF)
-
-                    put(target, here, cot[here].astype(F32) * slope)
-            return carry
-
-        lax.fori_loop(0, -(-count // CHUNK), forward, 0)
-        offset += count
-        source, target = target, source
-
+        stages.append((layer, kept[layer], functools.partial(forward, layer)))
     for step in range(LAYERS):
         layer = LAYERS - 1 - step
-        count = rows + 2 * layer
-
-        def backward(k, carry, layer=layer, source=source, target=target, step=step, count=count):
-            start = jnp.minimum(k * CHUNK, count - CHUNK)
-            total = conv(source, start, LAYERS + layer, CHUNK)
-            for side in range(CHUNK):
-                here = start + side
-                if layer > 0:
-                    put(target, here, total[side] * slopes[offsets[layer - 1] + here + 2 * (step + 1)])
-                else:
-                    grad[here] = total[side, PAIRS : PAIRS + mid].astype(BF)
+        stages.append((LAYERS + layer, rows + 2 * layer, functools.partial(backward, step)))
+
+    source, target = ping, pong
+    finish = None
+    for index, count, epilogue in stages:
+        size, starts = chunks_of(count)
+        arrivals[index].wait()
+        if finish is not None:
+            finish()
+        matmul(source, index, 0, size)
+        if index == LAYERS - 1:
+            cot_arrival.wait()
+
+        def steady(k, carry, index=index, count=count, size=size, source=source, target=target, epilogue=epilogue):
+            epilogue(target, (k - 1) * size, size)
+            matmul(source, index, jnp.minimum(k * size, count - size), size)
             return carry
 
-        lax.fori_loop(0, -(-count // CHUNK), backward, 0)
+        lax.fori_loop(1, len(starts), steady, 0)
+        finish = functools.partial(epilogue, target, starts[-1], size)
         source, target = target, source
+    finish()
 
 
 def convs(edges, middle, above, below, left, right, corner_above, corner_below, cot, weights):
@@ -324,24 +352,32 @@
     tall = rows + 2 * EXT
     kept = sum(tall - 2 - 2 * layer for layer in range(LAYERS - 1))
     vmem = pl.BlockSpec(memory_space=pltpu.VMEM)
+    hbm = pl.BlockSpec(memory_space=pltpu.HBM)
     buffer = pltpu.VMEM((tall, wide, 2 * double), BF)
     return pl.pallas_call(
         conv_kernel,
         out_shape=(
-            jax.ShapeDtypeStruct(middle.shape, BF),
+            jax.ShapeDtypeStruct((rows + 2 * LAYERS, mid, double), BF),
             jax.ShapeDtypeStruct(middle.shape, BF),
         ),
-        in_specs=[pl.BlockSpec(memory_space=pltpu.SMEM)] + [vmem] * 9,
+        in_specs=[pl.BlockSpec(memory_space=pltpu.SMEM)] + [vmem] * 7 + [hbm] * 2,
         out_specs=(vmem, vmem),
         scratch_shapes=[
             buffer,
             buffer,
             pltpu.VMEM((kept, wide, double), F32),
             pltpu.VMEM((2, wide, double), F32),
+            pltpu.VMEM((7, wide, double), F32),
+            pltpu.VMEM(weights.shape, BF),
+            pltpu.VMEM(cot.shape, BF),
+            pltpu.SemaphoreType.DMA((2 * LAYERS + 1,)),
         ],
-        compiler_params=pltpu.CompilerParams(vmem_limit_bytes=60 << 20),
+        compiler_params=pltpu.CompilerParams(vmem_limit_bytes=48 << 20),
         name="convs",
-    )(edges, middle, above, below, left, right, corner_above, corner_below, cot, weights)
+    )(
+        edges, middle, above, below, left, right, corner_above, corner_below,
+        in_hbm(cot), in_hbm(weights),
+    )
 
 
 def gather_kernel(tiles, message, grad, out, turned):
@@ -378,7 +414,7 @@
     chunk = owners // 8
     return pl.pallas_call(
         gather_kernel,
-        out_shape=jax.ShapeDtypeStruct((owners, channels, height - 8), BF),
+        out_shape=pltpu.HBM((owners, channels, height - 8), BF),
         grid=(owners // chunk,),
         in_specs=[
             pl.BlockSpec(memory_space=pltpu.SMEM),
@@ -392,7 +428,7 @@
     )(tiles, message, grad)
 
 
-def final_kernel(owner, returned, depth, context, grad_depth, grad_context, count):
+def final_kernel(tile_count, spots, returned, depth, context, grad_depth, grad_context, count):
     step = pl.program_id(0)
     blocks, bins, _ = depth.shape
 
@@ -401,10 +437,10 @@
         clear_counts(count, returned.shape[0])
 
     def block(b, carry):
-        to = owner[step * blocks + b]
+        to, _ = spot_of(spots, step * blocks + b, tile_count)
         rank = take_slot(to, count)
-        turned = returned[to].astype(F32).T
-        rows = jnp.where(rank == 0, turned[0:bins], turned[bins : 2 * bins]).astype(BF)
+        turned = returned[to].T
+        rows = jnp.where(rank == 0, turned[0:bins], turned[bins : 2 * bins])
         grad_depth[b] = lax.dot_general(
             rows, context[b], (((1,), (1,)), ((), ())), preferred_element_type=F32
         ).astype(BF)
@@ -416,7 +452,7 @@
     lax.fori_loop(0, blocks, block, 0, unroll=4)
 
 
-def final(owner, returned, depth, context):
+def final(spots, returned, depth, context, tile_count):
     blocks, bins, pixels = depth.shape
     channels = context.shape[2]
     chunk = blocks // 4
@@ -424,7 +460,7 @@
     depth_block = pl.BlockSpec((chunk, bins, pixels), lambda i: (i, 0, 0))
     context_block = pl.BlockSpec((chunk, pixels, channels), lambda i: (i, 0, 0))
     return pl.pallas_call(
-        final_kernel,
+        functools.partial(final_kernel, tile_count),
         out_shape=(
             jax.ShapeDtypeStruct(depth.shape, BF),
             jax.ShapeDtypeStruct(context.shape, BF),
@@ -435,7 +471,7 @@
         scratch_shapes=[pltpu.SMEM((returned.shape[0],), jnp.int32)],
         compiler_params=pltpu.CompilerParams(vmem_limit_bytes=40 << 20),
         name="final",
-    )(owner, returned, depth, context)
+    )(spots, in_hbm(returned), depth, context)
 
 
 def paired_weights(kernel):
@@ -457,16 +493,19 @@
     blocks = cams_here * blocks_cam
     depth = depth_weights.reshape(blocks, bins, pixels)
     flat_context = context.reshape(blocks, pixels, channels)
-    owner = block_owner.reshape(blocks)
-    local = block_local.reshape(blocks)
-
-    sent = pack(owner, local, block_cell.reshape(blocks, bins), depth, flat_context, owners)
+    tile_count = cols // TS
+    spots = block_owner[:, :, 0] * tile_count + block_local
+
+    sent = pack(
+        spots, block_cell.reshape(blocks, bins), in_hbm(depth), in_hbm(flat_context), owners, tile_count
+    )
     message = lax.all_to_all(sent, axes, split_axis=0, concat_axis=0, tiled=True)
 
     cot = cotangent.reshape(rows, mid, 2 * channels)
     cot = with_sides(with_sides(cot, "tile", 1, PAIRS), "cam", 0, LAYERS)
     turned_weight = conv_weight[:, ::-1, ::-1].swapaxes(3, 4)
     weights = jnp.concatenate([paired_weights(conv_weight), paired_weights(turned_weight)], axis=0)
+    weights = weights * jnp.asarray(0.5, BF)
     cam = lax.axis_index("cam")
     tile = lax.axis_index("tile")
     edges = jnp.stack(
@@ -490,9 +529,11 @@
     )
     rows_back = gather(tiles, message, grad)
     returned = lax.all_to_all(rows_back, axes, split_axis=0, concat_axis=0, tiled=True)
-    grad_depth, grad_context = final(owner, returned, depth, flat_context)
+    grad_depth, grad_context = final(
+        spots, returned, in_hbm(depth), in_hbm(flat_context), tile_count
+    )
     return (
-        bev.reshape(cotangent.shape),
+        bev[LAYERS : LAYERS + rows].reshape(cotangent.shape),
         grad_depth.reshape(depth_weights.shape),
         grad_context.reshape(context.shape),
     )

time: 252 us -> 226 us (0.90)
  Pallas kernels: 84 us -> 69.7 us
  local copies, waits for them, and re-layouts: 18.2 us -> 6.01 us
    pallas_call x4, Pallas kernels: 70.7 us -> 56.4 us  [the longest x1 30.8 us: convs(): pl.pallas_call(conv_kernel, out_shape=(jax.ShapeDtypeStruct((rows + 2 * L...]
    unnamed x44 -> x15, local copies, waits for them, and re-layouts: 11.6 us -> 1.25 us
    mul x0 -> x2, other arithmetic: none -> 3.88 us  [the longest x1 3.19 us: per_device(): weights = weights * jnp.asarray(0.5, BF)]
    concatenate x1 -> x0, other arithmetic: 3.18 us -> none  [per_device(): jnp.concatenate([paired_weights(conv_weight), paired_weights(turned_weigh...]
  transfers between devices with their start and end apart: 12 -> 12, of which waited for: 5 -> 5; matrix products, arithmetic and copies ran while one was open for 5% -> 5% of each run, Pallas kernels for 5% -> 6%
where the time goes in v3:
time: 226 us
  waiting for transfers between devices  89.5 us (40%)
  Pallas kernels  69.7 us (31%)
  starting transfers between devices  50.7 us (22%)
  other arithmetic  8.62 us (4%)
  local copies, waits for them, and re-layouts  6.01 us (3%)
    all_to_all x1, waiting for transfers between devices, per_device(): lax.all_to_all(rows_back, axes, split_axis=0, concat_axis=0, tiled=True)  52 us
    pallas_call x1, Pallas kernels, convs(): pl.pallas_call(conv_kernel, out_shape=(jax.ShapeDtypeStruct((rows + 2 * L...  30.8 us
    ppermute x2, waiting for transfers between devices, with_sides(): lax.ppermute(tail, axis, down)  28.6 us
    all_to_all x1, starting transfers between devices, per_device(): lax.all_to_all(rows_back, axes, split_axis=0, concat_axis=0, tiled=True)  16.7 us
    pallas_call x1, Pallas kernels, splat(): pl.pallas_call(splat_kernel, out_shape=(jax.ShapeDtypeStruct(shape, BF),...  13.3 us
    pallas_call x1, Pallas kernels, gather(): pl.pallas_call(gather_kernel, out_shape=pltpu.HBM((owners, channels, heig...  11.7 us
    all_to_all x1, starting transfers between devices, per_device(): lax.all_to_all(sent, axes, split_axis=0, concat_axis=0, tiled=True)  10.9 us
    pallas_call x1, Pallas kernels, final(): pl.pallas_call(functools.partial(final_kernel, tile_count), out_shape=(ja...  8.66 us
  transfers between devices with their start and end apart: 12, of which 5 were waited for; matrix products, arithmetic and copies ran while one was open for 5% of the time, Pallas kernels for 6%

profile of v3, /device:TPU:6, one launch (start us, length us, event | category | flops | bytes accessed | tf_op | source)
XLA Modules:
  0.0 225.5 jit_solution(15844351114526150133)
XLA Ops:
  2.8 5.3 %pack.1 = bf16[128,136,128]{2,1,0:T(8,128)(2,1)} custom-call(s32[4,16]{1,0:T(4,128)S(1)} %add.11.spots, s32[64,64]{1,0:T(8,128)S(1)} %bitcast.14, bf16[64,64,128]{2,1,0:T(8,128)(2,1)} %bitcast.19, bf16[64,128,128]{2,1,0:T(8,128)(2,1)} %bitcast.17), custom_call_target="tpu_custom_call" | custom-call | tf_op jit(solution)/shard_map/pack/pallas_call | solution.py:118
  8.1 10.9 %all-to-all-start = ((bf16[128,136,128]{2,1,0:T(8,128)(2,1)}), bf16[128,136,128]{2,1,0:T(8,128)(2,1)}, u32[]{:S(2)}, u32[]{:S(2)}) async-start(bf16[128,136,128]{2,1,0:T(8,128)(2,1)} %pack.1), calls=%async_computation | async-start | bytes 8912896 | tf_op jit(solution)/shard_map/all_to_all | solution.py:502
  19.5 1.3 collective-permute-start.7
  20.8 4.5 %collective-permute-start.6 = (bf16[16,8,256]{2,1,0:T(8,128)(2,1)S(1)}, bf16[16,8,256]{2,1,0:T(8,128)(2,1)S(1)}, u32[]{:S(2)}, u32[]{:S(2)}) collective-permute-start(bf16[16,8,256]{2,1,0:T(8,128)(2,1)S(1)} %get-tuple-element.18), channel_id=1, source_target_pairs={{0,1},{1,2},{2,3},{3,4},{4,5},{5,6},{6,7},{7,8},{8,9},{9,10},{10,1... | collective-permute-start | bytes 196616 | tf_op jit(solution)/shard_map/ppermute | solution.py:34
  25.8 2.8 %copy.10 = bf16[4,3,4,128,256]{4,3,2,1,0:T(8,128)(2,1)} copy(bf16[4,3,4,128,256]{3,4,2,1,0:T(8,128)(2,1)S(1)} %fusion.4) | data formatting | bytes 6291456 | tf_op jit(solution)/shard_map/concatenate | solution.py:481
  28.7 2.2 fusion.5
  31.3 3.2 %maximum_multiply_fusion.weights_far = bf16[8,1536,256]{2,1,0:T(8,128)(2,1)} fusion(bf16[4,1536,256]{2,1,0:T(8,128)(2,1)S(1)} %bitcast.15, bf16[4,1536,256]{2,1,0:T(8,128)(2,1)S(1)} %bitcast.16), kind=kLoop, calls=%fused_computation.4 | loop fusion | flops 6291456 | bytes 12582912 | tf_op jit(solution)/shard_map/mul | solution.py:508
  34.5 28.6 %collective-permute-done.6 = bf16[16,8,256]{2,1,0:T(8,128)(2,1)S(1)} collective-permute-done((bf16[16,8,256]{2,1,0:T(8,128)(2,1)S(1)}, bf16[16,8,256]{2,1,0:T(8,128)(2,1)S(1)}, u32[]{:S(2)}, u32[]{:S(2)}) %collective-permute-start.6) | collective-permute-done | bytes 65568 | tf_op jit(solution)/shard_map/ppermute | solution.py:34
  63.2 2.8 %collective-permute-start.8 = (bf16[4,144,256]{2,1,0:T(8,128)(2,1)S(1)}, bf16[4,144,256]{2,1,0:T(8,128)(2,1)S(1)}, u32[]{:S(2)}, u32[]{:S(2)}) collective-permute-start(bf16[4,144,256]{2,1,0:T(8,128)(2,1)S(1)} %get-tuple-element.15), channel_id=1, source_target_pairs={{0,16},{16,32},{32,48},{48,64},{64,80},{80,96},{96,112},{1,17},{17... | collective-permute-start | bytes 884744 | tf_op jit(solution)/shard_map/ppermute | solution.py:34
  66.1 2.8 %collective-permute-start.9 = (bf16[4,144,256]{2,1,0:T(8,128)(2,1)S(1)}, bf16[4,144,256]{2,1,0:T(8,128)(2,1)S(1)}, u32[]{:S(2)}, u32[]{:S(2)}) collective-permute-start(bf16[4,144,256]{2,1,0:T(8,128)(2,1)S(1)} %get-tuple-element.16), channel_id=1, source_target_pairs={{16,0},{32,16},{48,32},{64,48},{80,64},{96,80},{112,96},{17,1},{33... | collective-permute-start | bytes 884744 | tf_op jit(solution)/shard_map/ppermute | solution.py:34
  68.8 6.5 %all-to-all-done.meta_all.message = bf16[128,136,128]{2,1,0:T(8,128)(2,1)} async-done(((bf16[128,136,128]{2,1,0:T(8,128)(2,1)}), bf16[128,136,128]{2,1,0:T(8,128)(2,1)}, u32[]{:S(2)}, u32[]{:S(2)}) %all-to-all-start) | async-done | bytes 4456480 | tf_op jit(solution)/shard_map/all_to_all | solution.py:502
  75.3 13.3 %splat.1 = (bf16[16,128,256]{2,1,0:T(8,128)(2,1)S(1)}, s32[2,128]{1,0:T(2,128)S(1)}) custom-call(bf16[128,136,128]{2,1,0:T(8,128)(2,1)} %all-to-all-done.meta_all.message, bf16[128,136,128]{2,1,0:T(8,128)(2,1)} %all-to-all-done.meta_all.message), custom_call_target="tpu_custom_call" | custom-call | tf_op jit(solution)/shard_map/splat/pallas_call | solution.py:200
  88.6 1.3 collective-permute-start.2
  91.3 1.9 collective-permute-start.1
  93.3 2.4 %collective-permute-start = (bf16[8,128,256]{2,1,0:T(8,128)(2,1)S(1)}, bf16[8,128,256]{2,1,0:T(8,128)(2,1)S(1)}, u32[]{:S(2)}, u32[]{:S(2)}) collective-permute-start(bf16[8,128,256]{2,1,0:T(8,128)(2,1)S(1)} %get-tuple-element.22), channel_id=1, source_target_pairs={{0,16},{16,32},{32,48},{48,64},{64,80},{80,96},{96,112},{1,17},{17... | collective-permute-start | bytes 1572872 | tf_op jit(solution)/shard_map/ppermute | solution.py:519
  96.2 2.7 %collective-permute-start.5 = (bf16[8,16,256]{2,1,0:T(8,128)(2,1)S(1)}, bf16[8,16,256]{2,1,0:T(8,128)(2,1)S(1)}, u32[]{:S(2)}, u32[]{:S(2)}) collective-permute-start(bf16[8,16,256]{2,1,0:T(8,128)(2,1)S(1)} %get-tuple-element.23), channel_id=1, source_target_pairs={{16,0},{32,16},{48,32},{64,48},{80,64},{96,80},{112,96},{17,1},{33... | collective-permute-start | bytes 196616 | tf_op jit(solution)/shard_map/ppermute | solution.py:525
  98.9 2.1 collective-permute-start.4
  101.0 1.4 pad_maximum_fusion.cot_far
  102.5 2.0 collective-permute-done.4.corner_above
  104.5 30.8 %convs.1 = (bf16[24,128,256]{2,1,0:T(8,128)(2,1)S(1)}, bf16[16,128,256]{2,1,0:T(8,128)(2,1)S(1)}) custom-call(s32[4]{0:T(128)S(1)} %add_convert_fusion.edges, bf16[16,128,256]{2,1,0:T(8,128)(2,1)S(1)} %get-tuple-element.9.middle, bf16[8,128,256]{2,1,0:T(8,128)(2,1)S(1)} %collective-permute-done.above, bf16[8,128,256]{2,1,0:T(8,128)(2,1)S(1)} %collective-permute-done.1.below, ...), custom_call_target="tpu_custom_call" | custom-call | tf_op jit(solution)/shard_map/convs/pallas_call | solution.py:357
  135.3 11.7 %gather.1 = bf16[128,128,128]{2,1,0:T(8,128)(2,1)} custom-call(s32[2,128]{1,0:T(2,128)S(1)} %get-tuple-element.11.tiles, bf16[128,136,128]{2,1,0:T(8,128)(2,1)} %all-to-all-done.meta_all.message, bf16[16,128,256]{2,1,0:T(8,128)(2,1)S(1)} %get-tuple-element.12.grad), custom_call_target="tpu_custom_call" | custom-call | tf_op jit(solution)/shard_map/gather/pallas_call | solution.py:415
  146.9 16.7 %all-to-all-start.1 = ((bf16[128,128,128]{2,1,0:T(8,128)(2,1)}), bf16[128,128,128]{2,1,0:T(8,128)(2,1)}, u32[]{:S(2)}, u32[]{:S(2)}) async-start(bf16[128,128,128]{2,1,0:T(8,128)(2,1)} %gather.1), calls=%async_computation.1 | async-start | bytes 8388608 | tf_op jit(solution)/shard_map/all_to_all | solution.py:531
  164.9 52.0 %all-to-all-done.1.returned = bf16[128,128,128]{2,1,0:T(8,128)(2,1)} async-done(((bf16[128,128,128]{2,1,0:T(8,128)(2,1)}), bf16[128,128,128]{2,1,0:T(8,128)(2,1)}, u32[]{:S(2)}, u32[]{:S(2)}) %all-to-all-start.1) | async-done | bytes 4194336 | tf_op jit(solution)/shard_map/all_to_all | solution.py:531
  216.9 8.7 %final.1 = (bf16[64,64,128]{2,1,0:T(8,128)(2,1)}, bf16[64,128,128]{2,1,0:T(8,128)(2,1)}) custom-call(s32[4,16]{1,0:T(4,128)S(1)} %add.11.spots, bf16[128,128,128]{2,1,0:T(8,128)(2,1)} %all-to-all-done.1.returned, bf16[64,64,128]{2,1,0:T(8,128)(2,1)} %bitcast.20, bf16[64,128,128]{2,1,0:T(8,128)(2,1)} %bitcast.18), custom_call_target="tpu_custom_call" | custom-call | tf_op jit(solution)/shard_map/final/pallas_call | solution.py:462
  (39 shorter events, 6.7 us)
Async XLA Ops:
  2.0 0.8 copy-start
  8.1 10.9 %copy-start.5 = (bf16[16,256,128]{2,1,0:T(8,128)(2,1)S(1)}, bf16[16,256,128]{2,1,0:T(8,128)(2,1)}, u32[]{:S(2)}) copy-start(bf16[16,256,128]{2,1,0:T(8,128)(2,1)} %param.13) | copy-start | bytes 3145732
  8.1 67.2 %all-to-all-start = ((bf16[128,136,128]{2,1,0:T(8,128)(2,1)}), bf16[128,136,128]{2,1,0:T(8,128)(2,1)}, u32[]{:S(2)}, u32[]{:S(2)}) async-start(bf16[128,136,128]{2,1,0:T(8,128)(2,1)} %pack.1), calls=%async_computation | async-start | bytes 8912896 | tf_op jit(solution)/shard_map/all_to_all | solution.py:502
  19.0 6.3 %copy-start.4 = (bf16[4,3,3,128,128]{4,3,2,1,0:T(8,128)(2,1)S(1)}, bf16[4,3,3,128,128]{4,3,2,1,0:T(8,128)(2,1)}, u32[]{:S(2)}) copy-start(bf16[4,3,3,128,128]{4,3,2,1,0:T(8,128)(2,1)} %param.12) | copy-start | bytes 3538948
  19.4 5.9 %copy-start.2 = (bf16[16,128,256]{2,1,0:T(8,128)(2,1)}, bf16[16,128,256]{2,1,0:T(8,128)(2,1)S(1)}, u32[]{:S(2)}) copy-start(bf16[16,128,256]{2,1,0:T(8,128)(2,1)S(1)} %reshape.38) | copy-start | bytes 3145732
  19.5 43.7 %collective-permute-start.7 = (bf16[16,8,256]{2,1,0:T(8,128)(2,1)S(1)}, bf16[16,8,256]{2,1,0:T(8,128)(2,1)S(1)}, u32[]{:S(2)}, u32[]{:S(2)}) collective-permute-start(bf16[16,8,256]{2,1,0:T(8,128)(2,1)S(1)} %get-tuple-element.17), channel_id=1, source_target_pairs={{1,0},{2,1},{3,2},{4,3},{5,4},{6,5},{7,6},{8,7},{9,8},{10,9},{11,1... | collective-permute-start | bytes 196616 | tf_op jit(solution)/shard_map/ppermute | solution.py:34
  20.8 42.3 %collective-permute-start.6 = (bf16[16,8,256]{2,1,0:T(8,128)(2,1)S(1)}, bf16[16,8,256]{2,1,0:T(8,128)(2,1)S(1)}, u32[]{:S(2)}, u32[]{:S(2)}) collective-permute-start(bf16[16,8,256]{2,1,0:T(8,128)(2,1)S(1)} %get-tuple-element.18), channel_id=1, source_target_pairs={{0,1},{1,2},{2,3},{3,4},{4,5},{5,6},{6,7},{7,8},{8,9},{9,10},{10,1... | collective-permute-start | bytes 196616 | tf_op jit(solution)/shard_map/ppermute | solution.py:34
  28.7 2.6 %copy-start.1 = (bf16[4,3,4,128,256]{4,3,2,1,0:T(8,128)(2,1)S(1)}, bf16[4,3,4,128,256]{4,3,2,1,0:T(8,128)(2,1)}, u32[]{:S(2)}) copy-start(bf16[4,3,4,128,256]{4,3,2,1,0:T(8,128)(2,1)} %copy.10) | copy-start | bytes 9437188
  31.3 31.8 %copy-start.3 = (bf16[16,128,256]{2,1,0:T(8,128)(2,1)S(1)}, bf16[16,128,256]{2,1,0:T(8,128)(2,1)}, u32[]{:S(2)}) copy-start(bf16[16,128,256]{2,1,0:T(8,128)(2,1)} %copy-done.2) | copy-start | bytes 3145732
  63.2 35.7 %collective-permute-start.8 = (bf16[4,144,256]{2,1,0:T(8,128)(2,1)S(1)}, bf16[4,144,256]{2,1,0:T(8,128)(2,1)S(1)}, u32[]{:S(2)}, u32[]{:S(2)}) collective-permute-start(bf16[4,144,256]{2,1,0:T(8,128)(2,1)S(1)} %get-tuple-element.15), channel_id=1, source_target_pairs={{0,16},{16,32},{32,48},{48,64},{64,80},{80,96},{96,112},{1,17},{17... | collective-permute-start | bytes 884744 | tf_op jit(solution)/shard_map/ppermute | solution.py:34
  66.1 35.0 %collective-permute-start.9 = (bf16[4,144,256]{2,1,0:T(8,128)(2,1)S(1)}, bf16[4,144,256]{2,1,0:T(8,128)(2,1)S(1)}, u32[]{:S(2)}, u32[]{:S(2)}) collective-permute-start(bf16[4,144,256]{2,1,0:T(8,128)(2,1)S(1)} %get-tuple-element.16), channel_id=1, source_target_pairs={{16,0},{32,16},{48,32},{64,48},{80,64},{96,80},{112,96},{17,1},{33... | collective-permute-start | bytes 884744 | tf_op jit(solution)/shard_map/ppermute | solution.py:34
  88.6 4.6 %collective-permute-start.2 = (bf16[16,8,256]{2,1,0:T(8,128)(2,1)S(1)}, bf16[16,8,256]{2,1,0:T(8,128)(2,1)S(1)}, u32[]{:S(2)}, u32[]{:S(2)}) collective-permute-start(bf16[16,8,256]{2,1,0:T(8,128)(2,1)S(1)} %get-tuple-element.20), channel_id=1, source_target_pairs={{0,1},{1,2},{2,3},{3,4},{4,5},{5,6},{6,7},{7,8},{8,9},{9,10},{10,1... | collective-permute-start | bytes 196616 | tf_op jit(solution)/shard_map/ppermute | solution.py:521
  90.0 6.2 %collective-permute-start.3 = (bf16[16,8,256]{2,1,0:T(8,128)(2,1)S(1)}, bf16[16,8,256]{2,1,0:T(8,128)(2,1)S(1)}, u32[]{:S(2)}, u32[]{:S(2)}) collective-permute-start(bf16[16,8,256]{2,1,0:T(8,128)(2,1)S(1)} %get-tuple-element.19), channel_id=1, source_target_pairs={{1,0},{2,1},{3,2},{4,3},{5,4},{6,5},{7,6},{8,7},{9,8},{10,9},{11,1... | collective-permute-start | bytes 196616 | tf_op jit(solution)/shard_map/ppermute | solution.py:522
  91.3 13.2 %collective-permute-start.1 = (bf16[8,128,256]{2,1,0:T(8,128)(2,1)S(1)}, bf16[8,128,256]{2,1,0:T(8,128)(2,1)S(1)}, u32[]{:S(2)}, u32[]{:S(2)}) collective-permute-start(bf16[8,128,256]{2,1,0:T(8,128)(2,1)S(1)} %get-tuple-element.21), channel_id=1, source_target_pairs={{16,0},{32,16},{48,32},{64,48},{80,64},{96,80},{112,96},{17,1},{33... | collective-permute-start | bytes 1572872 | tf_op jit(solution)/shard_map/ppermute | solution.py:520
  93.3 11.2 %collective-permute-start = (bf16[8,128,256]{2,1,0:T(8,128)(2,1)S(1)}, bf16[8,128,256]{2,1,0:T(8,128)(2,1)S(1)}, u32[]{:S(2)}, u32[]{:S(2)}) collective-permute-start(bf16[8,128,256]{2,1,0:T(8,128)(2,1)S(1)} %get-tuple-element.22), channel_id=1, source_target_pairs={{0,16},{16,32},{32,48},{48,64},{64,80},{80,96},{96,112},{1,17},{17... | collective-permute-start | bytes 1572872 | tf_op jit(solution)/shard_map/ppermute | solution.py:519
  96.2 6.2 %collective-permute-start.5 = (bf16[8,16,256]{2,1,0:T(8,128)(2,1)S(1)}, bf16[8,16,256]{2,1,0:T(8,128)(2,1)S(1)}, u32[]{:S(2)}, u32[]{:S(2)}) collective-permute-start(bf16[8,16,256]{2,1,0:T(8,128)(2,1)S(1)} %get-tuple-element.23), channel_id=1, source_target_pairs={{16,0},{32,16},{48,32},{64,48},{80,64},{96,80},{112,96},{17,1},{33... | collective-permute-start | bytes 196616 | tf_op jit(solution)/shard_map/ppermute | solution.py:525
  98.9 5.6 %collective-permute-start.4 = (bf16[8,16,256]{2,1,0:T(8,128)(2,1)S(1)}, bf16[8,16,256]{2,1,0:T(8,128)(2,1)S(1)}, u32[]{:S(2)}, u32[]{:S(2)}) collective-permute-start(bf16[8,16,256]{2,1,0:T(8,128)(2,1)S(1)} %get-tuple-element.24), channel_id=1, source_target_pairs={{0,16},{16,32},{32,48},{48,64},{64,80},{80,96},{96,112},{1,17},{17... | collective-permute-start | bytes 196616 | tf_op jit(solution)/shard_map/ppermute | solution.py:524
  146.9 69.9 %all-to-all-start.1 = ((bf16[128,128,128]{2,1,0:T(8,128)(2,1)}), bf16[128,128,128]{2,1,0:T(8,128)(2,1)}, u32[]{:S(2)}, u32[]{:S(2)}) async-start(bf16[128,128,128]{2,1,0:T(8,128)(2,1)} %gather.1), calls=%async_computation.1 | async-start | bytes 8388608 | tf_op jit(solution)/shard_map/all_to_all | solution.py:531

commit v4 on v3

--- a/solution.py
+++ b/solution.py
@@ -25,16 +25,6 @@
     return down, up
 
 
-def with_sides(cells, axis, dim, width):
-    down, up = ring(axis)
-    size = cells.shape[dim]
-    head = lax.slice_in_dim(cells, 0, width, axis=dim)
-    tail = lax.slice_in_dim(cells, size - width, size, axis=dim)
-    return jnp.concatenate(
-        [lax.ppermute(tail, axis, down), cells, lax.ppermute(head, axis, up)], axis=dim
-    )
-
-
 def take_slot(owner, count):
     rank = count[owner]
     count[owner] = rank + 1
@@ -50,44 +40,44 @@
     return pltpu.with_memory_space_constraint(x, pltpu.HBM)
 
 
-def spot_of(spots, at, tiles):
-    value = spots[at // spots.shape[1], at % spots.shape[1]]
-    return value // tiles, value % tiles
+def owner_of(owner, at):
+    each = owner.shape[2]
+    return owner[lax.div(at, each), 0, lax.rem(at, each)]
 
 
 def pair_cells(cells):
     return (cells // TS) * TS + (cells % 2) * (TS // 2) + (cells % TS) // 2
 
 
-def pack_kernel(tile_count, spots, cells, depth, context, out, count, wide, lifted, meta, sems):
+def pack_kernel(owner, local, cells, depth, context, out, count, wide, lifted, meta, sems):
     step = pl.program_id(0)
     blocks, bins, _ = depth.shape
     owners = out.shape[0]
-    channels = context.shape[2]
 
     @pl.when(step == 0)
     def _():
         clear_counts(count, owners)
         kind = lax.broadcasted_iota(jnp.int32, meta.shape, 1)
         meta[...] = jnp.where(kind == 0, EMPTY, ABSENT)
-        numbers = pair_cells(cells[...]).astype(F32)
+        numbers = pair_cells(cells[...]).astype(F32).reshape(wide.shape[0], bins)
         wide[...] = jnp.concatenate([numbers, numbers], axis=1)
 
     lane = lax.broadcasted_iota(jnp.int32, (1, 2 * bins), 1)
 
     def block(b, carry):
         at = step * blocks + b
-        to, local = spot_of(spots, at, tile_count)
+        to = owner_of(owner, at)
+        each = local.shape[1]
+        tile = local[lax.div(at, each), lax.rem(at, each)].astype(F32)
         rank = take_slot(to, count)
         product = jnp.dot(depth[b], context[b], preferred_element_type=F32)
-        lifted[at // 2, pl.ds(pl.multiple_of((at % 2) * bins, bins), bins), :] = product.astype(BF)
+        lifted[lax.div(at, 2), pl.ds(pl.multiple_of(lax.rem(at, 2) * bins, bins), bins), :] = product.astype(BF)
         mine = (lane // bins) == rank
         row = wide[pl.ds(at, 1), :]
         meta[to, pl.ds(0, 1), :] = jnp.where(mine, row, meta[to, pl.ds(0, 1), :])
-        tile = local.astype(F32)
         meta[to, pl.ds(1, 1), :] = jnp.where(mine, tile, meta[to, pl.ds(1, 1), :])
         pltpu.make_async_copy(
-            lifted.at[at // 2, pl.ds(pl.multiple_of((at % 2) * bins, bins), bins), :],
+            lifted.at[lax.div(at, 2), pl.ds(pl.multiple_of(lax.rem(at, 2) * bins, bins), bins), :],
             out.at[to, pl.ds(pl.multiple_of(rank * bins, bins), bins), :],
             sems.at[0],
         ).start()
@@ -98,6 +88,7 @@
     @pl.when(step == pl.num_programs(0) - 1)
     def _():
         wide_meta = lifted.shape[0]
+
         def put_meta(small):
             small[...] = meta[...].astype(BF)
             copy = pltpu.make_async_copy(
@@ -105,23 +96,25 @@
             )
             copy.start()
             copy.wait()
+
         pl.run_scoped(put_meta, pltpu.VMEM(meta.shape, BF))
         pltpu.make_async_copy(
             lifted, out.at[pl.ds(0, wide_meta), pl.ds(0, 2 * bins), :], sems.at[0]
         ).wait()
 
 
-def pack(spots, cells, depth, context, owners, tile_count):
+def pack(owner, local, cells, depth, context, owners):
     blocks, bins, pixels = depth.shape
     channels = context.shape[2]
     chunk = blocks // 4
     return pl.pallas_call(
-        functools.partial(pack_kernel, tile_count),
+        pack_kernel,
         out_shape=pltpu.HBM((owners, 2 * bins + 8, channels), BF),
         grid=(blocks // chunk,),
         in_specs=[
             pl.BlockSpec(memory_space=pltpu.SMEM),
-            pl.BlockSpec(cells.shape, lambda i: (0, 0)),
+            pl.BlockSpec(memory_space=pltpu.SMEM),
+            pl.BlockSpec(cells.shape, lambda i: (0, 0, 0)),
             pl.BlockSpec((chunk, bins, pixels), lambda i: (i, 0, 0)),
             pl.BlockSpec((chunk, pixels, channels), lambda i: (i, 0, 0)),
         ],
@@ -135,7 +128,7 @@
         ],
         compiler_params=pltpu.CompilerParams(vmem_limit_bytes=24 << 20),
         name="pack",
-    )(spots, cells, depth, context)
+    )(owner, local, cells, depth, context)
 
 
 def cell_onehot(cell_row, cells):
@@ -185,7 +178,7 @@
                 acc[:, at, lanes] += part[:, side]
         return carry
 
-    lax.fori_loop(0, sources, source, 0, unroll=4)
+    lax.fori_loop(0, sources, source, 0, unroll=8)
 
     @pl.when(step == pl.num_programs(0) - 1)
     def _():
@@ -231,7 +224,8 @@
 
 
 def conv_kernel(
-    edges, middle, above, below, left, right, corner_above, corner_below, cot_far, weights_far,
+    edges, middle, above, below, left, right, corner_above, corner_below,
+    cot_middle, cot_above, cot_below, cot_left, cot_right, weights_far,
     bev, grad, ping, pong, slopes, mask, sums, weights, cot, sems,
 ):
     rows, mid, double = middle.shape
@@ -242,10 +236,8 @@
         pltpu.make_async_copy(weights_far.at[i], weights.at[i], sems.at[i])
         for i in range(2 * LAYERS)
     ]
-    cot_arrival = pltpu.make_async_copy(cot_far, cot, sems.at[2 * LAYERS])
     for copy in arrivals[:LAYERS]:
         copy.start()
-    cot_arrival.start()
     for copy in arrivals[: LAYERS - 1 : -1]:
         copy.start()
     column = lax.broadcasted_iota(jnp.int32, (wide, double), 0)
@@ -260,11 +252,11 @@
         ref[row, :, channels : 3 * channels] = value.astype(BF)
         ref[row, :, 3 * channels :] = pltpu.roll(first, wide - 1, 0).astype(BF)
 
+    def joined(west, center, east):
+        return jnp.concatenate([west.astype(F32), center.astype(F32), east.astype(F32)], axis=0)
+
     def load(row, west, center, east):
-        put(
-            ping, row,
-            jnp.concatenate([west.astype(F32), center.astype(F32), east.astype(F32)], axis=0),
-        )
+        put(ping, row, joined(west, center, east))
 
     def load_outer(k, carry):
         load(k, corner_above[k, 0:PAIRS], above[k], corner_above[k, PAIRS:])
@@ -276,7 +268,19 @@
         return carry
 
     lax.fori_loop(0, EXT, load_outer, 0)
+
+    def load_cot(k, carry):
+        cot[LAYERS + k] = joined(cot_left[k], cot_middle[k], cot_right[k]).astype(BF)
+        return carry
+
     lax.fori_loop(0, rows, load_inner, 0)
+    lax.fori_loop(0, rows, load_cot, 0)
+    for k in range(LAYERS):
+        for corner, field, base in (
+            (corner_above, cot_above, 0), (corner_below, cot_below, LAYERS + rows)
+        ):
+            west, east = corner[EXT + k, 0:PAIRS], corner[EXT + k, PAIRS:]
+            cot[base + k] = joined(west, field[k], east).astype(BF)
 
     def matmul(ref, index, start, size):
         taps = [ref[pl.ds(start + tap, size)].reshape(size * wide, 2 * double) for tap in range(3)]
@@ -332,8 +336,6 @@
         if finish is not None:
             finish()
         matmul(source, index, 0, size)
-        if index == LAYERS - 1:
-            cot_arrival.wait()
 
         def steady(k, carry, index=index, count=count, size=size, source=source, target=target, epilogue=epilogue):
             epilogue(target, (k - 1) * size, size)
@@ -346,7 +348,8 @@
     finish()
 
 
-def convs(edges, middle, above, below, left, right, corner_above, corner_below, cot, weights):
+def convs(edges, weights, *fields):
+    middle = fields[0]
     rows, mid, double = middle.shape
     wide = mid + 2 * PAIRS
     tall = rows + 2 * EXT
@@ -360,7 +363,7 @@
             jax.ShapeDtypeStruct((rows + 2 * LAYERS, mid, double), BF),
             jax.ShapeDtypeStruct(middle.shape, BF),
         ),
-        in_specs=[pl.BlockSpec(memory_space=pltpu.SMEM)] + [vmem] * 7 + [hbm] * 2,
+        in_specs=[pl.BlockSpec(memory_space=pltpu.SMEM)] + [vmem] * len(fields) + [hbm],
         out_specs=(vmem, vmem),
         scratch_shapes=[
             buffer,
@@ -369,21 +372,18 @@
             pltpu.VMEM((2, wide, double), F32),
             pltpu.VMEM((7, wide, double), F32),
             pltpu.VMEM(weights.shape, BF),
-            pltpu.VMEM(cot.shape, BF),
-            pltpu.SemaphoreType.DMA((2 * LAYERS + 1,)),
+            pltpu.VMEM((rows + 2 * LAYERS, wide, double), BF),
+            pltpu.SemaphoreType.DMA((2 * LAYERS,)),
         ],
         compiler_params=pltpu.CompilerParams(vmem_limit_bytes=48 << 20),
         name="convs",
-    )(
-        edges, middle, above, below, left, right, corner_above, corner_below,
-        in_hbm(cot), in_hbm(weights),
-    )
+    )(edges, *fields, in_hbm(weights))
 
 
 def gather_kernel(tiles, message, grad, out, turned):
     step = pl.program_id(0)
     sources, _, channels = message.shape
-    rows, mid, double = grad.shape
+    _, mid, _ = grad.shape
     cells = TS * TS
     bins = out.shape[2] // 2
 
@@ -395,18 +395,17 @@
             turned[tile] = piece.reshape(cells, channels).T.astype(BF)
 
     lane = lax.broadcasted_iota(jnp.int32, (1, 2 * bins), 1)
-    lift = (lane // bins) * cells
 
     def source(s, carry):
-        meta = message[s].astype(jnp.int32)[0:1]
-        hot = cell_onehot(jnp.where(meta < cells, meta + lift, 2 * cells), 2 * cells)
+        hot = cell_onehot(message[s].astype(jnp.int32)[0:1], cells)
         at = step * sources + s
         here = [jnp.minimum(tiles[rank, at], mid // 8 - 1) for rank in range(2)]
-        both = jnp.concatenate([turned[here[0]], turned[here[1]]], axis=1)
-        out[s] = jnp.dot(both, hot, preferred_element_type=F32).astype(BF)
-        return carry
-
-    lax.fori_loop(0, sources, source, 0, unroll=4)
+        both = jnp.concatenate([turned[here[0]], turned[here[1]]], axis=0)
+        picked = jnp.dot(both, hot, preferred_element_type=F32)
+        out[s] = jnp.where(lane < bins, picked[:channels], picked[channels:]).astype(BF)
+        return carry
+
+    lax.fori_loop(0, sources, source, 0, unroll=8)
 
 
 def gather(tiles, message, grad):
@@ -428,7 +427,7 @@
     )(tiles, message, grad)
 
 
-def final_kernel(tile_count, spots, returned, depth, context, grad_depth, grad_context, count):
+def final_kernel(owner, returned, depth, context, grad_depth, grad_context, count):
     step = pl.program_id(0)
     blocks, bins, _ = depth.shape
 
@@ -437,7 +436,7 @@
         clear_counts(count, returned.shape[0])
 
     def block(b, carry):
-        to, _ = spot_of(spots, step * blocks + b, tile_count)
+        to = owner_of(owner, step * blocks + b)
         rank = take_slot(to, count)
         turned = returned[to].T
         rows = jnp.where(rank == 0, turned[0:bins], turned[bins : 2 * bins])
@@ -449,10 +448,10 @@
         ).astype(BF)
         return carry
 
-    lax.fori_loop(0, blocks, block, 0, unroll=4)
-
-
-def final(spots, returned, depth, context, tile_count):
+    lax.fori_loop(0, blocks, block, 0, unroll=8)
+
+
+def final(owner, returned, depth, context):
     blocks, bins, pixels = depth.shape
     channels = context.shape[2]
     chunk = blocks // 4
@@ -460,7 +459,7 @@
     depth_block = pl.BlockSpec((chunk, bins, pixels), lambda i: (i, 0, 0))
     context_block = pl.BlockSpec((chunk, pixels, channels), lambda i: (i, 0, 0))
     return pl.pallas_call(
-        functools.partial(final_kernel, tile_count),
+        final_kernel,
         out_shape=(
             jax.ShapeDtypeStruct(depth.shape, BF),
             jax.ShapeDtypeStruct(context.shape, BF),
@@ -471,7 +470,7 @@
         scratch_shapes=[pltpu.SMEM((returned.shape[0],), jnp.int32)],
         compiler_params=pltpu.CompilerParams(vmem_limit_bytes=40 << 20),
         name="final",
-    )(spots, in_hbm(returned), depth, context)
+    )(owner, in_hbm(returned), depth, context)
 
 
 def paired_weights(kernel):
@@ -493,16 +492,21 @@
     blocks = cams_here * blocks_cam
     depth = depth_weights.reshape(blocks, bins, pixels)
     flat_context = context.reshape(blocks, pixels, channels)
-    tile_count = cols // TS
-    spots = block_owner[:, :, 0] * tile_count + block_local
+    owner = block_owner.transpose(0, 2, 1)
 
     sent = pack(
-        spots, block_cell.reshape(blocks, bins), in_hbm(depth), in_hbm(flat_context), owners, tile_count
+        in_hbm(owner), in_hbm(block_local), in_hbm(block_cell), in_hbm(depth),
+        in_hbm(flat_context), owners,
     )
     message = lax.all_to_all(sent, axes, split_axis=0, concat_axis=0, tiled=True)
 
     cot = cotangent.reshape(rows, mid, 2 * channels)
-    cot = with_sides(with_sides(cot, "tile", 1, PAIRS), "cam", 0, LAYERS)
+    down, up = ring("cam")
+    east, west = ring("tile")
+    cot_above = lax.ppermute(cot[rows - LAYERS :], "cam", down)
+    cot_below = lax.ppermute(cot[:LAYERS], "cam", up)
+    cot_left = lax.ppermute(cot[:, mid - PAIRS :], "tile", east)
+    cot_right = lax.ppermute(cot[:, :PAIRS], "tile", west)
     turned_weight = conv_weight[:, ::-1, ::-1].swapaxes(3, 4)
     weights = jnp.concatenate([paired_weights(conv_weight), paired_weights(turned_weight)], axis=0)
     weights = weights * jnp.asarray(0.5, BF)
@@ -514,24 +518,26 @@
 
     middle, tiles = splat(message, rows, cols)
 
-    down, up = ring("cam")
-    east, west = ring("tile")
     above = lax.ppermute(middle[rows - EXT :], "cam", down)
     below = lax.ppermute(middle[:EXT], "cam", up)
     left = lax.ppermute(middle[:, mid - PAIRS :], "tile", east)
     right = lax.ppermute(middle[:, :PAIRS], "tile", west)
     sides = jnp.concatenate([left, right], axis=1)
-    corner_above = lax.ppermute(sides[rows - EXT :], "cam", down)
-    corner_below = lax.ppermute(sides[:EXT], "cam", up)
+    cot_sides = jnp.concatenate([cot_left, cot_right], axis=1)
+    corner_above = lax.ppermute(
+        jnp.concatenate([sides[rows - EXT :], cot_sides[rows - LAYERS :]], axis=0), "cam", down
+    )
+    corner_below = lax.ppermute(
+        jnp.concatenate([sides[:EXT], cot_sides[:LAYERS]], axis=0), "cam", up
+    )
 
     bev, grad = convs(
-        edges, middle, above, below, left, right, corner_above, corner_below, cot, weights
+        edges, weights, middle, above, below, left, right, corner_above, corner_below,
+        cot, cot_above, cot_below, cot_left, cot_right,
     )
     rows_back = gather(tiles, message, grad)
     returned = lax.all_to_all(rows_back, axes, split_axis=0, concat_axis=0, tiled=True)
-    grad_depth, grad_context = final(
-        spots, returned, in_hbm(depth), in_hbm(flat_context), tile_count
-    )
+    grad_depth, grad_context = final(owner, returned, in_hbm(depth), in_hbm(flat_context))
     return (
         bev[LAYERS : LAYERS + rows].reshape(cotangent.shape),
         grad_depth.reshape(depth_weights.shape),

time: 226 us -> 214 us (0.947)
  Pallas kernels: 69.7 us -> 63.1 us
  starting transfers between devices: 50.7 us -> 47.2 us
  local copies, waits for them, and re-layouts: 6.01 us -> 9.19 us
  other arithmetic: 8.62 us -> 5.59 us
  waiting for transfers between devices: 89.5 us -> 86.5 us
    ppermute x6, waiting for transfers between devices: 30.6 us -> 21.9 us  [the longest x1 19.1 us: per_device(): cot_left = lax.ppermute(cot[:, mid - PAIRS:], 'tile', east)]
    all_to_all x1, waiting for transfers between devices: 6.5 us -> 12.2 us  [per_device(): lax.all_to_all(sent, axes, split_axis=0, concat_axis=0, tiled=True)]
    all_to_all x1, starting transfers between devices: 16.7 us -> 12.1 us  [per_device(): lax.all_to_all(rows_back, axes, split_axis=0, concat_axis=0, tiled=True)]
    pallas_call x1, Pallas kernels: 13.3 us -> 10.7 us  [splat(): pl.pallas_call(splat_kernel, out_shape=(jax.ShapeDtypeStruct(shape, BF),...]
    pallas_call x1, Pallas kernels: 11.7 us -> 9.11 us  [gather(): pl.pallas_call(gather_kernel, out_shape=pltpu.HBM((owners, channels, heig...]
  transfers between devices with their start and end apart: 12 -> 12, of which waited for: 5 -> 5; matrix products, arithmetic and copies ran while one was open for 5% -> 6% of each run, Pallas kernels for 6% -> 5%
where the time goes in v4:
time: 214 us; the launch traced here: 212 us
  waiting for transfers between devices  86.5 us (40%)
  Pallas kernels  63.1 us (29%)
  starting transfers between devices  47.2 us (22%)
  local copies, waits for them, and re-layouts  9.19 us (4%)
  other arithmetic  5.59 us (3%)
    all_to_all x1, waiting for transfers between devices, per_device(): lax.all_to_all(rows_back, axes, split_axis=0, concat_axis=0, tiled=True)  52 us
    pallas_call x1, Pallas kernels, convs(): pl.pallas_call(conv_kernel, out_shape=(jax.ShapeDtypeStruct((rows + 2 * L...  30.4 us
    ppermute x1, waiting for transfers between devices, per_device(): cot_left = lax.ppermute(cot[:, mid - PAIRS:], 'tile', east)  19.1 us
    all_to_all x1, waiting for transfers between devices, per_device(): lax.all_to_all(sent, axes, split_axis=0, concat_axis=0, tiled=True)  12.2 us
    all_to_all x1, starting transfers between devices, per_device(): lax.all_to_all(rows_back, axes, split_axis=0, concat_axis=0, tiled=True)  12.1 us
    all_to_all x1, starting transfers between devices, per_device(): lax.all_to_all(sent, axes, split_axis=0, concat_axis=0, tiled=True)  10.9 us
    pallas_call x1, Pallas kernels, splat(): pl.pallas_call(splat_kernel, out_shape=(jax.ShapeDtypeStruct(shape, BF),...  10.7 us
    pallas_call x1, Pallas kernels, gather(): pl.pallas_call(gather_kernel, out_shape=pltpu.HBM((owners, channels, heig...  9.11 us
  transfers between devices with their start and end apart: 12, of which 5 were waited for; matrix products, arithmetic and copies ran while one was open for 6% of the time, Pallas kernels for 5%

profile of v4, /device:TPU:6, one launch (start us, length us, event | category | flops | bytes accessed | tf_op | source)
XLA Modules:
  0.0 212.5 jit_solution(1922498702947909606)
XLA Ops:
  0.6 5.4 %pack.1 = bf16[128,136,128]{2,1,0:T(8,128)(2,1)} custom-call(s32[4,1,16]{2,1,0:T(1,128)} %bitcast.15, s32[4,16]{1,0:T(4,128)} %local.1, s32[4,16,64]{2,1,0:T(8,128)} %cells.1, bf16[64,64,128]{2,1,0:T(8,128)(2,1)} %bitcast.21, bf16[64,128,128]{2,1,0:T(8,128)(2,1)} %bitcast.19), custom_call_target="tpu_custom_call" | custom-call | tf_op jit(solution)/shard_map/pack/pallas_call | solution.py:110
  6.0 10.9 %all-to-all-start = ((bf16[128,136,128]{2,1,0:T(8,128)(2,1)}), bf16[128,136,128]{2,1,0:T(8,128)(2,1)}, u32[]{:S(2)}, u32[]{:S(2)}) async-start(bf16[128,136,128]{2,1,0:T(8,128)(2,1)} %pack.1), calls=%async_computation | async-start | bytes 8912896 | tf_op jit(solution)/shard_map/all_to_all | solution.py:501
  17.1 2.2 %collective-permute-start.8 = (bf16[4,128,256]{2,1,0:T(8,128)(2,1)S(1)}, bf16[4,128,256]{2,1,0:T(8,128)(2,1)S(1)}, u32[]{:S(2)}, u32[]{:S(2)}) collective-permute-start(bf16[4,128,256]{2,1,0:T(8,128)(2,1)S(1)} %slice.56), channel_id=1, source_target_pairs={{0,16},{16,32},{32,48},{48,64},{64,80},{80,96},{96,112},{1,17},{17... | collective-permute-start | bytes 786440 | tf_op jit(solution)/shard_map/ppermute | solution.py:506
  19.3 3.5 %collective-permute-start.9 = (bf16[4,128,256]{2,1,0:T(8,128)(2,1)S(1)}, bf16[4,128,256]{2,1,0:T(8,128)(2,1)S(1)}, u32[]{:S(2)}, u32[]{:S(2)}) collective-permute-start(bf16[4,128,256]{2,1,0:T(8,128)(2,1)S(1)} %slice.58), channel_id=1, source_target_pairs={{16,0},{32,16},{48,32},{64,48},{80,64},{96,80},{112,96},{17,1},{33... | collective-permute-start | bytes 786440 | tf_op jit(solution)/shard_map/ppermute | solution.py:507
  22.9 1.4 reshape.34.cot_middle
  25.6 4.5 %collective-permute-start.4 = (bf16[16,8,256]{2,1,0:T(8,128)(2,1)S(1)}, bf16[16,8,256]{2,1,0:T(8,128)(2,1)S(1)}, u32[]{:S(2)}, u32[]{:S(2)}) collective-permute-start(bf16[16,8,256]{2,1,0:T(8,128)(2,1)S(1)} %get-tuple-element.18), channel_id=1, source_target_pairs={{0,1},{1,2},{2,3},{3,4},{4,5},{5,6},{6,7},{7,8},{8,9},{9,10},{10,1... | collective-permute-start | bytes 196616 | tf_op jit(solution)/shard_map/ppermute | solution.py:508
  30.3 1.8 fusion.4
  32.1 4.7 %copy.11 = bf16[4,3,4,128,256]{4,3,2,1,0:T(8,128)(2,1)} copy(bf16[4,3,4,128,256]{3,4,2,1,0:T(8,128)(2,1)} %fusion.4) | data formatting | bytes 6291456 | tf_op jit(solution)/shard_map/concatenate | solution.py:480
  37.2 1.4 copy-done.1
  38.7 3.2 %maximum_multiply_fusion.weights_far = bf16[8,1536,256]{2,1,0:T(8,128)(2,1)} fusion(bf16[4,1536,256]{2,1,0:T(8,128)(2,1)S(1)} %bitcast.17, bf16[4,1536,256]{2,1,0:T(8,128)(2,1)S(1)} %bitcast.18), kind=kLoop, calls=%fused_computation.4 | loop fusion | flops 6291456 | bytes 12582912 | tf_op jit(solution)/shard_map/mul | solution.py:512
  41.9 19.1 %collective-permute-done.4.cot_left = bf16[16,8,256]{2,1,0:T(8,128)(2,1)S(1)} collective-permute-done((bf16[16,8,256]{2,1,0:T(8,128)(2,1)S(1)}, bf16[16,8,256]{2,1,0:T(8,128)(2,1)S(1)}, u32[]{:S(2)}, u32[]{:S(2)}) %collective-permute-start.4) | collective-permute-done | bytes 65568 | tf_op jit(solution)/shard_map/ppermute | solution.py:508
  61.0 12.2 %all-to-all-done.meta_all.message = bf16[128,136,128]{2,1,0:T(8,128)(2,1)} async-done(((bf16[128,136,128]{2,1,0:T(8,128)(2,1)}), bf16[128,136,128]{2,1,0:T(8,128)(2,1)}, u32[]{:S(2)}, u32[]{:S(2)}) %all-to-all-start) | async-done | bytes 4456480 | tf_op jit(solution)/shard_map/all_to_all | solution.py:501
  73.2 10.7 %splat.1 = (bf16[16,128,256]{2,1,0:T(8,128)(2,1)S(1)}, s32[2,128]{1,0:T(2,128)S(1)}) custom-call(bf16[128,136,128]{2,1,0:T(8,128)(2,1)} %all-to-all-done.meta_all.message, bf16[128,136,128]{2,1,0:T(8,128)(2,1)} %all-to-all-done.meta_all.message), custom_call_target="tpu_custom_call" | custom-call | tf_op jit(solution)/shard_map/splat/pallas_call | solution.py:193
  83.9 1.3 collective-permute-start.2
  86.6 1.9 collective-permute-start.1
  88.5 2.4 %collective-permute-start = (bf16[8,128,256]{2,1,0:T(8,128)(2,1)S(1)}, bf16[8,128,256]{2,1,0:T(8,128)(2,1)S(1)}, u32[]{:S(2)}, u32[]{:S(2)}) collective-permute-start(bf16[8,128,256]{2,1,0:T(8,128)(2,1)S(1)} %get-tuple-element.22), channel_id=1, source_target_pairs={{0,16},{16,32},{32,48},{48,64},{64,80},{80,96},{96,112},{1,17},{17... | collective-permute-start | bytes 1572872 | tf_op jit(solution)/shard_map/ppermute | solution.py:521
  91.5 1.9 collective-permute-start.6
  93.4 3.8 %collective-permute-start.7 = (bf16[12,16,256]{2,1,0:T(8,128)(2,1)S(1)}, bf16[12,16,256]{2,1,0:T(8,128)(2,1)S(1)}, u32[]{:S(2)}, u32[]{:S(2)}) collective-permute-start(bf16[12,16,256]{2,1,0:T(8,128)(2,1)S(1)} %pad_maximum_fusion.1), channel_id=1, source_target_pairs={{16,0},{32,16},{48,32},{64,48},{80,64},{96,80},{112,96},{17,1},{33... | collective-permute-start | bytes 294920 | tf_op jit(solution)/shard_map/ppermute | solution.py:530
  97.4 2.7 %collective-permute-done.6.corner_above = bf16[12,16,256]{2,1,0:T(8,128)(2,1)S(1)} collective-permute-done((bf16[12,16,256]{2,1,0:T(8,128)(2,1)S(1)}, bf16[12,16,256]{2,1,0:T(8,128)(2,1)S(1)}, u32[]{:S(2)}, u32[]{:S(2)}) %collective-permute-start.6) | collective-permute-done | bytes 98336 | tf_op jit(solution)/shard_map/ppermute | solution.py:527
  100.1 30.4 %convs.1 = (bf16[24,128,256]{2,1,0:T(8,128)(2,1)}, bf16[16,128,256]{2,1,0:T(8,128)(2,1)S(1)}) custom-call(s32[4]{0:T(128)S(1)} %add_convert_fusion.edges, bf16[16,128,256]{2,1,0:T(8,128)(2,1)S(1)} %get-tuple-element.9.middle, bf16[8,128,256]{2,1,0:T(8,128)(2,1)S(1)} %collective-permute-done.above, bf16[8,128,256]{2,1,0:T(8,128)(2,1)S(1)} %collective-permute-done.1.below, ...), custom_call_target="tpu_custom_call" | custom-call | tf_op jit(solution)/shard_map/convs/pallas_call | solution.py:360
  130.5 9.1 %gather.1 = bf16[128,128,128]{2,1,0:T(8,128)(2,1)} custom-call(s32[2,128]{1,0:T(2,128)S(1)} %get-tuple-element.11.tiles, bf16[128,136,128]{2,1,0:T(8,128)(2,1)} %all-to-all-done.meta_all.message, bf16[16,128,256]{2,1,0:T(8,128)(2,1)S(1)} %get-tuple-element.12.grad), custom_call_target="tpu_custom_call" | custom-call | tf_op jit(solution)/shard_map/gather/pallas_call | solution.py:414
  139.6 12.1 %all-to-all-start.1 = ((bf16[128,128,128]{2,1,0:T(8,128)(2,1)}), bf16[128,128,128]{2,1,0:T(8,128)(2,1)}, u32[]{:S(2)}, u32[]{:S(2)}) async-start(bf16[128,128,128]{2,1,0:T(8,128)(2,1)} %gather.1), calls=%async_computation.1 | async-start | bytes 8388608 | tf_op jit(solution)/shard_map/all_to_all | solution.py:539
  153.0 52.0 %all-to-all-done.1.returned = bf16[128,128,128]{2,1,0:T(8,128)(2,1)} async-done(((bf16[128,128,128]{2,1,0:T(8,128)(2,1)}), bf16[128,128,128]{2,1,0:T(8,128)(2,1)}, u32[]{:S(2)}, u32[]{:S(2)}) %all-to-all-start.1) | async-done | bytes 4194336 | tf_op jit(solution)/shard_map/all_to_all | solution.py:539
  205.0 7.5 %final.1 = (bf16[64,64,128]{2,1,0:T(8,128)(2,1)}, bf16[64,128,128]{2,1,0:T(8,128)(2,1)}) custom-call(s32[4,1,16]{2,1,0:T(1,128)S(1)} %bitcast.16, bf16[128,128,128]{2,1,0:T(8,128)(2,1)} %all-to-all-done.1.returned, bf16[64,64,128]{2,1,0:T(8,128)(2,1)} %bitcast.22, bf16[64,128,128]{2,1,0:T(8,128)(2,1)} %bitcast.20), custom_call_target="tpu_custom_call" | custom-call | tf_op jit(solution)/shard_map/final/pallas_call | solution.py:461
  (38 shorter events, 5.3 us)
Async XLA Ops:
  6.0 10.9 %copy-start.3 = (bf16[16,256,128]{2,1,0:T(8,128)(2,1)S(1)}, bf16[16,256,128]{2,1,0:T(8,128)(2,1)}, u32[]{:S(2)}) copy-start(bf16[16,256,128]{2,1,0:T(8,128)(2,1)} %param.13) | copy-start | bytes 3145732
  6.0 67.2 %all-to-all-start = ((bf16[128,136,128]{2,1,0:T(8,128)(2,1)}), bf16[128,136,128]{2,1,0:T(8,128)(2,1)}, u32[]{:S(2)}, u32[]{:S(2)}) async-start(bf16[128,136,128]{2,1,0:T(8,128)(2,1)} %pack.1), calls=%async_computation | async-start | bytes 8912896 | tf_op jit(solution)/shard_map/all_to_all | solution.py:501
  16.9 13.3 %copy-start.2 = (bf16[4,3,3,128,128]{4,3,2,1,0:T(8,128)(2,1)S(1)}, bf16[4,3,3,128,128]{4,3,2,1,0:T(8,128)(2,1)}, u32[]{:S(2)}) copy-start(bf16[4,3,3,128,128]{4,3,2,1,0:T(8,128)(2,1)} %param.12) | copy-start | bytes 3538948
  17.1 76.4 %collective-permute-start.8 = (bf16[4,128,256]{2,1,0:T(8,128)(2,1)S(1)}, bf16[4,128,256]{2,1,0:T(8,128)(2,1)S(1)}, u32[]{:S(2)}, u32[]{:S(2)}) collective-permute-start(bf16[4,128,256]{2,1,0:T(8,128)(2,1)S(1)} %slice.56), channel_id=1, source_target_pairs={{0,16},{16,32},{32,48},{48,64},{64,80},{80,96},{96,112},{1,17},{17... | collective-permute-start | bytes 786440 | tf_op jit(solution)/shard_map/ppermute | solution.py:506
  19.3 78.0 %collective-permute-start.9 = (bf16[4,128,256]{2,1,0:T(8,128)(2,1)S(1)}, bf16[4,128,256]{2,1,0:T(8,128)(2,1)S(1)}, u32[]{:S(2)}, u32[]{:S(2)}) collective-permute-start(bf16[4,128,256]{2,1,0:T(8,128)(2,1)S(1)} %slice.58), channel_id=1, source_target_pairs={{16,0},{32,16},{48,32},{64,48},{80,64},{96,80},{112,96},{17,1},{33... | collective-permute-start | bytes 786440 | tf_op jit(solution)/shard_map/ppermute | solution.py:507
  24.3 36.7 %collective-permute-start.5 = (bf16[16,8,256]{2,1,0:T(8,128)(2,1)S(1)}, bf16[16,8,256]{2,1,0:T(8,128)(2,1)S(1)}, u32[]{:S(2)}, u32[]{:S(2)}) collective-permute-start(bf16[16,8,256]{2,1,0:T(8,128)(2,1)S(1)} %get-tuple-element.17), channel_id=1, source_target_pairs={{1,0},{2,1},{3,2},{4,3},{5,4},{6,5},{7,6},{8,7},{9,8},{10,9},{11,1... | collective-permute-start | bytes 196616 | tf_op jit(solution)/shard_map/ppermute | solution.py:509
  25.6 35.4 %collective-permute-start.4 = (bf16[16,8,256]{2,1,0:T(8,128)(2,1)S(1)}, bf16[16,8,256]{2,1,0:T(8,128)(2,1)S(1)}, u32[]{:S(2)}, u32[]{:S(2)}) collective-permute-start(bf16[16,8,256]{2,1,0:T(8,128)(2,1)S(1)} %get-tuple-element.18), channel_id=1, source_target_pairs={{0,1},{1,2},{2,3},{3,4},{4,5},{5,6},{6,7},{7,8},{8,9},{9,10},{10,1... | collective-permute-start | bytes 196616 | tf_op jit(solution)/shard_map/ppermute | solution.py:508
  36.8 1.9 copy-start.1
  83.9 4.6 %collective-permute-start.2 = (bf16[16,8,256]{2,1,0:T(8,128)(2,1)S(1)}, bf16[16,8,256]{2,1,0:T(8,128)(2,1)S(1)}, u32[]{:S(2)}, u32[]{:S(2)}) collective-permute-start(bf16[16,8,256]{2,1,0:T(8,128)(2,1)S(1)} %get-tuple-element.20), channel_id=1, source_target_pairs={{0,1},{1,2},{2,3},{3,4},{4,5},{5,6},{6,7},{7,8},{8,9},{9,10},{10,1... | collective-permute-start | bytes 196616 | tf_op jit(solution)/shard_map/ppermute | solution.py:523
  85.3 6.2 %collective-permute-start.3 = (bf16[16,8,256]{2,1,0:T(8,128)(2,1)S(1)}, bf16[16,8,256]{2,1,0:T(8,128)(2,1)S(1)}, u32[]{:S(2)}, u32[]{:S(2)}) collective-permute-start(bf16[16,8,256]{2,1,0:T(8,128)(2,1)S(1)} %get-tuple-element.19), channel_id=1, source_target_pairs={{1,0},{2,1},{3,2},{4,3},{5,4},{6,5},{7,6},{8,7},{9,8},{10,9},{11,1... | collective-permute-start | bytes 196616 | tf_op jit(solution)/shard_map/ppermute | solution.py:524
  86.6 13.5 %collective-permute-start.1 = (bf16[8,128,256]{2,1,0:T(8,128)(2,1)S(1)}, bf16[8,128,256]{2,1,0:T(8,128)(2,1)S(1)}, u32[]{:S(2)}, u32[]{:S(2)}) collective-permute-start(bf16[8,128,256]{2,1,0:T(8,128)(2,1)S(1)} %get-tuple-element.21), channel_id=1, source_target_pairs={{16,0},{32,16},{48,32},{64,48},{80,64},{96,80},{112,96},{17,1},{33... | collective-permute-start | bytes 1572872 | tf_op jit(solution)/shard_map/ppermute | solution.py:522
  88.5 11.6 %collective-permute-start = (bf16[8,128,256]{2,1,0:T(8,128)(2,1)S(1)}, bf16[8,128,256]{2,1,0:T(8,128)(2,1)S(1)}, u32[]{:S(2)}, u32[]{:S(2)}) collective-permute-start(bf16[8,128,256]{2,1,0:T(8,128)(2,1)S(1)} %get-tuple-element.22), channel_id=1, source_target_pairs={{0,16},{16,32},{32,48},{48,64},{64,80},{80,96},{96,112},{1,17},{17... | collective-permute-start | bytes 1572872 | tf_op jit(solution)/shard_map/ppermute | solution.py:521
  91.5 8.6 %collective-permute-start.6 = (bf16[12,16,256]{2,1,0:T(8,128)(2,1)S(1)}, bf16[12,16,256]{2,1,0:T(8,128)(2,1)S(1)}, u32[]{:S(2)}, u32[]{:S(2)}) collective-permute-start(bf16[12,16,256]{2,1,0:T(8,128)(2,1)S(1)} %pad_maximum_fusion), channel_id=1, source_target_pairs={{0,16},{16,32},{32,48},{48,64},{64,80},{80,96},{96,112},{1,17},{17... | collective-permute-start | bytes 294920 | tf_op jit(solution)/shard_map/ppermute | solution.py:527
  93.4 6.6 %collective-permute-start.7 = (bf16[12,16,256]{2,1,0:T(8,128)(2,1)S(1)}, bf16[12,16,256]{2,1,0:T(8,128)(2,1)S(1)}, u32[]{:S(2)}, u32[]{:S(2)}) collective-permute-start(bf16[12,16,256]{2,1,0:T(8,128)(2,1)S(1)} %pad_maximum_fusion.1), channel_id=1, source_target_pairs={{16,0},{32,16},{48,32},{64,48},{80,64},{96,80},{112,96},{17,1},{33... | collective-permute-start | bytes 294920 | tf_op jit(solution)/shard_map/ppermute | solution.py:530
  139.6 12.1 %copy-start.4 = (bf16[24,128,256]{2,1,0:T(8,128)(2,1)S(1)}, bf16[24,128,256]{2,1,0:T(8,128)(2,1)}, u32[]{:S(2)}) copy-start(bf16[24,128,256]{2,1,0:T(8,128)(2,1)} %get-tuple-element.10) | copy-start | bytes 4718596
  139.6 65.3 %all-to-all-start.1 = ((bf16[128,128,128]{2,1,0:T(8,128)(2,1)}), bf16[128,128,128]{2,1,0:T(8,128)(2,1)}, u32[]{:S(2)}, u32[]{:S(2)}) async-start(bf16[128,128,128]{2,1,0:T(8,128)(2,1)} %gather.1), calls=%async_computation.1 | async-start | bytes 8388608 | tf_op jit(solution)/shard_map/all_to_all | solution.py:539
  151.7 53.2 %copy-start = (s32[4,16,1]{1,2,0:T(1,128)S(1)}, s32[4,16,1]{1,2,0:T(1,128)}, u32[]{:S(2)}) copy-start(s32[4,16,1]{1,2,0:T(1,128)} %param.9) | copy-start | bytes 772

commit v5 on v4

--- a/solution.py
+++ b/solution.py
@@ -49,7 +49,9 @@
     return (cells // TS) * TS + (cells % 2) * (TS // 2) + (cells % TS) // 2
 
 
-def pack_kernel(owner, local, cells, depth, context, out, count, wide, lifted, meta, sems):
+def pack_kernel(
+    owner, local, cells, depth, context, out, slots, count, wide, lifted, meta, sems
+):
     step = pl.program_id(0)
     blocks, bins, _ = depth.shape
     owners = out.shape[0]
@@ -70,6 +72,7 @@
         each = local.shape[1]
         tile = local[lax.div(at, each), lax.rem(at, each)].astype(F32)
         rank = take_slot(to, count)
+        slots[at] = 2 * to + rank
         product = jnp.dot(depth[b], context[b], preferred_element_type=F32)
         lifted[lax.div(at, 2), pl.ds(pl.multiple_of(lax.rem(at, 2) * bins, bins), bins), :] = product.astype(BF)
         mine = (lane // bins) == rank
@@ -109,7 +112,10 @@
     chunk = blocks // 4
     return pl.pallas_call(
         pack_kernel,
-        out_shape=pltpu.HBM((owners, 2 * bins + 8, channels), BF),
+        out_shape=(
+            pltpu.HBM((owners, 2 * bins + 8, channels), BF),
+            jax.ShapeDtypeStruct((blocks,), jnp.int32),
+        ),
         grid=(blocks // chunk,),
         in_specs=[
             pl.BlockSpec(memory_space=pltpu.SMEM),
@@ -118,7 +124,10 @@
             pl.BlockSpec((chunk, bins, pixels), lambda i: (i, 0, 0)),
             pl.BlockSpec((chunk, pixels, channels), lambda i: (i, 0, 0)),
         ],
-        out_specs=pl.BlockSpec(memory_space=pltpu.HBM),
+        out_specs=(
+            pl.BlockSpec(memory_space=pltpu.HBM),
+            pl.BlockSpec(memory_space=pltpu.SMEM),
+        ),
         scratch_shapes=[
             pltpu.SMEM((owners,), jnp.int32),
             pltpu.VMEM((blocks, 2 * bins), F32),
@@ -225,7 +234,7 @@
 
 def conv_kernel(
     edges, middle, above, below, left, right, corner_above, corner_below,
-    cot_middle, cot_above, cot_below, cot_left, cot_right, weights_far,
+    cot_above, cot_below, cot_far, weights_far,
     bev, grad, ping, pong, slopes, mask, sums, weights, cot, sems,
 ):
     rows, mid, double = middle.shape
@@ -236,8 +245,12 @@
         pltpu.make_async_copy(weights_far.at[i], weights.at[i], sems.at[i])
         for i in range(2 * LAYERS)
     ]
+    cot_arrival = pltpu.make_async_copy(
+        cot_far, cot.at[pl.ds(LAYERS, rows)], sems.at[2 * LAYERS]
+    )
     for copy in arrivals[:LAYERS]:
         copy.start()
+    cot_arrival.start()
     for copy in arrivals[: LAYERS - 1 : -1]:
         copy.start()
     column = lax.broadcasted_iota(jnp.int32, (wide, double), 0)
@@ -268,13 +281,7 @@
         return carry
 
     lax.fori_loop(0, EXT, load_outer, 0)
-
-    def load_cot(k, carry):
-        cot[LAYERS + k] = joined(cot_left[k], cot_middle[k], cot_right[k]).astype(BF)
-        return carry
-
     lax.fori_loop(0, rows, load_inner, 0)
-    lax.fori_loop(0, rows, load_cot, 0)
     for k in range(LAYERS):
         for corner, field, base in (
             (corner_above, cot_above, 0), (corner_below, cot_below, LAYERS + rows)
@@ -319,7 +326,12 @@
                 slope = slopes[offsets[layer - 1] + here + 2 * (step + 1)].astype(F32)
                 put(target, here, sums[side] * slope)
             else:
-                grad[here] = sums[side, PAIRS : PAIRS + mid].astype(BF)
+                value = sums[side, PAIRS : PAIRS + mid]
+                for tile in range(mid // 8):
+                    piece = value[tile * 8 : (tile + 1) * 8]
+                    piece = jnp.concatenate([piece[:, :channels], piece[:, channels:]], axis=0)
+                    at = pl.ds(pl.multiple_of(here * TS, TS), TS)
+                    grad[tile, at, :] = piece.astype(BF)
 
     stages = []
     for layer in range(LAYERS):
@@ -333,6 +345,8 @@
     for index, count, epilogue in stages:
         size, starts = chunks_of(count)
         arrivals[index].wait()
+        if index == LAYERS - 1:
+            cot_arrival.wait()
         if finish is not None:
             finish()
         matmul(source, index, 0, size)
@@ -348,7 +362,7 @@
     finish()
 
 
-def convs(edges, weights, *fields):
+def convs(edges, weights, cot, *fields):
     middle = fields[0]
     rows, mid, double = middle.shape
     wide = mid + 2 * PAIRS
@@ -361,9 +375,9 @@
         conv_kernel,
         out_shape=(
             jax.ShapeDtypeStruct((rows + 2 * LAYERS, mid, double), BF),
-            jax.ShapeDtypeStruct(middle.shape, BF),
-        ),
-        in_specs=[pl.BlockSpec(memory_space=pltpu.SMEM)] + [vmem] * len(fields) + [hbm],
+            jax.ShapeDtypeStruct((mid // 8, rows * TS, double // 2), BF),
+        ),
+        in_specs=[pl.BlockSpec(memory_space=pltpu.SMEM)] + [vmem] * len(fields) + [hbm] * 2,
         out_specs=(vmem, vmem),
         scratch_shapes=[
             buffer,
@@ -373,39 +387,33 @@
             pltpu.VMEM((7, wide, double), F32),
             pltpu.VMEM(weights.shape, BF),
             pltpu.VMEM((rows + 2 * LAYERS, wide, double), BF),
-            pltpu.SemaphoreType.DMA((2 * LAYERS,)),
+            pltpu.SemaphoreType.DMA((2 * LAYERS + 1,)),
         ],
         compiler_params=pltpu.CompilerParams(vmem_limit_bytes=48 << 20),
         name="convs",
-    )(edges, *fields, in_hbm(weights))
-
-
-def gather_kernel(tiles, message, grad, out, turned):
+    )(edges, *fields, in_hbm(cot), in_hbm(weights))
+
+
+def gather_kernel(tiles, meta_all, grad, out, columns):
     step = pl.program_id(0)
-    sources, _, channels = message.shape
-    _, mid, _ = grad.shape
-    cells = TS * TS
-    bins = out.shape[2] // 2
+    owners = meta_all.shape[0]
+    sources, slots, channels = out.shape
+    bins = slots // 2
+    count, cells, _ = grad.shape
 
     @pl.when(step == 0)
     def _():
-        for tile in range(mid // 8):
-            piece = grad[:, tile * 8 : (tile + 1) * 8, :].astype(F32)
-            piece = jnp.stack([piece[:, :, :channels], piece[:, :, channels:]], axis=1)
-            turned[tile] = piece.reshape(cells, channels).T.astype(BF)
-
-    lane = lax.broadcasted_iota(jnp.int32, (1, 2 * bins), 1)
-
-    def source(s, carry):
-        hot = cell_onehot(message[s].astype(jnp.int32)[0:1], cells)
-        at = step * sources + s
-        here = [jnp.minimum(tiles[rank, at], mid // 8 - 1) for rank in range(2)]
-        both = jnp.concatenate([turned[here[0]], turned[here[1]]], axis=0)
-        picked = jnp.dot(both, hot, preferred_element_type=F32)
-        out[s] = jnp.where(lane < bins, picked[:channels], picked[channels:]).astype(BF)
-        return carry
-
-    lax.fori_loop(0, sources, source, 0, unroll=8)
+        columns[...] = meta_all[...].astype(F32)[:, 0, :].T.astype(jnp.int32)
+
+    mine = pltpu.roll(columns[...], lax.rem(owners - step * sources, owners), 1)
+    number = lax.broadcasted_iota(jnp.int32, (slots, cells), 1)
+    for s in range(sources):
+        hot = jnp.where(mine[:, s : s + 1] == number, 1.0, 0.0).astype(BF)
+        here = [jnp.minimum(tiles[rank, step * sources + s], count - 1) for rank in range(2)]
+        both = jnp.concatenate([grad[here[0]], grad[here[1]]], axis=1)
+        picked = jnp.dot(hot, both, preferred_element_type=F32)
+        out[s, 0:bins, :] = picked[:bins, :channels].astype(BF)
+        out[s, bins:, :] = picked[bins:, channels:].astype(BF)
 
 
 def gather(tiles, message, grad):
@@ -413,49 +421,57 @@
     chunk = owners // 8
     return pl.pallas_call(
         gather_kernel,
-        out_shape=pltpu.HBM((owners, channels, height - 8), BF),
+        out_shape=pltpu.HBM((owners, height - 8, channels), BF),
         grid=(owners // chunk,),
         in_specs=[
             pl.BlockSpec(memory_space=pltpu.SMEM),
-            pl.BlockSpec((chunk, 8, channels), lambda i: (i, height // 8 - 1, 0)),
+            pl.BlockSpec((owners, 8, channels), lambda i: (0, height // 8 - 1, 0)),
             pl.BlockSpec(grad.shape, lambda i: (0, 0, 0)),
         ],
-        out_specs=pl.BlockSpec((chunk, channels, height - 8), lambda i: (i, 0, 0)),
-        scratch_shapes=[pltpu.VMEM((grad.shape[1] // 8, channels, TS * TS), BF)],
-        compiler_params=pltpu.CompilerParams(vmem_limit_bytes=40 << 20),
+        out_specs=pl.BlockSpec((chunk, height - 8, channels), lambda i: (i, 0, 0)),
+        scratch_shapes=[pltpu.VMEM((height - 8, owners), jnp.int32)],
+        compiler_params=pltpu.CompilerParams(vmem_limit_bytes=24 << 20),
         name="gather",
     )(tiles, message, grad)
 
 
-def final_kernel(owner, returned, depth, context, grad_depth, grad_context, count):
+def final_kernel(slots, returned, depth, context, grad_depth, grad_context, fetched, sems):
     step = pl.program_id(0)
     blocks, bins, _ = depth.shape
+    halves = blocks // 2
 
     @pl.when(step == 0)
     def _():
-        clear_counts(count, returned.shape[0])
-
-    def block(b, carry):
-        to = owner_of(owner, step * blocks + b)
-        rank = take_slot(to, count)
-        turned = returned[to].T
-        rows = jnp.where(rank == 0, turned[0:bins], turned[bins : 2 * bins])
+        for b in range(2 * fetched.shape[0]):
+            slot = slots[b]
+            start = pl.multiple_of(lax.rem(slot, 2) * bins, bins)
+            pltpu.make_async_copy(
+                returned.at[lax.div(slot, 2), pl.ds(start, bins), :],
+                fetched.at[b // 2, pl.ds((b % 2) * bins, bins), :],
+                sems.at[b // blocks],
+            ).start()
+
+    pltpu.make_async_copy(
+        returned.at[pl.ds(0, halves)],
+        fetched.at[pl.ds(pl.multiple_of(step * halves, halves), halves)],
+        sems.at[step],
+    ).wait()
+
+    for b in range(blocks):
+        rows = fetched[step * halves + b // 2, (b % 2) * bins : (b % 2 + 1) * bins, :]
         grad_depth[b] = lax.dot_general(
             rows, context[b], (((1,), (1,)), ((), ())), preferred_element_type=F32
         ).astype(BF)
         grad_context[b] = lax.dot_general(
             depth[b], rows, (((0,), (0,)), ((), ())), preferred_element_type=F32
         ).astype(BF)
-        return carry
-
-    lax.fori_loop(0, blocks, block, 0, unroll=8)
-
-
-def final(owner, returned, depth, context):
+
+
+def final(slots, returned, depth, context):
     blocks, bins, pixels = depth.shape
     channels = context.shape[2]
-    chunk = blocks // 4
-    whole = pl.BlockSpec(returned.shape, lambda i: (0, 0, 0))
+    steps = 4
+    chunk = blocks // steps
     depth_block = pl.BlockSpec((chunk, bins, pixels), lambda i: (i, 0, 0))
     context_block = pl.BlockSpec((chunk, pixels, channels), lambda i: (i, 0, 0))
     return pl.pallas_call(
@@ -464,13 +480,21 @@
             jax.ShapeDtypeStruct(depth.shape, BF),
             jax.ShapeDtypeStruct(context.shape, BF),
         ),
-        grid=(blocks // chunk,),
-        in_specs=[pl.BlockSpec(memory_space=pltpu.SMEM), whole, depth_block, context_block],
+        grid=(steps,),
+        in_specs=[
+            pl.BlockSpec(memory_space=pltpu.SMEM),
+            pl.BlockSpec(memory_space=pltpu.HBM),
+            depth_block,
+            context_block,
+        ],
         out_specs=(depth_block, context_block),
-        scratch_shapes=[pltpu.SMEM((returned.shape[0],), jnp.int32)],
-        compiler_params=pltpu.CompilerParams(vmem_limit_bytes=40 << 20),
+        scratch_shapes=[
+            pltpu.VMEM((blocks // 2,) + returned.shape[1:], BF),
+            pltpu.SemaphoreType.DMA((steps,)),
+        ],
+        compiler_params=pltpu.CompilerParams(vmem_limit_bytes=24 << 20),
         name="final",
-    )(owner, in_hbm(returned), depth, context)
+    )(slots, in_hbm(returned), depth, context)
 
 
 def paired_weights(kernel):
@@ -494,7 +518,7 @@
     flat_context = context.reshape(blocks, pixels, channels)
     owner = block_owner.transpose(0, 2, 1)
 
-    sent = pack(
+    sent, slots = pack(
         in_hbm(owner), in_hbm(block_local), in_hbm(block_cell), in_hbm(depth),
         in_hbm(flat_context), owners,
     )
@@ -507,6 +531,7 @@
     cot_below = lax.ppermute(cot[:LAYERS], "cam", up)
     cot_left = lax.ppermute(cot[:, mid - PAIRS :], "tile", east)
     cot_right = lax.ppermute(cot[:, :PAIRS], "tile", west)
+    cot_middle = jnp.concatenate([cot_left, cot, cot_right], axis=1)
     turned_weight = conv_weight[:, ::-1, ::-1].swapaxes(3, 4)
     weights = jnp.concatenate([paired_weights(conv_weight), paired_weights(turned_weight)], axis=0)
     weights = weights * jnp.asarray(0.5, BF)
@@ -523,21 +548,19 @@
     left = lax.ppermute(middle[:, mid - PAIRS :], "tile", east)
     right = lax.ppermute(middle[:, :PAIRS], "tile", west)
     sides = jnp.concatenate([left, right], axis=1)
-    cot_sides = jnp.concatenate([cot_left, cot_right], axis=1)
-    corner_above = lax.ppermute(
-        jnp.concatenate([sides[rows - EXT :], cot_sides[rows - LAYERS :]], axis=0), "cam", down
-    )
-    corner_below = lax.ppermute(
-        jnp.concatenate([sides[:EXT], cot_sides[:LAYERS]], axis=0), "cam", up
-    )
+    cot_sides = jnp.concatenate([cot_middle[:, :PAIRS], cot_middle[:, PAIRS + mid :]], axis=1)
+    lower = jnp.concatenate([sides[rows - EXT :], cot_sides[rows - LAYERS :]], axis=0)
+    upper = jnp.concatenate([sides[:EXT], cot_sides[:LAYERS]], axis=0)
+    corner_above = lax.ppermute(lower, "cam", down)
+    corner_below = lax.ppermute(upper, "cam", up)
 
     bev, grad = convs(
-        edges, weights, middle, above, below, left, right, corner_above, corner_below,
-        cot, cot_above, cot_below, cot_left, cot_right,
+        edges, weights, cot_middle, middle, above, below, left, right, corner_above,
+        corner_below, cot_above, cot_below,
     )
     rows_back = gather(tiles, message, grad)
     returned = lax.all_to_all(rows_back, axes, split_axis=0, concat_axis=0, tiled=True)
-    grad_depth, grad_context = final(owner, returned, in_hbm(depth), in_hbm(flat_context))
+    grad_depth, grad_context = final(slots, returned, in_hbm(depth), in_hbm(flat_context))
     return (
         bev[LAYERS : LAYERS + rows].reshape(cotangent.shape),
         grad_depth.reshape(depth_weights.shape),

time: 214 us -> 212 us (level)
  transfers between devices with their start and end apart: 12 -> 12, of which waited for: 5 -> 5; matrix products, arithmetic and copies ran while one was open for 6% -> 7% of each run, Pallas kernels for 5% -> 5%
where the time goes in v5:
time: 212 us; the launch traced here: 211 us
  waiting for transfers between devices  85.5 us (40%)
  Pallas kernels  61.4 us (29%)
  starting transfers between devices  47.1 us (22%)
  local copies, waits for them, and re-layouts  9.18 us (4%)
  other arithmetic  6.65 us (3%)
    all_to_all x1, waiting for transfers between devices, per_device(): lax.all_to_all(rows_back, axes, split_axis=0, concat_axis=0, tiled=True)  52 us
    pallas_call x1, Pallas kernels, convs(): pl.pallas_call(conv_kernel, out_shape=(jax.ShapeDtypeStruct((rows + 2 * L...  30.8 us
    ppermute x1, waiting for transfers between devices, per_device(): cot_left = lax.ppermute(cot[:, mid - PAIRS:], 'tile', east)  19.1 us
    all_to_all x1, waiting for transfers between devices, per_device(): lax.all_to_all(sent, axes, split_axis=0, concat_axis=0, tiled=True)  12.2 us
    all_to_all x1, starting transfers between devices, per_device(): lax.all_to_all(rows_back, axes, split_axis=0, concat_axis=0, tiled=True)  12 us
    all_to_all x1, starting transfers between devices, per_device(): lax.all_to_all(sent, axes, split_axis=0, concat_axis=0, tiled=True)  10.9 us
    pallas_call x1, Pallas kernels, splat(): pl.pallas_call(splat_kernel, out_shape=(jax.ShapeDtypeStruct(shape, BF),...  10.6 us
    pallas_call x1, Pallas kernels, gather(): pl.pallas_call(gather_kernel, out_shape=pltpu.HBM((owners, height - 8, ch...  7.53 us
  transfers between devices with their start and end apart: 12, of which 5 were waited for; matrix products, arithmetic and copies ran while one was open for 7% of the time, Pallas kernels for 5%

profile of v5, /device:TPU:6, one launch (start us, length us, event | category | flops | bytes accessed | tf_op | source)
XLA Modules:
  0.0 211.0 jit_solution(11055831090588843000)
XLA Ops:
  0.6 6.1 %pack.1 = (bf16[128,136,128]{2,1,0:T(8,128)(2,1)}, s32[64]{0:T(128)S(1)}) custom-call(s32[4,1,16]{2,1,0:T(1,128)} %bitcast.21, s32[4,16]{1,0:T(4,128)} %local.1, s32[4,16,64]{2,1,0:T(8,128)} %cells.1, bf16[64,64,128]{2,1,0:T(8,128)(2,1)} %bitcast.19, bf16[64,128,128]{2,1,0:T(8,128)(2,1)} %bitcast.17), custom_call_target="tpu_custom_call" | custom-call | tf_op jit(solution)/shard_map/pack/pallas_call | solution.py:113
  6.7 10.9 %all-to-all-start = ((bf16[128,136,128]{2,1,0:T(8,128)(2,1)}), bf16[128,136,128]{2,1,0:T(8,128)(2,1)}, u32[]{:S(2)}, u32[]{:S(2)}) async-start(bf16[128,136,128]{2,1,0:T(8,128)(2,1)} %get-tuple-element.11), calls=%async_computation | async-start | bytes 8912896 | tf_op jit(solution)/shard_map/all_to_all | solution.py:525
  17.8 2.2 %collective-permute-start.8 = (bf16[4,128,256]{2,1,0:T(8,128)(2,1)S(1)}, bf16[4,128,256]{2,1,0:T(8,128)(2,1)S(1)}, u32[]{:S(2)}, u32[]{:S(2)}) collective-permute-start(bf16[4,128,256]{2,1,0:T(8,128)(2,1)S(1)} %slice.56), channel_id=1, source_target_pairs={{0,16},{16,32},{32,48},{48,64},{64,80},{80,96},{96,112},{1,17},{17... | collective-permute-start | bytes 786440 | tf_op jit(solution)/shard_map/ppermute | solution.py:530
  20.0 3.5 %collective-permute-start.9 = (bf16[4,128,256]{2,1,0:T(8,128)(2,1)S(1)}, bf16[4,128,256]{2,1,0:T(8,128)(2,1)S(1)}, u32[]{:S(2)}, u32[]{:S(2)}) collective-permute-start(bf16[4,128,256]{2,1,0:T(8,128)(2,1)S(1)} %slice.58), channel_id=1, source_target_pairs={{16,0},{32,16},{48,32},{64,48},{80,64},{96,80},{112,96},{17,1},{33... | collective-permute-start | bytes 786440 | tf_op jit(solution)/shard_map/ppermute | solution.py:531
  23.6 1.4 reshape.34
  26.3 4.5 %collective-permute-start.4 = (bf16[16,8,256]{2,1,0:T(8,128)(2,1)S(1)}, bf16[16,8,256]{2,1,0:T(8,128)(2,1)S(1)}, u32[]{:S(2)}, u32[]{:S(2)}) collective-permute-start(bf16[16,8,256]{2,1,0:T(8,128)(2,1)S(1)} %get-tuple-element.22), channel_id=1, source_target_pairs={{0,1},{1,2},{2,3},{3,4},{4,5},{5,6},{6,7},{7,8},{8,9},{9,10},{10,1... | collective-permute-start | bytes 196616 | tf_op jit(solution)/shard_map/ppermute | solution.py:532
  31.0 1.8 fusion.4
  32.8 4.7 %copy.11 = bf16[4,3,4,128,256]{4,3,2,1,0:T(8,128)(2,1)} copy(bf16[4,3,4,128,256]{3,4,2,1,0:T(8,128)(2,1)} %fusion.4) | data formatting | bytes 6291456 | tf_op jit(solution)/shard_map/concatenate | solution.py:504
  38.0 1.4 copy-done
  39.4 3.2 %maximum_multiply_fusion.weights_far = bf16[8,1536,256]{2,1,0:T(8,128)(2,1)} fusion(bf16[4,1536,256]{2,1,0:T(8,128)(2,1)S(1)} %bitcast.15, bf16[4,1536,256]{2,1,0:T(8,128)(2,1)S(1)} %bitcast.16), kind=kLoop, calls=%fused_computation.4 | loop fusion | flops 6291456 | bytes 12582912 | tf_op jit(solution)/shard_map/mul | solution.py:537
  42.6 19.1 %collective-permute-done.4 = bf16[16,8,256]{2,1,0:T(8,128)(2,1)S(1)} collective-permute-done((bf16[16,8,256]{2,1,0:T(8,128)(2,1)S(1)}, bf16[16,8,256]{2,1,0:T(8,128)(2,1)S(1)}, u32[]{:S(2)}, u32[]{:S(2)}) %collective-permute-start.4) | collective-permute-done | bytes 65568 | tf_op jit(solution)/shard_map/ppermute | solution.py:532
  61.7 12.2 %all-to-all-done.meta_all.message = bf16[128,136,128]{2,1,0:T(8,128)(2,1)} async-done(((bf16[128,136,128]{2,1,0:T(8,128)(2,1)}), bf16[128,136,128]{2,1,0:T(8,128)(2,1)}, u32[]{:S(2)}, u32[]{:S(2)}) %all-to-all-start) | async-done | bytes 4456480 | tf_op jit(solution)/shard_map/all_to_all | solution.py:525
  73.9 10.6 %splat.1 = (bf16[16,128,256]{2,1,0:T(8,128)(2,1)S(1)}, s32[2,128]{1,0:T(2,128)S(1)}) custom-call(bf16[128,136,128]{2,1,0:T(8,128)(2,1)} %all-to-all-done.meta_all.message, bf16[128,136,128]{2,1,0:T(8,128)(2,1)} %all-to-all-done.meta_all.message), custom_call_target="tpu_custom_call" | custom-call | tf_op jit(solution)/shard_map/splat/pallas_call | solution.py:202
  84.6 1.3 collective-permute-start.2
  87.3 1.9 collective-permute-start.1
  89.2 2.4 %collective-permute-start = (bf16[8,128,256]{2,1,0:T(8,128)(2,1)S(1)}, bf16[8,128,256]{2,1,0:T(8,128)(2,1)S(1)}, u32[]{:S(2)}, u32[]{:S(2)}) collective-permute-start(bf16[8,128,256]{2,1,0:T(8,128)(2,1)S(1)} %get-tuple-element.26), channel_id=1, source_target_pairs={{0,16},{16,32},{32,48},{48,64},{64,80},{80,96},{96,112},{1,17},{17... | collective-permute-start | bytes 1572872 | tf_op jit(solution)/shard_map/ppermute | solution.py:546
  92.2 1.9 collective-permute-start.6
  94.2 3.8 %collective-permute-start.7 = (bf16[12,16,256]{2,1,0:T(8,128)(2,1)S(1)}, bf16[12,16,256]{2,1,0:T(8,128)(2,1)S(1)}, u32[]{:S(2)}, u32[]{:S(2)}) collective-permute-start(bf16[12,16,256]{2,1,0:T(8,128)(2,1)S(1)} %pad_maximum_fusion.2), channel_id=1, source_target_pairs={{16,0},{32,16},{48,32},{64,48},{80,64},{96,80},{112,96},{17,1},{33... | collective-permute-start | bytes 294920 | tf_op jit(solution)/shard_map/ppermute | solution.py:555
  99.1 1.7 collective-permute-done.6.corner_above
  100.8 30.8 %convs.1 = (bf16[24,128,256]{2,1,0:T(8,128)(2,1)S(1)}, bf16[16,256,128]{2,1,0:T(8,128)(2,1)S(1)}) custom-call(s32[4]{0:T(128)S(1)} %add_convert_fusion.edges, bf16[16,128,256]{2,1,0:T(8,128)(2,1)S(1)} %get-tuple-element.12.middle, bf16[8,128,256]{2,1,0:T(8,128)(2,1)S(1)} %collective-permute-done.above, ...), custom_call_target="tpu_custom_call" | custom-call | tf_op jit(solution)/shard_map/convs/pallas_call | solution.py:374
  131.6 7.5 %gather.1 = bf16[128,128,128]{2,1,0:T(8,128)(2,1)} custom-call(s32[2,128]{1,0:T(2,128)S(1)} %get-tuple-element.15.tiles, bf16[128,136,128]{2,1,0:T(8,128)(2,1)} %all-to-all-done.meta_all.message, bf16[16,256,128]{2,1,0:T(8,128)(2,1)S(1)} %get-tuple-element.16.grad), custom_call_target="tpu_custom_call" | custom-call | tf_op jit(solution)/shard_map/gather/pallas_call | solution.py:422
  139.1 12.0 %all-to-all-start.1 = ((bf16[128,128,128]{2,1,0:T(8,128)(2,1)}), bf16[128,128,128]{2,1,0:T(8,128)(2,1)}, u32[]{:S(2)}, u32[]{:S(2)}) async-start(bf16[128,128,128]{2,1,0:T(8,128)(2,1)} %gather.1), calls=%async_computation.1 | async-start | bytes 8388608 | tf_op jit(solution)/shard_map/all_to_all | solution.py:562
  152.4 52.0 %all-to-all-done.1.returned = bf16[128,128,128]{2,1,0:T(8,128)(2,1)} async-done(((bf16[128,128,128]{2,1,0:T(8,128)(2,1)}), bf16[128,128,128]{2,1,0:T(8,128)(2,1)}, u32[]{:S(2)}, u32[]{:S(2)}) %all-to-all-start.1) | async-done | bytes 4194336 | tf_op jit(solution)/shard_map/all_to_all | solution.py:562
  204.4 6.4 %final.1 = (bf16[64,64,128]{2,1,0:T(8,128)(2,1)}, bf16[64,128,128]{2,1,0:T(8,128)(2,1)}) custom-call(s32[64]{0:T(128)S(1)} %get-tuple-element.14.slots, bf16[128,128,128]{2,1,0:T(8,128)(2,1)} %all-to-all-done.1.returned, bf16[64,64,128]{2,1,0:T(8,128)(2,1)} %bitcast.20, bf16[64,128,128]{2,1,0:T(8,128)(2,1)} %bitcast.18), custom_call_target="tpu_custom_call" | custom-call | tf_op jit(solution)/shard_map/final/pallas_call | solution.py:477
  (35 shorter events, 6.4 us)
Async XLA Ops:
  6.7 10.9 %copy-start.2 = (bf16[16,256,128]{2,1,0:T(8,128)(2,1)S(1)}, bf16[16,256,128]{2,1,0:T(8,128)(2,1)}, u32[]{:S(2)}) copy-start(bf16[16,256,128]{2,1,0:T(8,128)(2,1)} %param.13) | copy-start | bytes 3145732
  6.7 67.2 %all-to-all-start = ((bf16[128,136,128]{2,1,0:T(8,128)(2,1)}), bf16[128,136,128]{2,1,0:T(8,128)(2,1)}, u32[]{:S(2)}, u32[]{:S(2)}) async-start(bf16[128,136,128]{2,1,0:T(8,128)(2,1)} %get-tuple-element.11), calls=%async_computation | async-start | bytes 8912896 | tf_op jit(solution)/shard_map/all_to_all | solution.py:525
  17.6 13.3 %copy-start.1 = (bf16[4,3,3,128,128]{4,3,2,1,0:T(8,128)(2,1)S(1)}, bf16[4,3,3,128,128]{4,3,2,1,0:T(8,128)(2,1)}, u32[]{:S(2)}) copy-start(bf16[4,3,3,128,128]{4,3,2,1,0:T(8,128)(2,1)} %param.12) | copy-start | bytes 3538948
  17.8 76.4 %collective-permute-start.8 = (bf16[4,128,256]{2,1,0:T(8,128)(2,1)S(1)}, bf16[4,128,256]{2,1,0:T(8,128)(2,1)S(1)}, u32[]{:S(2)}, u32[]{:S(2)}) collective-permute-start(bf16[4,128,256]{2,1,0:T(8,128)(2,1)S(1)} %slice.56), channel_id=1, source_target_pairs={{0,16},{16,32},{32,48},{48,64},{64,80},{80,96},{96,112},{1,17},{17... | collective-permute-start | bytes 786440 | tf_op jit(solution)/shard_map/ppermute | solution.py:530
  20.0 79.1 %collective-permute-start.9 = (bf16[4,128,256]{2,1,0:T(8,128)(2,1)S(1)}, bf16[4,128,256]{2,1,0:T(8,128)(2,1)S(1)}, u32[]{:S(2)}, u32[]{:S(2)}) collective-permute-start(bf16[4,128,256]{2,1,0:T(8,128)(2,1)S(1)} %slice.58), channel_id=1, source_target_pairs={{16,0},{32,16},{48,32},{64,48},{80,64},{96,80},{112,96},{17,1},{33... | collective-permute-start | bytes 786440 | tf_op jit(solution)/shard_map/ppermute | solution.py:531
  25.0 36.7 %collective-permute-start.5 = (bf16[16,8,256]{2,1,0:T(8,128)(2,1)S(1)}, bf16[16,8,256]{2,1,0:T(8,128)(2,1)S(1)}, u32[]{:S(2)}, u32[]{:S(2)}) collective-permute-start(bf16[16,8,256]{2,1,0:T(8,128)(2,1)S(1)} %get-tuple-element.21), channel_id=1, source_target_pairs={{1,0},{2,1},{3,2},{4,3},{5,4},{6,5},{7,6},{8,7},{9,8},{10,9},{11,1... | collective-permute-start | bytes 196616 | tf_op jit(solution)/shard_map/ppermute | solution.py:533
  26.3 35.4 %collective-permute-start.4 = (bf16[16,8,256]{2,1,0:T(8,128)(2,1)S(1)}, bf16[16,8,256]{2,1,0:T(8,128)(2,1)S(1)}, u32[]{:S(2)}, u32[]{:S(2)}) collective-permute-start(bf16[16,8,256]{2,1,0:T(8,128)(2,1)S(1)} %get-tuple-element.22), channel_id=1, source_target_pairs={{0,1},{1,2},{2,3},{3,4},{4,5},{5,6},{6,7},{7,8},{8,9},{9,10},{10,1... | collective-permute-start | bytes 196616 | tf_op jit(solution)/shard_map/ppermute | solution.py:532
  37.5 1.9 copy-start
  84.6 4.6 %collective-permute-start.2 = (bf16[16,8,256]{2,1,0:T(8,128)(2,1)S(1)}, bf16[16,8,256]{2,1,0:T(8,128)(2,1)S(1)}, u32[]{:S(2)}, u32[]{:S(2)}) collective-permute-start(bf16[16,8,256]{2,1,0:T(8,128)(2,1)S(1)} %get-tuple-element.24), channel_id=1, source_target_pairs={{0,1},{1,2},{2,3},{3,4},{4,5},{5,6},{6,7},{7,8},{8,9},{9,10},{10,1... | collective-permute-start | bytes 196616 | tf_op jit(solution)/shard_map/ppermute | solution.py:548
  86.0 6.2 %collective-permute-start.3 = (bf16[16,8,256]{2,1,0:T(8,128)(2,1)S(1)}, bf16[16,8,256]{2,1,0:T(8,128)(2,1)S(1)}, u32[]{:S(2)}, u32[]{:S(2)}) collective-permute-start(bf16[16,8,256]{2,1,0:T(8,128)(2,1)S(1)} %get-tuple-element.23), channel_id=1, source_target_pairs={{1,0},{2,1},{3,2},{4,3},{5,4},{6,5},{7,6},{8,7},{9,8},{10,9},{11,1... | collective-permute-start | bytes 196616 | tf_op jit(solution)/shard_map/ppermute | solution.py:549
  87.3 13.5 %collective-permute-start.1 = (bf16[8,128,256]{2,1,0:T(8,128)(2,1)S(1)}, bf16[8,128,256]{2,1,0:T(8,128)(2,1)S(1)}, u32[]{:S(2)}, u32[]{:S(2)}) collective-permute-start(bf16[8,128,256]{2,1,0:T(8,128)(2,1)S(1)} %get-tuple-element.25), channel_id=1, source_target_pairs={{16,0},{32,16},{48,32},{64,48},{80,64},{96,80},{112,96},{17,1},{33... | collective-permute-start | bytes 1572872 | tf_op jit(solution)/shard_map/ppermute | solution.py:547
  89.2 11.6 %collective-permute-start = (bf16[8,128,256]{2,1,0:T(8,128)(2,1)S(1)}, bf16[8,128,256]{2,1,0:T(8,128)(2,1)S(1)}, u32[]{:S(2)}, u32[]{:S(2)}) collective-permute-start(bf16[8,128,256]{2,1,0:T(8,128)(2,1)S(1)} %get-tuple-element.26), channel_id=1, source_target_pairs={{0,16},{16,32},{32,48},{48,64},{64,80},{80,96},{96,112},{1,17},{17... | collective-permute-start | bytes 1572872 | tf_op jit(solution)/shard_map/ppermute | solution.py:546
  92.2 8.6 %collective-permute-start.6 = (bf16[12,16,256]{2,1,0:T(8,128)(2,1)S(1)}, bf16[12,16,256]{2,1,0:T(8,128)(2,1)S(1)}, u32[]{:S(2)}, u32[]{:S(2)}) collective-permute-start(bf16[12,16,256]{2,1,0:T(8,128)(2,1)S(1)} %pad_maximum_fusion.1), channel_id=1, source_target_pairs={{0,16},{16,32},{32,48},{48,64},{64,80},{80,96},{96,112},{1,17},{17... | collective-permute-start | bytes 294920 | tf_op jit(solution)/shard_map/ppermute | solution.py:554
  94.2 6.6 %collective-permute-start.7 = (bf16[12,16,256]{2,1,0:T(8,128)(2,1)S(1)}, bf16[12,16,256]{2,1,0:T(8,128)(2,1)S(1)}, u32[]{:S(2)}, u32[]{:S(2)}) collective-permute-start(bf16[12,16,256]{2,1,0:T(8,128)(2,1)S(1)} %pad_maximum_fusion.2), channel_id=1, source_target_pairs={{16,0},{32,16},{48,32},{64,48},{80,64},{96,80},{112,96},{17,1},{33... | collective-permute-start | bytes 294920 | tf_op jit(solution)/shard_map/ppermute | solution.py:555
  139.1 65.3 %all-to-all-start.1 = ((bf16[128,128,128]{2,1,0:T(8,128)(2,1)}), bf16[128,128,128]{2,1,0:T(8,128)(2,1)}, u32[]{:S(2)}, u32[]{:S(2)}) async-start(bf16[128,128,128]{2,1,0:T(8,128)(2,1)} %gather.1), calls=%async_computation.1 | async-start | bytes 8388608 | tf_op jit(solution)/shard_map/all_to_all | solution.py:562

commit v6 on v5

--- a/solution.py
+++ b/solution.py
@@ -145,70 +145,107 @@
     return jnp.where(number == cell_row, 1.0, 0.0).astype(BF)
 
 
-def splat_kernel(meta_all, message, out, tiles_out, even, odd, turned, tiles, sem):
-    step = pl.program_id(0)
-    sources, rows, channels = message.shape
-    bins = (rows - 8) // 2
-    cells = TS * TS
-
-    @pl.when(step == 0)
-    def _():
-        numbers = meta_all[:, 0:8, :].astype(F32)
-        flat = numbers[:, 1, :].T
-        turned[0:1, :] = flat[0:1].astype(jnp.int32)
-        turned[1:2, :] = flat[bins : bins + 1].astype(jnp.int32)
-        copy = pltpu.make_async_copy(turned, tiles, sem)
-        copy.start()
-        even[...] = jnp.zeros(even.shape, F32)
-        odd[...] = jnp.zeros(odd.shape, F32)
-        copy.wait()
-
-    def source(s, carry):
-        meta = message[s, pl.ds(2 * bins, 8), :].astype(jnp.int32)
-        hot = cell_onehot(meta[0:1], cells)
-        tile = [tiles[rank, step * sources + s] for rank in range(2)]
-        nothing = jnp.zeros((bins, channels), BF)
-        first = jnp.where(tile[0] < ABSENT, message[s, 0:bins, :], nothing)
-        second = jnp.where(tile[1] < ABSENT, message[s, bins : 2 * bins, :], nothing)
-        both = jnp.concatenate(
-            [
-                jnp.concatenate([first, nothing], axis=0),
-                jnp.concatenate([nothing, second], axis=0),
-            ],
-            axis=1,
-        )
-        sums = jnp.dot(hot, both, preferred_element_type=F32)
-        for rank, acc in enumerate((even, odd)):
-            here = jnp.minimum(tile[rank], acc.shape[1] // 8 - 1)
-            at = pl.ds(pl.multiple_of(here * 8, 8), 8)
-            part = sums[:, rank * channels : (rank + 1) * channels].reshape(TS, 2, 8, channels)
+def splat_kernel(
+    meta_all, message, out, tiles_out, acc, rows, cells, codes, numbers, group, group_tile, sems
+):
+    owners, _, channels = meta_all.shape
+    bins = channels // 2
+    tile_count = acc.shape[1] // 8
+    groups = group_tile.shape[0] - owners // 2
+    arrival = pltpu.make_async_copy(
+        message.at[:, pl.ds(0, 2 * bins), :], rows.at[pl.ds(0, owners)], sems.at[0]
+    )
+    arrival.start()
+    meta = meta_all[...].astype(F32)
+    cells[0:owners, :] = meta[:, 0, :].astype(jnp.int32)
+    cells[owners:, :] = jnp.full((8, channels), TS * TS, jnp.int32)
+    rows[owners] = jnp.zeros((2 * bins, channels), BF)
+    lane = lax.broadcasted_iota(jnp.int32, (owners, channels), 1)
+    line = lax.broadcasted_iota(jnp.int32, (owners, channels), 0)
+    named = meta[:, 1, :]
+    swapped = pltpu.roll(named, bins, 1)
+    across, place, amount = [], [], []
+    for rank in range(2):
+        down = jnp.where((lane < bins) == (rank == 0), named, swapped).astype(jnp.int32)
+        tile = down.T
+        earlier = (down == tile) & (line < lane)
+        across.append(tile)
+        place.append(jnp.sum(earlier.astype(jnp.int32), axis=0, keepdims=True))
+        amount.append(jnp.sum((line == tile).astype(jnp.int32), axis=1, keepdims=True))
+    needed = lax.shift_right_logical(jnp.maximum(amount[0], amount[1]) + 1, 1)
+    needed = jnp.where(line < tile_count, needed, 0)
+    for rank in range(2):
+        tile = across[rank][0:1]
+        base = jnp.sum(jnp.where(line < across[rank], needed, 0), axis=0, keepdims=True)
+        at = jnp.where(tile < tile_count, base, groups) + lax.shift_right_logical(place[rank], 1)
+        codes[rank : rank + 1, :] = 4 * at + 2 * rank + (place[rank] & 1)
+        codes[2 + rank : 3 + rank, :] = tile
+        tiles_out[rank : rank + 1, :] = jnp.minimum(tile, tile_count - 1)
+    codes[4:5, :] = jnp.sum(needed, axis=0, keepdims=True)
+    copy = pltpu.make_async_copy(codes, numbers, sems.at[1])
+    copy.start()
+    acc[...] = jnp.zeros(acc.shape, F32)
+    for i in range(4 * groups):
+        group[i] = owners
+    for i in range(groups):
+        group_tile[i] = 0
+    copy.wait()
+    total = numbers[4, 0]
+
+    def place_source(s, carry):
+        for rank in range(2):
+            at = numbers[rank, s]
+            group[at] = s
+            group_tile[lax.shift_right_logical(at, 2)] = numbers[2 + rank, s]
+        return carry
+
+    lax.fori_loop(0, owners, place_source, 0, unroll=16)
+    arrival.wait()
+    low = lax.broadcasted_iota(jnp.int32, (1, channels), 1) < bins
+
+    def batch(b, carry):
+        for q in range(8):
+            at = 8 * b + q
+            ids = [group[4 * at + slot] for slot in range(4)]
+            hot = [
+                cell_onehot(
+                    jnp.where(low, cells[pl.ds(ids[k], 1), :], cells[pl.ds(ids[2 + k], 1), :]),
+                    TS * TS,
+                )
+                for k in range(2)
+            ]
+            parts = []
+            for k in range(2):
+                parts += [rows[ids[k], 0:bins, :], rows[ids[2 + k], bins : 2 * bins, :]]
+            sums = jnp.dot(
+                jnp.concatenate(hot, axis=1),
+                jnp.concatenate(parts, axis=0),
+                preferred_element_type=F32,
+            ).reshape(TS, 2, 8, channels)
+            here = pl.ds(pl.multiple_of(group_tile[at] * 8, 8), 8)
             for side in range(2):
-                lanes = slice(side * channels, (side + 1) * channels)
-                acc[:, at, lanes] += part[:, side]
+                acc[:, here, side * channels : (side + 1) * channels] += sums[:, side]
         return carry
 
-    lax.fori_loop(0, sources, source, 0, unroll=8)
-
-    @pl.when(step == pl.num_programs(0) - 1)
-    def _():
-        out[...] = (even[...] + odd[...]).astype(BF)
-        tiles_out[...] = turned[...]
+    lax.fori_loop(0, lax.div(total + 7, 8), batch, 0)
+    out[...] = acc[...].astype(BF)
 
 
 def splat(message, rows, cols):
     owners, height, channels = message.shape
-    chunk = owners // 8
     shape = (rows, cols // 2, 2 * channels)
+    groups = owners + cols // TS
+    spare = groups + owners // 2
     return pl.pallas_call(
         splat_kernel,
         out_shape=(
             jax.ShapeDtypeStruct(shape, BF),
             jax.ShapeDtypeStruct((2, owners), jnp.int32),
         ),
-        grid=(owners // chunk,),
+        grid=(1,),
         in_specs=[
             pl.BlockSpec((owners, 8, channels), lambda i: (0, height // 8 - 1, 0)),
-            pl.BlockSpec((chunk, height, channels), lambda i: (i, 0, 0)),
+            pl.BlockSpec(memory_space=pltpu.HBM),
         ],
         out_specs=(
             pl.BlockSpec(shape, lambda i: (0, 0, 0)),
@@ -216,14 +253,17 @@
         ),
         scratch_shapes=[
             pltpu.VMEM(shape, F32),
-            pltpu.VMEM(shape, F32),
-            pltpu.VMEM((2, owners), jnp.int32),
-            pltpu.SMEM((2, owners), jnp.int32),
-            pltpu.SemaphoreType.DMA,
-        ],
-        compiler_params=pltpu.CompilerParams(vmem_limit_bytes=40 << 20),
+            pltpu.VMEM((owners + 1, height - 8, channels), BF),
+            pltpu.VMEM((owners + 8, channels), jnp.int32),
+            pltpu.VMEM((8, owners), jnp.int32),
+            pltpu.SMEM((8, owners), jnp.int32),
+            pltpu.SMEM((4 * spare,), jnp.int32),
+            pltpu.SMEM((spare,), jnp.int32),
+            pltpu.SemaphoreType.DMA((2,)),
+        ],
+        compiler_params=pltpu.CompilerParams(vmem_limit_bytes=24 << 20),
         name="splat",
-    )(message, message)
+    )(in_hbm(message), in_hbm(message))
 
 
 def chunks_of(count):
@@ -235,7 +275,7 @@
 def conv_kernel(
     edges, middle, above, below, left, right, corner_above, corner_below,
     cot_above, cot_below, cot_far, weights_far,
-    bev, grad, ping, pong, slopes, mask, sums, weights, cot, sems,
+    bev, grad, ping, pong, slopes, sums, weights, cot, sems,
 ):
     rows, mid, double = middle.shape
     channels = double // 2
@@ -253,10 +293,6 @@
     cot_arrival.start()
     for copy in arrivals[: LAYERS - 1 : -1]:
         copy.start()
-    column = lax.broadcasted_iota(jnp.int32, (wide, double), 0)
-    gone = ((column < PAIRS) & (edges[2] == 1)) | ((column >= wide - PAIRS) & (edges[3] == 1))
-    mask[0] = jnp.zeros((wide, double), F32)
-    mask[1] = jnp.where(gone, 0.0, 1.0)
 
     def put(ref, row, value):
         first = value[:, :channels]
@@ -304,11 +340,18 @@
             here = start + side
             row = layer + 1 + here
             inside = jnp.where(
-                ((row < EXT) & (edges[0] == 1)) | ((row >= EXT + rows) & (edges[1] == 1)), 0, 1
+                ((row < EXT) & (edges[0] == 1)) | ((row >= EXT + rows) & (edges[1] == 1)), 0.0, 1.0
             )
             part = sums[side]
-            flag = mask[inside]
-            twice = flag + flag * jnp.tanh(part)
+            twice = 1.0 + jnp.tanh(part)
+            twice = jnp.concatenate(
+                [
+                    twice[:PAIRS] * jnp.where(edges[2] == 1, 0.0, inside),
+                    twice[PAIRS : PAIRS + mid] * inside,
+                    twice[PAIRS + mid :] * jnp.where(edges[3] == 1, 0.0, inside),
+                ],
+                axis=0,
+            )
             active = part * twice
             slope = twice + active * (2.0 - twice)
             if layer < LAYERS - 1:
@@ -383,7 +426,6 @@
             buffer,
             buffer,
             pltpu.VMEM((kept, wide, double), F32),
-            pltpu.VMEM((2, wide, double), F32),
             pltpu.VMEM((7, wide, double), F32),
             pltpu.VMEM(weights.shape, BF),
             pltpu.VMEM((rows + 2 * LAYERS, wide, double), BF),
@@ -440,16 +482,26 @@
     blocks, bins, _ = depth.shape
     halves = blocks // 2
 
+    def fetch(first, group):
+        for b in range(blocks):
+            slot = slots[first + b]
+            pltpu.make_async_copy(
+                returned.at[
+                    lax.shift_right_logical(slot, 1),
+                    pl.ds(pl.multiple_of((slot & 1) * bins, bins), bins),
+                    :,
+                ],
+                fetched.at[group * halves + b // 2, pl.ds((b % 2) * bins, bins), :],
+                sems.at[group],
+            ).start()
+
     @pl.when(step == 0)
     def _():
-        for b in range(2 * fetched.shape[0]):
-            slot = slots[b]
-            start = pl.multiple_of(lax.rem(slot, 2) * bins, bins)
-            pltpu.make_async_copy(
-                returned.at[lax.div(slot, 2), pl.ds(start, bins), :],
-                fetched.at[b // 2, pl.ds((b % 2) * bins, bins), :],
-                sems.at[b // blocks],
-            ).start()
+        fetch(0, 0)
+
+    @pl.when(step + 1 < pl.num_programs(0))
+    def _():
+        fetch((step + 1) * blocks, step + 1)
 
     pltpu.make_async_copy(
         returned.at[pl.ds(0, halves)],

time: 212 us -> 210 us (level)
  Pallas kernels: 61.4 us -> 56.2 us
  starting transfers between devices: 47.1 us -> 50.1 us
    pallas_call x1, Pallas kernels: 10.6 us -> 5.47 us  [splat(): pl.pallas_call(splat_kernel, out_shape=(jax.ShapeDtypeStruct(shape, BF),...]
    ppermute x1, starting transfers between devices: 1.92 us -> 4.08 us  [per_device(): below = lax.ppermute(middle[:EXT], 'cam', up)]
  transfers between devices with their start and end apart: 12 -> 12, of which waited for: 5 -> 4; matrix products, arithmetic and copies ran while one was open for 7% -> 7% of each run, Pallas kernels for 5% -> 3%
where the time goes in v6:
time: 210 us; the launch traced here: 209 us
  waiting for transfers between devices  85.9 us (41%)
  Pallas kernels  56.2 us (27%)
  starting transfers between devices  50.1 us (24%)
  local copies, waits for them, and re-layouts  9.19 us (4%)
  other arithmetic  6.65 us (3%)
    all_to_all x1, waiting for transfers between devices, per_device(): lax.all_to_all(rows_back, axes, split_axis=0, concat_axis=0, tiled=True)  52 us
    pallas_call x1, Pallas kernels, convs(): pl.pallas_call(conv_kernel, out_shape=(jax.ShapeDtypeStruct((rows + 2 * L...  30.5 us
    ppermute x1, waiting for transfers between devices, per_device(): cot_left = lax.ppermute(cot[:, mid - PAIRS:], 'tile', east)  19.1 us
    all_to_all x1, starting transfers between devices, per_device(): lax.all_to_all(rows_back, axes, split_axis=0, concat_axis=0, tiled=True)  13.3 us
    all_to_all x1, waiting for transfers between devices, per_device(): lax.all_to_all(sent, axes, split_axis=0, concat_axis=0, tiled=True)  12.2 us
    all_to_all x1, starting transfers between devices, per_device(): lax.all_to_all(sent, axes, split_axis=0, concat_axis=0, tiled=True)  10.9 us
    pallas_call x1, Pallas kernels, gather(): pl.pallas_call(gather_kernel, out_shape=pltpu.HBM((owners, height - 8, ch...  7.53 us
    pallas_call x1, Pallas kernels, final(): pl.pallas_call(final_kernel, out_shape=(jax.ShapeDtypeStruct(depth.shape,...  6.64 us
  transfers between devices with their start and end apart: 12, of which 4 were waited for; matrix products, arithmetic and copies ran while one was open for 7% of the time, Pallas kernels for 3%

profile of v6, /device:TPU:6, one launch (start us, length us, event | category | flops | bytes accessed | tf_op | source)
XLA Modules:
  0.0 209.2 jit_solution(9826579544820497097)
XLA Ops:
  0.6 6.1 %pack.1 = (bf16[128,136,128]{2,1,0:T(8,128)(2,1)}, s32[64]{0:T(128)S(1)}) custom-call(s32[4,1,16]{2,1,0:T(1,128)} %bitcast.21, s32[4,16]{1,0:T(4,128)} %local.1, s32[4,16,64]{2,1,0:T(8,128)} %cells.1, bf16[64,64,128]{2,1,0:T(8,128)(2,1)} %bitcast.19, bf16[64,128,128]{2,1,0:T(8,128)(2,1)} %bitcast.17), custom_call_target="tpu_custom_call" | custom-call | tf_op jit(solution)/shard_map/pack/pallas_call | solution.py:113
  6.7 10.9 %all-to-all-start = ((bf16[128,136,128]{2,1,0:T(8,128)(2,1)}), bf16[128,136,128]{2,1,0:T(8,128)(2,1)}, u32[]{:S(2)}, u32[]{:S(2)}) async-start(bf16[128,136,128]{2,1,0:T(8,128)(2,1)} %get-tuple-element.11), calls=%async_computation | async-start | bytes 8912896 | tf_op jit(solution)/shard_map/all_to_all | solution.py:577
  17.8 2.2 %collective-permute-start.8 = (bf16[4,128,256]{2,1,0:T(8,128)(2,1)S(1)}, bf16[4,128,256]{2,1,0:T(8,128)(2,1)S(1)}, u32[]{:S(2)}, u32[]{:S(2)}) collective-permute-start(bf16[4,128,256]{2,1,0:T(8,128)(2,1)S(1)} %slice.56), channel_id=1, source_target_pairs={{0,16},{16,32},{32,48},{48,64},{64,80},{80,96},{96,112},{1,17},{17... | collective-permute-start | bytes 786440 | tf_op jit(solution)/shard_map/ppermute | solution.py:582
  20.0 3.5 %collective-permute-start.9 = (bf16[4,128,256]{2,1,0:T(8,128)(2,1)S(1)}, bf16[4,128,256]{2,1,0:T(8,128)(2,1)S(1)}, u32[]{:S(2)}, u32[]{:S(2)}) collective-permute-start(bf16[4,128,256]{2,1,0:T(8,128)(2,1)S(1)} %slice.58), channel_id=1, source_target_pairs={{16,0},{32,16},{48,32},{64,48},{80,64},{96,80},{112,96},{17,1},{33... | collective-permute-start | bytes 786440 | tf_op jit(solution)/shard_map/ppermute | solution.py:583
  23.6 1.4 reshape.34
  26.3 4.5 %collective-permute-start.4 = (bf16[16,8,256]{2,1,0:T(8,128)(2,1)S(1)}, bf16[16,8,256]{2,1,0:T(8,128)(2,1)S(1)}, u32[]{:S(2)}, u32[]{:S(2)}) collective-permute-start(bf16[16,8,256]{2,1,0:T(8,128)(2,1)S(1)} %get-tuple-element.22), channel_id=1, source_target_pairs={{0,1},{1,2},{2,3},{3,4},{4,5},{5,6},{6,7},{7,8},{8,9},{9,10},{10,1... | collective-permute-start | bytes 196616 | tf_op jit(solution)/shard_map/ppermute | solution.py:584
  31.0 1.8 fusion.4
  32.8 4.7 %copy.11 = bf16[4,3,4,128,256]{4,3,2,1,0:T(8,128)(2,1)} copy(bf16[4,3,4,128,256]{3,4,2,1,0:T(8,128)(2,1)} %fusion.4) | data formatting | bytes 6291456 | tf_op jit(solution)/shard_map/concatenate | solution.py:556
  38.0 1.4 copy-done
  39.4 3.2 %maximum_multiply_fusion.weights_far = bf16[8,1536,256]{2,1,0:T(8,128)(2,1)} fusion(bf16[4,1536,256]{2,1,0:T(8,128)(2,1)S(1)} %bitcast.15, bf16[4,1536,256]{2,1,0:T(8,128)(2,1)S(1)} %bitcast.16), kind=kLoop, calls=%fused_computation.4 | loop fusion | flops 6291456 | bytes 12582912 | tf_op jit(solution)/shard_map/mul | solution.py:589
  42.6 19.1 %collective-permute-done.4 = bf16[16,8,256]{2,1,0:T(8,128)(2,1)S(1)} collective-permute-done((bf16[16,8,256]{2,1,0:T(8,128)(2,1)S(1)}, bf16[16,8,256]{2,1,0:T(8,128)(2,1)S(1)}, u32[]{:S(2)}, u32[]{:S(2)}) %collective-permute-start.4) | collective-permute-done | bytes 65568 | tf_op jit(solution)/shard_map/ppermute | solution.py:584
  61.7 12.2 %all-to-all-done.meta_all.message = bf16[128,136,128]{2,1,0:T(8,128)(2,1)} async-done(((bf16[128,136,128]{2,1,0:T(8,128)(2,1)}), bf16[128,136,128]{2,1,0:T(8,128)(2,1)}, u32[]{:S(2)}, u32[]{:S(2)}) %all-to-all-start) | async-done | bytes 4456480 | tf_op jit(solution)/shard_map/all_to_all | solution.py:577
  73.9 5.5 %splat.1 = (bf16[16,128,256]{2,1,0:T(8,128)(2,1)S(1)}, s32[2,128]{1,0:T(2,128)S(1)}) custom-call(bf16[128,136,128]{2,1,0:T(8,128)(2,1)} %all-to-all-done.meta_all.message, bf16[128,136,128]{2,1,0:T(8,128)(2,1)} %all-to-all-done.meta_all.message), custom_call_target="tpu_custom_call" | custom-call | tf_op jit(solution)/shard_map/splat/pallas_call | solution.py:239
  79.4 1.3 collective-permute-start.2
  82.1 4.1 %collective-permute-start.1 = (bf16[8,128,256]{2,1,0:T(8,128)(2,1)S(1)}, bf16[8,128,256]{2,1,0:T(8,128)(2,1)S(1)}, u32[]{:S(2)}, u32[]{:S(2)}) collective-permute-start(bf16[8,128,256]{2,1,0:T(8,128)(2,1)S(1)} %get-tuple-element.25), channel_id=1, source_target_pairs={{16,0},{32,16},{48,32},{64,48},{80,64},{96,80},{112,96},{17,1},{33... | collective-permute-start | bytes 1572872 | tf_op jit(solution)/shard_map/ppermute | solution.py:599
  86.2 1.9 collective-permute-start
  88.2 1.9 collective-permute-start.6
  90.2 3.8 %collective-permute-start.7 = (bf16[12,16,256]{2,1,0:T(8,128)(2,1)S(1)}, bf16[12,16,256]{2,1,0:T(8,128)(2,1)S(1)}, u32[]{:S(2)}, u32[]{:S(2)}) collective-permute-start(bf16[12,16,256]{2,1,0:T(8,128)(2,1)S(1)} %pad_maximum_fusion.2), channel_id=1, source_target_pairs={{16,0},{32,16},{48,32},{64,48},{80,64},{96,80},{112,96},{17,1},{33... | collective-permute-start | bytes 294920 | tf_op jit(solution)/shard_map/ppermute | solution.py:607
  95.1 2.7 %collective-permute-done.6.corner_above = bf16[12,16,256]{2,1,0:T(8,128)(2,1)S(1)} collective-permute-done((bf16[12,16,256]{2,1,0:T(8,128)(2,1)S(1)}, bf16[12,16,256]{2,1,0:T(8,128)(2,1)S(1)}, u32[]{:S(2)}, u32[]{:S(2)}) %collective-permute-start.6) | collective-permute-done | bytes 98336 | tf_op jit(solution)/shard_map/ppermute | solution.py:606
  97.8 30.5 %convs.1 = (bf16[24,128,256]{2,1,0:T(8,128)(2,1)S(1)}, bf16[16,256,128]{2,1,0:T(8,128)(2,1)S(1)}) custom-call(s32[4]{0:T(128)S(1)} %add_convert_fusion.edges, bf16[16,128,256]{2,1,0:T(8,128)(2,1)S(1)} %get-tuple-element.12.middle, bf16[8,128,256]{2,1,0:T(8,128)(2,1)S(1)} %collective-permute-done.above, ...), custom_call_target="tpu_custom_call" | custom-call | tf_op jit(solution)/shard_map/convs/pallas_call | solution.py:417
  128.3 7.5 %gather.1 = bf16[128,128,128]{2,1,0:T(8,128)(2,1)} custom-call(s32[2,128]{1,0:T(2,128)S(1)} %get-tuple-element.15.tiles, bf16[128,136,128]{2,1,0:T(8,128)(2,1)} %all-to-all-done.meta_all.message, bf16[16,256,128]{2,1,0:T(8,128)(2,1)S(1)} %get-tuple-element.16.grad), custom_call_target="tpu_custom_call" | custom-call | tf_op jit(solution)/shard_map/gather/pallas_call | solution.py:464
  135.8 13.3 %all-to-all-start.1 = ((bf16[128,128,128]{2,1,0:T(8,128)(2,1)}), bf16[128,128,128]{2,1,0:T(8,128)(2,1)}, u32[]{:S(2)}, u32[]{:S(2)}) async-start(bf16[128,128,128]{2,1,0:T(8,128)(2,1)} %gather.1), calls=%async_computation.1 | async-start | bytes 8388608 | tf_op jit(solution)/shard_map/all_to_all | solution.py:614
  150.4 52.0 %all-to-all-done.1.returned = bf16[128,128,128]{2,1,0:T(8,128)(2,1)} async-done(((bf16[128,128,128]{2,1,0:T(8,128)(2,1)}), bf16[128,128,128]{2,1,0:T(8,128)(2,1)}, u32[]{:S(2)}, u32[]{:S(2)}) %all-to-all-start.1) | async-done | bytes 4194336 | tf_op jit(solution)/shard_map/all_to_all | solution.py:614
  202.4 6.6 %final.1 = (bf16[64,64,128]{2,1,0:T(8,128)(2,1)}, bf16[64,128,128]{2,1,0:T(8,128)(2,1)}) custom-call(s32[64]{0:T(128)S(1)} %get-tuple-element.14.slots, bf16[128,128,128]{2,1,0:T(8,128)(2,1)} %all-to-all-done.1.returned, bf16[64,64,128]{2,1,0:T(8,128)(2,1)} %bitcast.20, bf16[64,128,128]{2,1,0:T(8,128)(2,1)} %bitcast.18), custom_call_target="tpu_custom_call" | custom-call | tf_op jit(solution)/shard_map/final/pallas_call | solution.py:529
  (35 shorter events, 6.0 us)
Async XLA Ops:
  6.7 10.9 %copy-start.2 = (bf16[16,256,128]{2,1,0:T(8,128)(2,1)S(1)}, bf16[16,256,128]{2,1,0:T(8,128)(2,1)}, u32[]{:S(2)}) copy-start(bf16[16,256,128]{2,1,0:T(8,128)(2,1)} %param.13) | copy-start | bytes 3145732
  6.7 67.2 %all-to-all-start = ((bf16[128,136,128]{2,1,0:T(8,128)(2,1)}), bf16[128,136,128]{2,1,0:T(8,128)(2,1)}, u32[]{:S(2)}, u32[]{:S(2)}) async-start(bf16[128,136,128]{2,1,0:T(8,128)(2,1)} %get-tuple-element.11), calls=%async_computation | async-start | bytes 8912896 | tf_op jit(solution)/shard_map/all_to_all | solution.py:577
  17.6 13.3 %copy-start.1 = (bf16[4,3,3,128,128]{4,3,2,1,0:T(8,128)(2,1)S(1)}, bf16[4,3,3,128,128]{4,3,2,1,0:T(8,128)(2,1)}, u32[]{:S(2)}) copy-start(bf16[4,3,3,128,128]{4,3,2,1,0:T(8,128)(2,1)} %param.12) | copy-start | bytes 3538948
  17.8 72.4 %collective-permute-start.8 = (bf16[4,128,256]{2,1,0:T(8,128)(2,1)S(1)}, bf16[4,128,256]{2,1,0:T(8,128)(2,1)S(1)}, u32[]{:S(2)}, u32[]{:S(2)}) collective-permute-start(bf16[4,128,256]{2,1,0:T(8,128)(2,1)S(1)} %slice.56), channel_id=1, source_target_pairs={{0,16},{16,32},{32,48},{48,64},{64,80},{80,96},{96,112},{1,17},{17... | collective-permute-start | bytes 786440 | tf_op jit(solution)/shard_map/ppermute | solution.py:582
  20.0 75.1 %collective-permute-start.9 = (bf16[4,128,256]{2,1,0:T(8,128)(2,1)S(1)}, bf16[4,128,256]{2,1,0:T(8,128)(2,1)S(1)}, u32[]{:S(2)}, u32[]{:S(2)}) collective-permute-start(bf16[4,128,256]{2,1,0:T(8,128)(2,1)S(1)} %slice.58), channel_id=1, source_target_pairs={{16,0},{32,16},{48,32},{64,48},{80,64},{96,80},{112,96},{17,1},{33... | collective-permute-start | bytes 786440 | tf_op jit(solution)/shard_map/ppermute | solution.py:583
  25.0 36.7 %collective-permute-start.5 = (bf16[16,8,256]{2,1,0:T(8,128)(2,1)S(1)}, bf16[16,8,256]{2,1,0:T(8,128)(2,1)S(1)}, u32[]{:S(2)}, u32[]{:S(2)}) collective-permute-start(bf16[16,8,256]{2,1,0:T(8,128)(2,1)S(1)} %get-tuple-element.21), channel_id=1, source_target_pairs={{1,0},{2,1},{3,2},{4,3},{5,4},{6,5},{7,6},{8,7},{9,8},{10,9},{11,1... | collective-permute-start | bytes 196616 | tf_op jit(solution)/shard_map/ppermute | solution.py:585
  26.3 35.4 %collective-permute-start.4 = (bf16[16,8,256]{2,1,0:T(8,128)(2,1)S(1)}, bf16[16,8,256]{2,1,0:T(8,128)(2,1)S(1)}, u32[]{:S(2)}, u32[]{:S(2)}) collective-permute-start(bf16[16,8,256]{2,1,0:T(8,128)(2,1)S(1)} %get-tuple-element.22), channel_id=1, source_target_pairs={{0,1},{1,2},{2,3},{3,4},{4,5},{5,6},{6,7},{7,8},{8,9},{9,10},{10,1... | collective-permute-start | bytes 196616 | tf_op jit(solution)/shard_map/ppermute | solution.py:584
  37.5 1.9 copy-start
  79.4 6.8 %collective-permute-start.2 = (bf16[16,8,256]{2,1,0:T(8,128)(2,1)S(1)}, bf16[16,8,256]{2,1,0:T(8,128)(2,1)S(1)}, u32[]{:S(2)}, u32[]{:S(2)}) collective-permute-start(bf16[16,8,256]{2,1,0:T(8,128)(2,1)S(1)} %get-tuple-element.24), channel_id=1, source_target_pairs={{0,1},{1,2},{2,3},{3,4},{4,5},{5,6},{6,7},{7,8},{8,9},{9,10},{10,1... | collective-permute-start | bytes 196616 | tf_op jit(solution)/shard_map/ppermute | solution.py:600
  80.8 7.3 %collective-permute-start.3 = (bf16[16,8,256]{2,1,0:T(8,128)(2,1)S(1)}, bf16[16,8,256]{2,1,0:T(8,128)(2,1)S(1)}, u32[]{:S(2)}, u32[]{:S(2)}) collective-permute-start(bf16[16,8,256]{2,1,0:T(8,128)(2,1)S(1)} %get-tuple-element.23), channel_id=1, source_target_pairs={{1,0},{2,1},{3,2},{4,3},{5,4},{6,5},{7,6},{8,7},{9,8},{10,9},{11,1... | collective-permute-start | bytes 196616 | tf_op jit(solution)/shard_map/ppermute | solution.py:601
  82.1 15.7 %collective-permute-start.1 = (bf16[8,128,256]{2,1,0:T(8,128)(2,1)S(1)}, bf16[8,128,256]{2,1,0:T(8,128)(2,1)S(1)}, u32[]{:S(2)}, u32[]{:S(2)}) collective-permute-start(bf16[8,128,256]{2,1,0:T(8,128)(2,1)S(1)} %get-tuple-element.25), channel_id=1, source_target_pairs={{16,0},{32,16},{48,32},{64,48},{80,64},{96,80},{112,96},{17,1},{33... | collective-permute-start | bytes 1572872 | tf_op jit(solution)/shard_map/ppermute | solution.py:599
  86.2 11.6 %collective-permute-start = (bf16[8,128,256]{2,1,0:T(8,128)(2,1)S(1)}, bf16[8,128,256]{2,1,0:T(8,128)(2,1)S(1)}, u32[]{:S(2)}, u32[]{:S(2)}) collective-permute-start(bf16[8,128,256]{2,1,0:T(8,128)(2,1)S(1)} %get-tuple-element.26), channel_id=1, source_target_pairs={{0,16},{16,32},{32,48},{48,64},{64,80},{80,96},{96,112},{1,17},{17... | collective-permute-start | bytes 1572872 | tf_op jit(solution)/shard_map/ppermute | solution.py:598
  88.2 9.5 %collective-permute-start.6 = (bf16[12,16,256]{2,1,0:T(8,128)(2,1)S(1)}, bf16[12,16,256]{2,1,0:T(8,128)(2,1)S(1)}, u32[]{:S(2)}, u32[]{:S(2)}) collective-permute-start(bf16[12,16,256]{2,1,0:T(8,128)(2,1)S(1)} %pad_maximum_fusion.1), channel_id=1, source_target_pairs={{0,16},{16,32},{32,48},{48,64},{64,80},{80,96},{96,112},{1,17},{17... | collective-permute-start | bytes 294920 | tf_op jit(solution)/shard_map/ppermute | solution.py:606
  90.2 7.6 %collective-permute-start.7 = (bf16[12,16,256]{2,1,0:T(8,128)(2,1)S(1)}, bf16[12,16,256]{2,1,0:T(8,128)(2,1)S(1)}, u32[]{:S(2)}, u32[]{:S(2)}) collective-permute-start(bf16[12,16,256]{2,1,0:T(8,128)(2,1)S(1)} %pad_maximum_fusion.2), channel_id=1, source_target_pairs={{16,0},{32,16},{48,32},{64,48},{80,64},{96,80},{112,96},{17,1},{33... | collective-permute-start | bytes 294920 | tf_op jit(solution)/shard_map/ppermute | solution.py:607
  135.8 66.6 %all-to-all-start.1 = ((bf16[128,128,128]{2,1,0:T(8,128)(2,1)}), bf16[128,128,128]{2,1,0:T(8,128)(2,1)}, u32[]{:S(2)}, u32[]{:S(2)}) async-start(bf16[128,128,128]{2,1,0:T(8,128)(2,1)} %gather.1), calls=%async_computation.1 | async-start | bytes 8388608 | tf_op jit(solution)/shard_map/all_to_all | solution.py:614

commit v7 on v6

--- a/solution.py
+++ b/solution.py
@@ -11,6 +11,8 @@
 LAYERS = 4
 EXT = 2 * LAYERS
 PAIRS = 8
+PARTS = 4
+CHUNK = 16
 EMPTY = 256.0
 ABSENT = 255
 BF = jnp.bfloat16
@@ -50,90 +52,91 @@
 
 
 def pack_kernel(
-    owner, local, cells, depth, context, out, slots, count, wide, lifted, meta, sems
+    owner, local, cells, depth_far, context_far, out, slots,
+    count, depth, context, wide, lifted, meta, small, sems,
 ):
-    step = pl.program_id(0)
     blocks, bins, _ = depth.shape
     owners = out.shape[0]
-
-    @pl.when(step == 0)
-    def _():
-        clear_counts(count, owners)
-        kind = lax.broadcasted_iota(jnp.int32, meta.shape, 1)
-        meta[...] = jnp.where(kind == 0, EMPTY, ABSENT)
-        numbers = pair_cells(cells[...]).astype(F32).reshape(wide.shape[0], bins)
-        wide[...] = jnp.concatenate([numbers, numbers], axis=1)
-
+    chunk = blocks // PARTS
+    arrivals = []
+    for part in range(PARTS):
+        here = pl.ds(part * chunk, chunk)
+        for k, (far, near) in enumerate(((depth_far, depth), (context_far, context))):
+            copy = pltpu.make_async_copy(far.at[here], near.at[here], sems.at[2 * part + k])
+            copy.start()
+            arrivals.append(copy)
+    clear_counts(count, owners)
+    kind = lax.broadcasted_iota(jnp.int32, meta.shape, 1)
+    meta[...] = jnp.where(kind == 0, EMPTY, ABSENT)
+    numbers = pair_cells(cells[...]).astype(F32).reshape(blocks, bins)
+    wide[...] = jnp.concatenate([numbers, numbers], axis=1)
     lane = lax.broadcasted_iota(jnp.int32, (1, 2 * bins), 1)
-
-    def block(b, carry):
-        at = step * blocks + b
-        to = owner_of(owner, at)
-        each = local.shape[1]
-        tile = local[lax.div(at, each), lax.rem(at, each)].astype(F32)
+    each = local.shape[1]
+
+    def describe(b, carry):
+        to = owner_of(owner, b)
+        tile = local[lax.div(b, each), lax.rem(b, each)].astype(F32)
         rank = take_slot(to, count)
-        slots[at] = 2 * to + rank
-        product = jnp.dot(depth[b], context[b], preferred_element_type=F32)
-        lifted[lax.div(at, 2), pl.ds(pl.multiple_of(lax.rem(at, 2) * bins, bins), bins), :] = product.astype(BF)
+        slots[b] = 2 * to + rank
         mine = (lane // bins) == rank
-        row = wide[pl.ds(at, 1), :]
+        row = wide[pl.ds(b, 1), :]
         meta[to, pl.ds(0, 1), :] = jnp.where(mine, row, meta[to, pl.ds(0, 1), :])
         meta[to, pl.ds(1, 1), :] = jnp.where(mine, tile, meta[to, pl.ds(1, 1), :])
-        pltpu.make_async_copy(
-            lifted.at[lax.div(at, 2), pl.ds(pl.multiple_of(lax.rem(at, 2) * bins, bins), bins), :],
-            out.at[to, pl.ds(pl.multiple_of(rank * bins, bins), bins), :],
-            sems.at[0],
-        ).start()
         return carry
 
-    lax.fori_loop(0, blocks, block, 0, unroll=4)
-
-    @pl.when(step == pl.num_programs(0) - 1)
-    def _():
-        wide_meta = lifted.shape[0]
-
-        def put_meta(small):
-            small[...] = meta[...].astype(BF)
-            copy = pltpu.make_async_copy(
-                small, out.at[:, pl.ds(2 * bins, 8), :], sems.at[1]
-            )
-            copy.start()
+    lax.fori_loop(0, blocks, describe, 0, unroll=8)
+    small[...] = meta[...].astype(BF)
+    meta_copy = pltpu.make_async_copy(
+        small, out.at[:, pl.ds(2 * bins, 8), :], sems.at[2 * PARTS]
+    )
+    meta_copy.start()
+
+    for part in range(PARTS):
+        for copy in arrivals[2 * part : 2 * part + 2]:
             copy.wait()
-
-        pl.run_scoped(put_meta, pltpu.VMEM(meta.shape, BF))
-        pltpu.make_async_copy(
-            lifted, out.at[pl.ds(0, wide_meta), pl.ds(0, 2 * bins), :], sems.at[0]
-        ).wait()
+        for b in range(part * chunk, (part + 1) * chunk):
+            product = jnp.dot(depth[b], context[b], preferred_element_type=F32)
+            half = pl.ds((b % 2) * bins, bins)
+            lifted[b // 2, half, :] = product.astype(BF)
+        for b in range(part * chunk, (part + 1) * chunk):
+            slot = slots[b]
+            pltpu.make_async_copy(
+                lifted.at[b // 2, pl.ds((b % 2) * bins, bins), :],
+                out.at[
+                    lax.shift_right_logical(slot, 1),
+                    pl.ds(pl.multiple_of((slot & 1) * bins, bins), bins),
+                    :,
+                ],
+                sems.at[2 * PARTS + 1],
+            ).start()
+    meta_copy.wait()
+    pltpu.make_async_copy(
+        lifted, out.at[pl.ds(0, blocks // 2), pl.ds(0, 2 * bins), :], sems.at[2 * PARTS + 1]
+    ).wait()
 
 
 def pack(owner, local, cells, depth, context, owners):
-    blocks, bins, pixels = depth.shape
+    blocks, bins, _ = depth.shape
     channels = context.shape[2]
-    chunk = blocks // 4
+    smem = pl.BlockSpec(memory_space=pltpu.SMEM)
+    hbm = pl.BlockSpec(memory_space=pltpu.HBM)
     return pl.pallas_call(
         pack_kernel,
         out_shape=(
             pltpu.HBM((owners, 2 * bins + 8, channels), BF),
             jax.ShapeDtypeStruct((blocks,), jnp.int32),
         ),
-        grid=(blocks // chunk,),
-        in_specs=[
-            pl.BlockSpec(memory_space=pltpu.SMEM),
-            pl.BlockSpec(memory_space=pltpu.SMEM),
-            pl.BlockSpec(cells.shape, lambda i: (0, 0, 0)),
-            pl.BlockSpec((chunk, bins, pixels), lambda i: (i, 0, 0)),
-            pl.BlockSpec((chunk, pixels, channels), lambda i: (i, 0, 0)),
-        ],
-        out_specs=(
-            pl.BlockSpec(memory_space=pltpu.HBM),
-            pl.BlockSpec(memory_space=pltpu.SMEM),
-        ),
+        in_specs=[smem, smem, pl.BlockSpec(memory_space=pltpu.VMEM), hbm, hbm],
+        out_specs=(hbm, smem),
         scratch_shapes=[
             pltpu.SMEM((owners,), jnp.int32),
+            pltpu.VMEM(depth.shape, BF),
+            pltpu.VMEM(context.shape, BF),
             pltpu.VMEM((blocks, 2 * bins), F32),
             pltpu.VMEM((blocks // 2, 2 * bins, channels), BF),
             pltpu.VMEM((owners, 8, 2 * bins), F32),
-            pltpu.SemaphoreType.DMA((2,)),
+            pltpu.VMEM((owners, 8, 2 * bins), BF),
+            pltpu.SemaphoreType.DMA((2 * PARTS + 2,)),
         ],
         compiler_params=pltpu.CompilerParams(vmem_limit_bytes=24 << 20),
         name="pack",
@@ -274,8 +277,8 @@
 
 def conv_kernel(
     edges, middle, above, below, left, right, corner_above, corner_below,
-    cot_above, cot_below, cot_far, weights_far,
-    bev, grad, ping, pong, slopes, sums, weights, cot, sems,
+    cot_above, cot_below, tiles, meta_far, cot_far, weights_far,
+    bev_far, back_far, ping, pong, slopes, sums, weights, cot, bev, grad, back, meta, columns, sems,
 ):
     rows, mid, double = middle.shape
     channels = double // 2
@@ -288,9 +291,14 @@
     cot_arrival = pltpu.make_async_copy(
         cot_far, cot.at[pl.ds(LAYERS, rows)], sems.at[2 * LAYERS]
     )
+    slots = back.shape[1]
+    meta_arrival = pltpu.make_async_copy(
+        meta_far.at[:, pl.ds(slots, 8), :], meta, sems.at[2 * LAYERS + 1]
+    )
     for copy in arrivals[:LAYERS]:
         copy.start()
     cot_arrival.start()
+    meta_arrival.start()
     for copy in arrivals[: LAYERS - 1 : -1]:
         copy.start()
 
@@ -402,26 +410,59 @@
         lax.fori_loop(1, len(starts), steady, 0)
         finish = functools.partial(epilogue, target, starts[-1], size)
         source, target = target, source
+        if index == 2 * LAYERS - 1:
+            bev_copy = pltpu.make_async_copy(
+                bev.at[pl.ds(LAYERS, rows)], bev_far, sems.at[2 * LAYERS + 2]
+            )
+            bev_copy.start()
+            meta_arrival.wait()
+            columns[...] = meta[...].astype(F32)[:, 0, :].T.astype(jnp.int32)
     finish()
 
-
-def convs(edges, weights, cot, *fields):
+    owners = back.shape[0]
+    bins = slots // 2
+    _, cells, _ = grad.shape
+    number = lax.broadcasted_iota(jnp.int32, (slots, cells), 1)
+
+    def answer(chunk, carry):
+        first = chunk * CHUNK
+        mine = pltpu.roll(columns[...], lax.rem(owners - first, owners), 1)
+        for s in range(CHUNK):
+            hot = jnp.where(mine[:, s : s + 1] == number, 1.0, 0.0).astype(BF)
+            both = jnp.concatenate(
+                [grad[tiles[0, first + s]], grad[tiles[1, first + s]]], axis=1
+            )
+            picked = jnp.dot(hot, both, preferred_element_type=F32)
+            back[first + s, 0:bins, :] = picked[:bins, :channels].astype(BF)
+            back[first + s, bins:, :] = picked[bins:, channels:].astype(BF)
+        here = pl.ds(pl.multiple_of(first, CHUNK), CHUNK)
+        pltpu.make_async_copy(back.at[here], back_far.at[here], sems.at[2 * LAYERS + 3]).start()
+        return carry
+
+    lax.fori_loop(0, owners // CHUNK, answer, 0)
+    bev_copy.wait()
+    pltpu.make_async_copy(back, back_far, sems.at[2 * LAYERS + 3]).wait()
+
+
+def convs(edges, tiles, message, cot, weights, *fields):
     middle = fields[0]
     rows, mid, double = middle.shape
     wide = mid + 2 * PAIRS
     tall = rows + 2 * EXT
+    owners, height, channels = message.shape
     kept = sum(tall - 2 - 2 * layer for layer in range(LAYERS - 1))
     vmem = pl.BlockSpec(memory_space=pltpu.VMEM)
+    smem = pl.BlockSpec(memory_space=pltpu.SMEM)
     hbm = pl.BlockSpec(memory_space=pltpu.HBM)
     buffer = pltpu.VMEM((tall, wide, 2 * double), BF)
     return pl.pallas_call(
         conv_kernel,
         out_shape=(
-            jax.ShapeDtypeStruct((rows + 2 * LAYERS, mid, double), BF),
-            jax.ShapeDtypeStruct((mid // 8, rows * TS, double // 2), BF),
+            pltpu.HBM(middle.shape, BF),
+            pltpu.HBM((owners, height - 8, channels), BF),
         ),
-        in_specs=[pl.BlockSpec(memory_space=pltpu.SMEM)] + [vmem] * len(fields) + [hbm] * 2,
-        out_specs=(vmem, vmem),
+        in_specs=[smem] + [vmem] * len(fields) + [smem] + [hbm] * 3,
+        out_specs=(hbm, hbm),
         scratch_shapes=[
             buffer,
             buffer,
@@ -429,52 +470,16 @@
             pltpu.VMEM((7, wide, double), F32),
             pltpu.VMEM(weights.shape, BF),
             pltpu.VMEM((rows + 2 * LAYERS, wide, double), BF),
-            pltpu.SemaphoreType.DMA((2 * LAYERS + 1,)),
+            pltpu.VMEM((rows + 2 * LAYERS, mid, double), BF),
+            pltpu.VMEM((mid // 8, rows * TS, channels), BF),
+            pltpu.VMEM((owners, height - 8, channels), BF),
+            pltpu.VMEM((owners, 8, channels), BF),
+            pltpu.VMEM((height - 8, owners), jnp.int32),
+            pltpu.SemaphoreType.DMA((2 * LAYERS + 4,)),
         ],
-        compiler_params=pltpu.CompilerParams(vmem_limit_bytes=48 << 20),
+        compiler_params=pltpu.CompilerParams(vmem_limit_bytes=50 << 20),
         name="convs",
-    )(edges, *fields, in_hbm(cot), in_hbm(weights))
-
-
-def gather_kernel(tiles, meta_all, grad, out, columns):
-    step = pl.program_id(0)
-    owners = meta_all.shape[0]
-    sources, slots, channels = out.shape
-    bins = slots // 2
-    count, cells, _ = grad.shape
-
-    @pl.when(step == 0)
-    def _():
-        columns[...] = meta_all[...].astype(F32)[:, 0, :].T.astype(jnp.int32)
-
-    mine = pltpu.roll(columns[...], lax.rem(owners - step * sources, owners), 1)
-    number = lax.broadcasted_iota(jnp.int32, (slots, cells), 1)
-    for s in range(sources):
-        hot = jnp.where(mine[:, s : s + 1] == number, 1.0, 0.0).astype(BF)
-        here = [jnp.minimum(tiles[rank, step * sources + s], count - 1) for rank in range(2)]
-        both = jnp.concatenate([grad[here[0]], grad[here[1]]], axis=1)
-        picked = jnp.dot(hot, both, preferred_element_type=F32)
-        out[s, 0:bins, :] = picked[:bins, :channels].astype(BF)
-        out[s, bins:, :] = picked[bins:, channels:].astype(BF)
-
-
-def gather(tiles, message, grad):
-    owners, height, channels = message.shape
-    chunk = owners // 8
-    return pl.pallas_call(
-        gather_kernel,
-        out_shape=pltpu.HBM((owners, height - 8, channels), BF),
-        grid=(owners // chunk,),
-        in_specs=[
-            pl.BlockSpec(memory_space=pltpu.SMEM),
-            pl.BlockSpec((owners, 8, channels), lambda i: (0, height // 8 - 1, 0)),
-            pl.BlockSpec(grad.shape, lambda i: (0, 0, 0)),
-        ],
-        out_specs=pl.BlockSpec((chunk, height - 8, channels), lambda i: (i, 0, 0)),
-        scratch_shapes=[pltpu.VMEM((height - 8, owners), jnp.int32)],
-        compiler_params=pltpu.CompilerParams(vmem_limit_bytes=24 << 20),
-        name="gather",
-    )(tiles, message, grad)
+    )(edges, *fields, tiles, in_hbm(message), in_hbm(cot), in_hbm(weights))
 
 
 def final_kernel(slots, returned, depth, context, grad_depth, grad_context, fetched, sems):
@@ -606,15 +611,14 @@
     corner_above = lax.ppermute(lower, "cam", down)
     corner_below = lax.ppermute(upper, "cam", up)
 
-    bev, grad = convs(
-        edges, weights, cot_middle, middle, above, below, left, right, corner_above,
+    bev, rows_back = convs(
+        edges, tiles, message, cot_middle, weights, middle, above, below, left, right, corner_above,
         corner_below, cot_above, cot_below,
     )
-    rows_back = gather(tiles, message, grad)
     returned = lax.all_to_all(rows_back, axes, split_axis=0, concat_axis=0, tiled=True)
-    grad_depth, grad_context = final(slots, returned, in_hbm(depth), in_hbm(flat_context))
+    grad_depth, grad_context = final(slots, returned, depth, flat_context)
     return (
-        bev[LAYERS : LAYERS + rows].reshape(cotangent.shape),
+        bev.reshape(cotangent.shape),
         grad_depth.reshape(depth_weights.shape),
         grad_context.reshape(context.shape),
     )

time: 210 us -> 206 us (0.981)
  Pallas kernels: 56.2 us -> 51.5 us
    pallas_call x2 -> x1, Pallas kernels: 38 us -> 36.1 us  [convs(): pl.pallas_call(conv_kernel, out_shape=(pltpu.HBM(middle.shape, BF), pltpu...]
  transfers between devices with their start and end apart: 12 -> 12, of which waited for: 4 -> 4; matrix products, arithmetic and copies ran while one was open for 7% -> 8% of each run, Pallas kernels for 3% -> 3%
where the time goes in v7:
time: 206 us; the launch traced here: 205 us
  waiting for transfers between devices  84.2 us (41%)
  Pallas kernels  51.5 us (25%)
  starting transfers between devices  50 us (24%)
  local copies, waits for them, and re-layouts  11 us (5%)
  other arithmetic  6.73 us (3%)
    all_to_all x1, waiting for transfers between devices, per_device(): lax.all_to_all(rows_back, axes, split_axis=0, concat_axis=0, tiled=True)  50.9 us
    pallas_call x1, Pallas kernels, convs(): pl.pallas_call(conv_kernel, out_shape=(pltpu.HBM(middle.shape, BF), pltpu...  36.1 us
    ppermute x1, waiting for transfers between devices, per_device(): cot_left = lax.ppermute(cot[:, mid - PAIRS:], 'tile', east)  18.4 us
    all_to_all x1, starting transfers between devices, per_device(): lax.all_to_all(rows_back, axes, split_axis=0, concat_axis=0, tiled=True)  13.4 us
    all_to_all x1, waiting for transfers between devices, per_device(): lax.all_to_all(sent, axes, split_axis=0, concat_axis=0, tiled=True)  12.2 us
    all_to_all x1, starting transfers between devices, per_device(): lax.all_to_all(sent, axes, split_axis=0, concat_axis=0, tiled=True)  10.9 us
    pallas_call x1, Pallas kernels, final(): pl.pallas_call(final_kernel, out_shape=(jax.ShapeDtypeStruct(depth.shape,...  5.54 us
    pallas_call x1, Pallas kernels, splat(): pl.pallas_call(splat_kernel, out_shape=(jax.ShapeDtypeStruct(shape, BF),...  5.47 us
  transfers between devices with their start and end apart: 12, of which 4 were waited for; matrix products, arithmetic and copies ran while one was open for 8% of the time, Pallas kernels for 3%

profile of v7, /device:TPU:6, one launch (start us, length us, event | category | flops | bytes accessed | tf_op | source)
XLA Modules:
  0.0 204.6 jit_solution(15940005251054929382)
XLA Ops:
  0.6 4.4 %pack.1 = (bf16[128,136,128]{2,1,0:T(8,128)(2,1)}, s32[64]{0:T(128)S(1)}) custom-call(s32[4,1,16]{2,1,0:T(1,128)} %bitcast.21, s32[4,16]{1,0:T(4,128)} %local.1, s32[4,16,64]{2,1,0:T(8,128)} %cells.1, bf16[64,64,128]{2,1,0:T(8,128)(2,1)} %bitcast.17, bf16[64,128,128]{2,1,0:T(8,128)(2,1)} %bitcast.15), custom_call_target="tpu_custom_call" | custom-call | tf_op jit(solution)/shard_map/pack/pallas_call | solution.py:123
  5.1 10.9 %all-to-all-start = ((bf16[128,136,128]{2,1,0:T(8,128)(2,1)}), bf16[128,136,128]{2,1,0:T(8,128)(2,1)}, u32[]{:S(2)}, u32[]{:S(2)}) async-start(bf16[128,136,128]{2,1,0:T(8,128)(2,1)} %get-tuple-element.11), calls=%async_computation | async-start | bytes 8912896 | tf_op jit(solution)/shard_map/all_to_all | solution.py:582
  16.9 2.0 collective-permute-start.8
  19.0 3.5 %collective-permute-start.9 = (bf16[4,128,256]{2,1,0:T(8,128)(2,1)S(1)}, bf16[4,128,256]{2,1,0:T(8,128)(2,1)S(1)}, u32[]{:S(2)}, u32[]{:S(2)}) collective-permute-start(bf16[4,128,256]{2,1,0:T(8,128)(2,1)S(1)} %slice.55), channel_id=1, source_target_pairs={{16,0},{32,16},{48,32},{64,48},{80,64},{96,80},{112,96},{17,1},{33... | collective-permute-start | bytes 786440 | tf_op jit(solution)/shard_map/ppermute | solution.py:588
  22.5 1.4 reshape.34
  25.3 4.5 %collective-permute-start.4 = (bf16[16,8,256]{2,1,0:T(8,128)(2,1)S(1)}, bf16[16,8,256]{2,1,0:T(8,128)(2,1)S(1)}, u32[]{:S(2)}, u32[]{:S(2)}) collective-permute-start(bf16[16,8,256]{2,1,0:T(8,128)(2,1)S(1)} %get-tuple-element.22), channel_id=1, source_target_pairs={{0,1},{1,2},{2,3},{3,4},{4,5},{5,6},{6,7},{7,8},{8,9},{9,10},{10,1... | collective-permute-start | bytes 196616 | tf_op jit(solution)/shard_map/ppermute | solution.py:589
  30.0 1.8 fusion.4
  31.8 4.7 %copy.11 = bf16[4,3,4,128,256]{4,3,2,1,0:T(8,128)(2,1)} copy(bf16[4,3,4,128,256]{3,4,2,1,0:T(8,128)(2,1)} %fusion.4) | data formatting | bytes 6291456 | tf_op jit(solution)/shard_map/concatenate | solution.py:561
  36.9 1.4 copy-done.2
  38.3 3.2 %maximum_multiply_fusion.weights_far = bf16[8,1536,256]{2,1,0:T(8,128)(2,1)} fusion(bf16[4,1536,256]{2,1,0:T(8,128)(2,1)S(1)} %bitcast.19, bf16[4,1536,256]{2,1,0:T(8,128)(2,1)S(1)} %bitcast.20), kind=kLoop, calls=%fused_computation.4 | loop fusion | flops 6291456 | bytes 12582912 | tf_op jit(solution)/shard_map/mul | solution.py:594
  41.6 18.4 %collective-permute-done.4 = bf16[16,8,256]{2,1,0:T(8,128)(2,1)S(1)} collective-permute-done((bf16[16,8,256]{2,1,0:T(8,128)(2,1)S(1)}, bf16[16,8,256]{2,1,0:T(8,128)(2,1)S(1)}, u32[]{:S(2)}, u32[]{:S(2)}) %collective-permute-start.4) | collective-permute-done | bytes 65568 | tf_op jit(solution)/shard_map/ppermute | solution.py:589
  60.1 12.2 %all-to-all-done.meta_all.message.meta_far = bf16[128,136,128]{2,1,0:T(8,128)(2,1)} async-done(((bf16[128,136,128]{2,1,0:T(8,128)(2,1)}), bf16[128,136,128]{2,1,0:T(8,128)(2,1)}, u32[]{:S(2)}, u32[]{:S(2)}) %all-to-all-start) | async-done | bytes 4456480 | tf_op jit(solution)/shard_map/all_to_all | solution.py:582
  72.3 5.5 %splat.1 = (bf16[16,128,256]{2,1,0:T(8,128)(2,1)S(1)}, s32[2,128]{1,0:T(2,128)S(1)}) custom-call(bf16[128,136,128]{2,1,0:T(8,128)(2,1)} %all-to-all-done.meta_all.message.meta_far, bf16[128,136,128]{2,1,0:T(8,128)(2,1)} %all-to-all-done.meta_all.message.meta_far), custom_call_target="tpu_custom_call" | custom-call | tf_op jit(solution)/shard_map/splat/pallas_call | solution.py:242
  77.8 1.3 collective-permute-start.2
  80.5 4.1 %collective-permute-start.1 = (bf16[8,128,256]{2,1,0:T(8,128)(2,1)S(1)}, bf16[8,128,256]{2,1,0:T(8,128)(2,1)S(1)}, u32[]{:S(2)}, u32[]{:S(2)}) collective-permute-start(bf16[8,128,256]{2,1,0:T(8,128)(2,1)S(1)} %get-tuple-element.25), channel_id=1, source_target_pairs={{16,0},{32,16},{48,32},{64,48},{80,64},{96,80},{112,96},{17,1},{33... | collective-permute-start | bytes 1572872 | tf_op jit(solution)/shard_map/ppermute | solution.py:604
  84.6 1.9 collective-permute-start
  86.6 1.9 collective-permute-start.6
  88.5 3.8 %collective-permute-start.7 = (bf16[12,16,256]{2,1,0:T(8,128)(2,1)S(1)}, bf16[12,16,256]{2,1,0:T(8,128)(2,1)S(1)}, u32[]{:S(2)}, u32[]{:S(2)}) collective-permute-start(bf16[12,16,256]{2,1,0:T(8,128)(2,1)S(1)} %pad_maximum_fusion.2), channel_id=1, source_target_pairs={{16,0},{32,16},{48,32},{64,48},{80,64},{96,80},{112,96},{17,1},{33... | collective-permute-start | bytes 294920 | tf_op jit(solution)/shard_map/ppermute | solution.py:612
  93.5 2.7 %collective-permute-done.6.corner_above = bf16[12,16,256]{2,1,0:T(8,128)(2,1)S(1)} collective-permute-done((bf16[12,16,256]{2,1,0:T(8,128)(2,1)S(1)}, bf16[12,16,256]{2,1,0:T(8,128)(2,1)S(1)}, u32[]{:S(2)}, u32[]{:S(2)}) %collective-permute-start.6) | collective-permute-done | bytes 98336 | tf_op jit(solution)/shard_map/ppermute | solution.py:611
  96.1 36.1 %convs.1 = (bf16[16,128,256]{2,1,0:T(8,128)(2,1)}, bf16[128,128,128]{2,1,0:T(8,128)(2,1)}) custom-call(s32[4]{0:T(128)S(1)} %add_convert_fusion.edges, bf16[16,128,256]{2,1,0:T(8,128)(2,1)S(1)} %get-tuple-element.12.middle, bf16[8,128,256]{2,1,0:T(8,128)(2,1)S(1)} %collective-permute-done.above, bf16[8,128,256]{2,1,0:T(8,128)(2,1)S(1)} %collective-permute-done.1.below, ...), custom_call_target="tpu_custom_call" | custom-call | tf_op jit(solution)/shard_map/convs/pallas_call | solution.py:458
  132.3 13.4 %all-to-all-start.1 = ((bf16[128,128,128]{2,1,0:T(8,128)(2,1)}), bf16[128,128,128]{2,1,0:T(8,128)(2,1)}, u32[]{:S(2)}, u32[]{:S(2)}) async-start(bf16[128,128,128]{2,1,0:T(8,128)(2,1)} %get-tuple-element.16), calls=%async_computation.1 | async-start | bytes 8388608 | tf_op jit(solution)/shard_map/all_to_all | solution.py:618
  145.6 2.3 %reshape.37 = bf16[16,256,128]{2,1,0:T(8,128)(2,1)} reshape(bf16[16,128,256]{2,1,0:T(8,128)(2,1)} %get-tuple-element.14) | data formatting | bytes 2097152 | tf_op jit(solution)/shard_map/reshape | solution.py:621
  148.0 50.9 %all-to-all-done.1.returned = bf16[128,128,128]{2,1,0:T(8,128)(2,1)} async-done(((bf16[128,128,128]{2,1,0:T(8,128)(2,1)}), bf16[128,128,128]{2,1,0:T(8,128)(2,1)}, u32[]{:S(2)}, u32[]{:S(2)}) %all-to-all-start.1) | async-done | bytes 4194336 | tf_op jit(solution)/shard_map/all_to_all | solution.py:618
  198.9 5.5 %final.1 = (bf16[64,64,128]{2,1,0:T(8,128)(2,1)}, bf16[64,128,128]{2,1,0:T(8,128)(2,1)}) custom-call(s32[64]{0:T(128)S(1)} %get-tuple-element.15.slots, bf16[128,128,128]{2,1,0:T(8,128)(2,1)} %all-to-all-done.1.returned, bf16[64,64,128]{2,1,0:T(8,128)(2,1)S(1)} %bitcast.18, bf16[64,128,128]{2,1,0:T(8,128)(2,1)S(1)} %bitcast.16), custom_call_target="tpu_custom_call" | custom-call | tf_op jit(solution)/shard_map/final/pallas_call | solution.py:534
  (37 shorter events, 5.5 us)
Async XLA Ops:
  5.1 10.9 %copy-start.4 = (bf16[16,256,128]{2,1,0:T(8,128)(2,1)S(1)}, bf16[16,256,128]{2,1,0:T(8,128)(2,1)}, u32[]{:S(2)}) copy-start(bf16[16,256,128]{2,1,0:T(8,128)(2,1)} %param.13) | copy-start | bytes 3145732
  5.1 67.2 %all-to-all-start = ((bf16[128,136,128]{2,1,0:T(8,128)(2,1)}), bf16[128,136,128]{2,1,0:T(8,128)(2,1)}, u32[]{:S(2)}, u32[]{:S(2)}) async-start(bf16[128,136,128]{2,1,0:T(8,128)(2,1)} %get-tuple-element.11), calls=%async_computation | async-start | bytes 8912896 | tf_op jit(solution)/shard_map/all_to_all | solution.py:582
  16.0 13.8 %copy-start.3 = (bf16[4,3,3,128,128]{4,3,2,1,0:T(8,128)(2,1)S(1)}, bf16[4,3,3,128,128]{4,3,2,1,0:T(8,128)(2,1)}, u32[]{:S(2)}) copy-start(bf16[4,3,3,128,128]{4,3,2,1,0:T(8,128)(2,1)} %param.12) | copy-start | bytes 3538948
  16.9 71.7 %collective-permute-start.8 = (bf16[4,128,256]{2,1,0:T(8,128)(2,1)}, bf16[4,128,256]{2,1,0:T(8,128)(2,1)S(1)}, u32[]{:S(2)}, u32[]{:S(2)}) collective-permute-start(bf16[4,128,256]{2,1,0:T(8,128)(2,1)} %slice.53), channel_id=1, source_target_pairs={{0,16},{16,32},{32,48},{48,64},{64,80},{80,96},{96,112},{1,17},{17... | collective-permute-start | bytes 786440 | tf_op jit(solution)/shard_map/ppermute | solution.py:587
  19.0 74.5 %collective-permute-start.9 = (bf16[4,128,256]{2,1,0:T(8,128)(2,1)S(1)}, bf16[4,128,256]{2,1,0:T(8,128)(2,1)S(1)}, u32[]{:S(2)}, u32[]{:S(2)}) collective-permute-start(bf16[4,128,256]{2,1,0:T(8,128)(2,1)S(1)} %slice.55), channel_id=1, source_target_pairs={{16,0},{32,16},{48,32},{64,48},{80,64},{96,80},{112,96},{17,1},{33... | collective-permute-start | bytes 786440 | tf_op jit(solution)/shard_map/ppermute | solution.py:588
  24.0 36.1 %collective-permute-start.5 = (bf16[16,8,256]{2,1,0:T(8,128)(2,1)S(1)}, bf16[16,8,256]{2,1,0:T(8,128)(2,1)S(1)}, u32[]{:S(2)}, u32[]{:S(2)}) collective-permute-start(bf16[16,8,256]{2,1,0:T(8,128)(2,1)S(1)} %get-tuple-element.21), channel_id=1, source_target_pairs={{1,0},{2,1},{3,2},{4,3},{5,4},{6,5},{7,6},{8,7},{9,8},{10,9},{11,1... | collective-permute-start | bytes 196616 | tf_op jit(solution)/shard_map/ppermute | solution.py:590
  25.3 34.8 %collective-permute-start.4 = (bf16[16,8,256]{2,1,0:T(8,128)(2,1)S(1)}, bf16[16,8,256]{2,1,0:T(8,128)(2,1)S(1)}, u32[]{:S(2)}, u32[]{:S(2)}) collective-permute-start(bf16[16,8,256]{2,1,0:T(8,128)(2,1)S(1)} %get-tuple-element.22), channel_id=1, source_target_pairs={{0,1},{1,2},{2,3},{3,4},{4,5},{5,6},{6,7},{7,8},{8,9},{9,10},{10,1... | collective-permute-start | bytes 196616 | tf_op jit(solution)/shard_map/ppermute | solution.py:589
  36.5 1.9 copy-start.2
  77.8 6.8 %collective-permute-start.2 = (bf16[16,8,256]{2,1,0:T(8,128)(2,1)S(1)}, bf16[16,8,256]{2,1,0:T(8,128)(2,1)S(1)}, u32[]{:S(2)}, u32[]{:S(2)}) collective-permute-start(bf16[16,8,256]{2,1,0:T(8,128)(2,1)S(1)} %get-tuple-element.24), channel_id=1, source_target_pairs={{0,1},{1,2},{2,3},{3,4},{4,5},{5,6},{6,7},{7,8},{8,9},{9,10},{10,1... | collective-permute-start | bytes 196616 | tf_op jit(solution)/shard_map/ppermute | solution.py:605
  79.2 7.3 %collective-permute-start.3 = (bf16[16,8,256]{2,1,0:T(8,128)(2,1)S(1)}, bf16[16,8,256]{2,1,0:T(8,128)(2,1)S(1)}, u32[]{:S(2)}, u32[]{:S(2)}) collective-permute-start(bf16[16,8,256]{2,1,0:T(8,128)(2,1)S(1)} %get-tuple-element.23), channel_id=1, source_target_pairs={{1,0},{2,1},{3,2},{4,3},{5,4},{6,5},{7,6},{8,7},{9,8},{10,9},{11,1... | collective-permute-start | bytes 196616 | tf_op jit(solution)/shard_map/ppermute | solution.py:606
  80.5 15.6 %collective-permute-start.1 = (bf16[8,128,256]{2,1,0:T(8,128)(2,1)S(1)}, bf16[8,128,256]{2,1,0:T(8,128)(2,1)S(1)}, u32[]{:S(2)}, u32[]{:S(2)}) collective-permute-start(bf16[8,128,256]{2,1,0:T(8,128)(2,1)S(1)} %get-tuple-element.25), channel_id=1, source_target_pairs={{16,0},{32,16},{48,32},{64,48},{80,64},{96,80},{112,96},{17,1},{33... | collective-permute-start | bytes 1572872 | tf_op jit(solution)/shard_map/ppermute | solution.py:604
  84.6 11.6 %collective-permute-start = (bf16[8,128,256]{2,1,0:T(8,128)(2,1)S(1)}, bf16[8,128,256]{2,1,0:T(8,128)(2,1)S(1)}, u32[]{:S(2)}, u32[]{:S(2)}) collective-permute-start(bf16[8,128,256]{2,1,0:T(8,128)(2,1)S(1)} %get-tuple-element.26), channel_id=1, source_target_pairs={{0,16},{16,32},{32,48},{48,64},{64,80},{80,96},{96,112},{1,17},{17... | collective-permute-start | bytes 1572872 | tf_op jit(solution)/shard_map/ppermute | solution.py:603
  86.6 9.5 %collective-permute-start.6 = (bf16[12,16,256]{2,1,0:T(8,128)(2,1)S(1)}, bf16[12,16,256]{2,1,0:T(8,128)(2,1)S(1)}, u32[]{:S(2)}, u32[]{:S(2)}) collective-permute-start(bf16[12,16,256]{2,1,0:T(8,128)(2,1)S(1)} %pad_maximum_fusion.1), channel_id=1, source_target_pairs={{0,16},{16,32},{32,48},{48,64},{64,80},{80,96},{96,112},{1,17},{17... | collective-permute-start | bytes 294920 | tf_op jit(solution)/shard_map/ppermute | solution.py:611
  88.5 7.6 %collective-permute-start.7 = (bf16[12,16,256]{2,1,0:T(8,128)(2,1)S(1)}, bf16[12,16,256]{2,1,0:T(8,128)(2,1)S(1)}, u32[]{:S(2)}, u32[]{:S(2)}) collective-permute-start(bf16[12,16,256]{2,1,0:T(8,128)(2,1)S(1)} %pad_maximum_fusion.2), channel_id=1, source_target_pairs={{16,0},{32,16},{48,32},{64,48},{80,64},{96,80},{112,96},{17,1},{33... | collective-permute-start | bytes 294920 | tf_op jit(solution)/shard_map/ppermute | solution.py:612
  132.3 66.6 %copy-start.1 = (bf16[4,16,64,128]{3,2,1,0:T(8,128)(2,1)S(1)}, bf16[4,16,64,128]{3,2,1,0:T(8,128)(2,1)}, u32[]{:S(2)}) copy-start(bf16[4,16,64,128]{3,2,1,0:T(8,128)(2,1)} %param.7) | copy-start | bytes 3145732
  132.3 66.6 %all-to-all-start.1 = ((bf16[128,128,128]{2,1,0:T(8,128)(2,1)}), bf16[128,128,128]{2,1,0:T(8,128)(2,1)}, u32[]{:S(2)}, u32[]{:S(2)}) async-start(bf16[128,128,128]{2,1,0:T(8,128)(2,1)} %get-tuple-element.16), calls=%async_computation.1 | async-start | bytes 8388608 | tf_op jit(solution)/shard_map/all_to_all | solution.py:618
  145.6 53.2 %copy-start = (bf16[4,16,128,128]{3,2,1,0:T(8,128)(2,1)S(1)}, bf16[4,16,128,128]{3,2,1,0:T(8,128)(2,1)}, u32[]{:S(2)}) copy-start(bf16[4,16,128,128]{3,2,1,0:T(8,128)(2,1)} %param.8) | copy-start | bytes 6291460

commit v8 on v7

--- a/solution.py
+++ b/solution.py
@@ -149,12 +149,12 @@
 
 
 def splat_kernel(
-    meta_all, message, out, tiles_out, acc, rows, cells, codes, numbers, group, group_tile, sems
+    meta_all, message, out, tiles_out, acc, rows, cells, codes, numbers, group, sems
 ):
     owners, _, channels = meta_all.shape
     bins = channels // 2
     tile_count = acc.shape[1] // 8
-    groups = group_tile.shape[0] - owners // 2
+    groups = group.shape[0] // 4 - owners // 2
     arrival = pltpu.make_async_copy(
         message.at[:, pl.ds(0, 2 * bins), :], rows.at[pl.ds(0, owners)], sems.at[0]
     )
@@ -182,7 +182,7 @@
         base = jnp.sum(jnp.where(line < across[rank], needed, 0), axis=0, keepdims=True)
         at = jnp.where(tile < tile_count, base, groups) + lax.shift_right_logical(place[rank], 1)
         codes[rank : rank + 1, :] = 4 * at + 2 * rank + (place[rank] & 1)
-        codes[2 + rank : 3 + rank, :] = tile
+        codes[2 + rank : 3 + rank, :] = 256 * tile + lane[0:1]
         tiles_out[rank : rank + 1, :] = jnp.minimum(tile, tile_count - 1)
     codes[4:5, :] = jnp.sum(needed, axis=0, keepdims=True)
     copy = pltpu.make_async_copy(codes, numbers, sems.at[1])
@@ -190,26 +190,20 @@
     acc[...] = jnp.zeros(acc.shape, F32)
     for i in range(4 * groups):
         group[i] = owners
-    for i in range(groups):
-        group_tile[i] = 0
     copy.wait()
     total = numbers[4, 0]
 
-    def place_source(s, carry):
+    for s in range(owners):
         for rank in range(2):
-            at = numbers[rank, s]
-            group[at] = s
-            group_tile[lax.shift_right_logical(at, 2)] = numbers[2 + rank, s]
-        return carry
-
-    lax.fori_loop(0, owners, place_source, 0, unroll=16)
+            group[numbers[rank, s]] = numbers[2 + rank, s]
     arrival.wait()
     low = lax.broadcasted_iota(jnp.int32, (1, channels), 1) < bins
 
     def batch(b, carry):
         for q in range(8):
-            at = 8 * b + q
-            ids = [group[4 * at + slot] for slot in range(4)]
+            named_slots = [group[4 * (8 * b + q) + slot] for slot in range(4)]
+            ids = [slot & 255 for slot in named_slots]
+            tile = lax.shift_right_logical(jnp.maximum(named_slots[0], named_slots[2]), 8)
             hot = [
                 cell_onehot(
                     jnp.where(low, cells[pl.ds(ids[k], 1), :], cells[pl.ds(ids[2 + k], 1), :]),
@@ -225,7 +219,7 @@
                 jnp.concatenate(parts, axis=0),
                 preferred_element_type=F32,
             ).reshape(TS, 2, 8, channels)
-            here = pl.ds(pl.multiple_of(group_tile[at] * 8, 8), 8)
+            here = pl.ds(pl.multiple_of(tile * 8, 8), 8)
             for side in range(2):
                 acc[:, here, side * channels : (side + 1) * channels] += sums[:, side]
         return carry
@@ -261,7 +255,6 @@
             pltpu.VMEM((8, owners), jnp.int32),
             pltpu.SMEM((8, owners), jnp.int32),
             pltpu.SMEM((4 * spare,), jnp.int32),
-            pltpu.SMEM((spare,), jnp.int32),
             pltpu.SemaphoreType.DMA((2,)),
         ],
         compiler_params=pltpu.CompilerParams(vmem_limit_bytes=24 << 20),
@@ -598,6 +591,7 @@
         [cam == 0, cam == lax.axis_size("cam") - 1, tile == 0, tile == lax.axis_size("tile") - 1]
     ).astype(jnp.int32)
 
+    message, cot_middle = lax.optimization_barrier((message, cot_middle))
     middle, tiles = splat(message, rows, cols)
 
     above = lax.ppermute(middle[rows - EXT :], "cam", down)

time: 206 us -> 205 us (level)
  waiting for transfers between devices: 84.2 us -> 86.9 us
  transfers between devices with their start and end apart: 12 -> 12, of which waited for: 4 -> 4; matrix products, arithmetic and copies ran while one was open for 8% -> 7% of each run, Pallas kernels for 3% -> 3%
where the time goes in v8:
time: 205 us; the launch traced here: 204 us
  waiting for transfers between devices  86.9 us (42%)
  Pallas kernels  51.5 us (25%)
  starting transfers between devices  48.1 us (23%)
  local copies, waits for them, and re-layouts  10.3 us (5%)
  other arithmetic  5.7 us (3%)
    all_to_all x1, waiting for transfers between devices, per_device(): lax.all_to_all(rows_back, axes, split_axis=0, concat_axis=0, tiled=True)  50.9 us
    pallas_call x1, Pallas kernels, convs(): pl.pallas_call(conv_kernel, out_shape=(pltpu.HBM(middle.shape, BF), pltpu...  36.1 us
    ppermute x1, waiting for transfers between devices, per_device(): cot_left = lax.ppermute(cot[:, mid - PAIRS:], 'tile', east)  20.1 us
    all_to_all x1, starting transfers between devices, per_device(): lax.all_to_all(rows_back, axes, split_axis=0, concat_axis=0, tiled=True)  12.4 us
    all_to_all x1, waiting for transfers between devices, per_device(): lax.all_to_all(sent, axes, split_axis=0, concat_axis=0, tiled=True)  12.1 us
    all_to_all x1, starting transfers between devices, per_device(): lax.all_to_all(sent, axes, split_axis=0, concat_axis=0, tiled=True)  10.9 us
    pallas_call x1, Pallas kernels, final(): pl.pallas_call(final_kernel, out_shape=(jax.ShapeDtypeStruct(depth.shape,...  5.53 us
    pallas_call x1, Pallas kernels, splat(): pl.pallas_call(splat_kernel, out_shape=(jax.ShapeDtypeStruct(shape, BF),...  5.38 us
  transfers between devices with their start and end apart: 12, of which 4 were waited for; matrix products, arithmetic and copies ran while one was open for 7% of the time, Pallas kernels for 3%

profile of v8, /device:TPU:6, one launch (start us, length us, event | category | flops | bytes accessed | tf_op | source)
XLA Modules:
  0.0 203.6 jit_solution(9996935803194246291)
XLA Ops:
  0.6 4.4 %pack.1 = (bf16[128,136,128]{2,1,0:T(8,128)(2,1)}, s32[64]{0:T(128)S(1)}) custom-call(s32[4,1,16]{2,1,0:T(1,128)} %bitcast.21, s32[4,16]{1,0:T(4,128)} %local.1, s32[4,16,64]{2,1,0:T(8,128)} %cells.1, bf16[64,64,128]{2,1,0:T(8,128)(2,1)} %bitcast.17, bf16[64,128,128]{2,1,0:T(8,128)(2,1)} %bitcast.15), custom_call_target="tpu_custom_call" | custom-call | tf_op jit(solution)/shard_map/pack/pallas_call | solution.py:123
  5.1 10.9 %all-to-all-start = ((bf16[128,136,128]{2,1,0:T(8,128)(2,1)}), bf16[128,136,128]{2,1,0:T(8,128)(2,1)}, u32[]{:S(2)}, u32[]{:S(2)}) async-start(bf16[128,136,128]{2,1,0:T(8,128)(2,1)} %get-tuple-element.13), calls=%async_computation | async-start | bytes 8912896 | tf_op jit(solution)/shard_map/all_to_all | solution.py:575
  16.1 2.2 %collective-permute-start.8 = (bf16[4,128,256]{2,1,0:T(8,128)(2,1)S(1)}, bf16[4,128,256]{2,1,0:T(8,128)(2,1)S(1)}, u32[]{:S(2)}, u32[]{:S(2)}) collective-permute-start(bf16[4,128,256]{2,1,0:T(8,128)(2,1)S(1)} %slice.61), channel_id=1, source_target_pairs={{0,16},{16,32},{32,48},{48,64},{64,80},{80,96},{96,112},{1,17},{17... | collective-permute-start | bytes 786440 | tf_op jit(solution)/shard_map/ppermute | solution.py:580
  18.4 3.5 %collective-permute-start.9 = (bf16[4,128,256]{2,1,0:T(8,128)(2,1)S(1)}, bf16[4,128,256]{2,1,0:T(8,128)(2,1)S(1)}, u32[]{:S(2)}, u32[]{:S(2)}) collective-permute-start(bf16[4,128,256]{2,1,0:T(8,128)(2,1)S(1)} %slice.63), channel_id=1, source_target_pairs={{16,0},{32,16},{48,32},{64,48},{80,64},{96,80},{112,96},{17,1},{33... | collective-permute-start | bytes 786440 | tf_op jit(solution)/shard_map/ppermute | solution.py:581
  21.9 1.4 reshape.34
  23.4 3.5 %collective-permute-start = (bf16[16,8,256]{2,1,0:T(8,128)(2,1)S(1)}, bf16[16,8,256]{2,1,0:T(8,128)(2,1)S(1)}, u32[]{:S(2)}, u32[]{:S(2)}) collective-permute-start(bf16[16,8,256]{2,1,0:T(8,128)(2,1)S(1)} %get-tuple-element.31), channel_id=1, source_target_pairs={{0,1},{1,2},{2,3},{3,4},{4,5},{5,6},{6,7},{7,8},{8,9},{9,10},{10,1... | collective-permute-start | bytes 196616 | tf_op jit(solution)/shard_map/ppermute | solution.py:582
  28.3 1.8 fusion.4
  30.2 4.7 %copy.11 = bf16[4,3,4,128,256]{4,3,2,1,0:T(8,128)(2,1)} copy(bf16[4,3,4,128,256]{3,4,2,1,0:T(8,128)(2,1)} %fusion.4) | data formatting | bytes 6291456 | tf_op jit(solution)/shard_map/concatenate | solution.py:554
  35.3 1.4 copy-done.2
  36.7 3.2 %maximum_multiply_fusion.weights_far = bf16[8,1536,256]{2,1,0:T(8,128)(2,1)} fusion(bf16[4,1536,256]{2,1,0:T(8,128)(2,1)S(1)} %bitcast.19, bf16[4,1536,256]{2,1,0:T(8,128)(2,1)S(1)} %bitcast.20), kind=kLoop, calls=%fused_computation.4 | loop fusion | flops 6291456 | bytes 12582912 | tf_op jit(solution)/shard_map/mul | solution.py:587
  39.9 20.1 %collective-permute-done = bf16[16,8,256]{2,1,0:T(8,128)(2,1)S(1)} collective-permute-done((bf16[16,8,256]{2,1,0:T(8,128)(2,1)S(1)}, bf16[16,8,256]{2,1,0:T(8,128)(2,1)S(1)}, u32[]{:S(2)}, u32[]{:S(2)}) %collective-permute-start) | collective-permute-done | bytes 65568 | tf_op jit(solution)/shard_map/ppermute | solution.py:582
  60.2 12.1 %all-to-all-done.meta_all.message.meta_far = bf16[128,136,128]{2,1,0:T(8,128)(2,1)} async-done(((bf16[128,136,128]{2,1,0:T(8,128)(2,1)}), bf16[128,136,128]{2,1,0:T(8,128)(2,1)}, u32[]{:S(2)}, u32[]{:S(2)}) %all-to-all-start) | async-done | bytes 4456480 | tf_op jit(solution)/shard_map/all_to_all | solution.py:575
  72.3 5.4 %splat.1 = (bf16[16,128,256]{2,1,0:T(8,128)(2,1)S(1)}, s32[2,128]{1,0:T(2,128)S(1)}) custom-call(bf16[128,136,128]{2,1,0:T(8,128)(2,1)} %all-to-all-done.meta_all.message.meta_far, bf16[128,136,128]{2,1,0:T(8,128)(2,1)} %all-to-all-done.meta_all.message.meta_far), custom_call_target="tpu_custom_call" | custom-call | tf_op jit(solution)/shard_map/splat/pallas_call | solution.py:236
  77.8 1.3 collective-permute-start.4
  80.4 4.1 %collective-permute-start.3 = (bf16[8,128,256]{2,1,0:T(8,128)(2,1)S(1)}, bf16[8,128,256]{2,1,0:T(8,128)(2,1)S(1)}, u32[]{:S(2)}, u32[]{:S(2)}) collective-permute-start(bf16[8,128,256]{2,1,0:T(8,128)(2,1)S(1)} %get-tuple-element.29), channel_id=1, source_target_pairs={{16,0},{32,16},{48,32},{64,48},{80,64},{96,80},{112,96},{17,1},{33... | collective-permute-start | bytes 1572872 | tf_op jit(solution)/shard_map/ppermute | solution.py:598
  84.5 1.9 collective-permute-start.2
  86.5 3.6 %collective-permute-start.7 = (bf16[12,16,256]{2,1,0:T(8,128)(2,1)S(1)}, bf16[12,16,256]{2,1,0:T(8,128)(2,1)S(1)}, u32[]{:S(2)}, u32[]{:S(2)}) collective-permute-start(bf16[12,16,256]{2,1,0:T(8,128)(2,1)S(1)} %get-tuple-element.33), channel_id=1, source_target_pairs={{16,0},{32,16},{48,32},{64,48},{80,64},{96,80},{112,96},{17,1},{33... | collective-permute-start | bytes 294920 | tf_op jit(solution)/shard_map/ppermute | solution.py:606
  90.2 2.1 %collective-permute-start.6 = (bf16[12,16,256]{2,1,0:T(8,128)(2,1)S(1)}, bf16[12,16,256]{2,1,0:T(8,128)(2,1)S(1)}, u32[]{:S(2)}, u32[]{:S(2)}) collective-permute-start(bf16[12,16,256]{2,1,0:T(8,128)(2,1)S(1)} %get-tuple-element.34), channel_id=1, source_target_pairs={{0,16},{16,32},{32,48},{48,64},{64,80},{80,96},{96,112},{1,17},{17... | collective-permute-start | bytes 294920 | tf_op jit(solution)/shard_map/ppermute | solution.py:605
  92.3 3.7 %collective-permute-done.6.corner_above = bf16[12,16,256]{2,1,0:T(8,128)(2,1)S(1)} collective-permute-done((bf16[12,16,256]{2,1,0:T(8,128)(2,1)S(1)}, bf16[12,16,256]{2,1,0:T(8,128)(2,1)S(1)}, u32[]{:S(2)}, u32[]{:S(2)}) %collective-permute-start.6) | collective-permute-done | bytes 98336 | tf_op jit(solution)/shard_map/ppermute | solution.py:605
  96.1 36.1 %convs.1 = (bf16[16,128,256]{2,1,0:T(8,128)(2,1)}, bf16[128,128,128]{2,1,0:T(8,128)(2,1)}) custom-call(s32[4]{0:T(128)S(1)} %add_convert_fusion.edges, bf16[16,128,256]{2,1,0:T(8,128)(2,1)S(1)} %get-tuple-element.15.middle, bf16[8,128,256]{2,1,0:T(8,128)(2,1)S(1)} %collective-permute-done.2.above, bf16[8,128,256]{2,1,0:T(8,128)(2,1)S(1)} %collective-permute-done.3.below, ...), custom_call_target="tpu_custom_call" | custom-call | tf_op jit(solution)/shard_map/convs/pallas_call | solution.py:451
  132.2 12.4 %all-to-all-start.1 = ((bf16[128,128,128]{2,1,0:T(8,128)(2,1)}), bf16[128,128,128]{2,1,0:T(8,128)(2,1)}, u32[]{:S(2)}, u32[]{:S(2)}) async-start(bf16[128,128,128]{2,1,0:T(8,128)(2,1)} %get-tuple-element.20), calls=%async_computation.1 | async-start | bytes 8388608 | tf_op jit(solution)/shard_map/all_to_all | solution.py:612
  144.6 2.3 %reshape.37 = bf16[16,256,128]{2,1,0:T(8,128)(2,1)} reshape(bf16[16,128,256]{2,1,0:T(8,128)(2,1)} %get-tuple-element.18) | data formatting | bytes 2097152 | tf_op jit(solution)/shard_map/reshape | solution.py:615
  147.0 50.9 %all-to-all-done.1.returned = bf16[128,128,128]{2,1,0:T(8,128)(2,1)} async-done(((bf16[128,128,128]{2,1,0:T(8,128)(2,1)}), bf16[128,128,128]{2,1,0:T(8,128)(2,1)}, u32[]{:S(2)}, u32[]{:S(2)}) %all-to-all-start.1) | async-done | bytes 4194336 | tf_op jit(solution)/shard_map/all_to_all | solution.py:612
  197.9 5.5 %final.1 = (bf16[64,64,128]{2,1,0:T(8,128)(2,1)}, bf16[64,128,128]{2,1,0:T(8,128)(2,1)}) custom-call(s32[64]{0:T(128)S(1)} %get-tuple-element.19.slots, bf16[128,128,128]{2,1,0:T(8,128)(2,1)} %all-to-all-done.1.returned, bf16[64,64,128]{2,1,0:T(8,128)(2,1)S(1)} %bitcast.18, bf16[64,128,128]{2,1,0:T(8,128)(2,1)S(1)} %bitcast.16), custom_call_target="tpu_custom_call" | custom-call | tf_op jit(solution)/shard_map/final/pallas_call | solution.py:527
  (36 shorter events, 3.7 us)
Async XLA Ops:
  5.1 10.9 %copy-start.5 = (bf16[16,256,128]{2,1,0:T(8,128)(2,1)S(1)}, bf16[16,256,128]{2,1,0:T(8,128)(2,1)}, u32[]{:S(2)}) copy-start(bf16[16,256,128]{2,1,0:T(8,128)(2,1)} %param.13) | copy-start | bytes 3145732
  5.1 67.2 %all-to-all-start = ((bf16[128,136,128]{2,1,0:T(8,128)(2,1)}), bf16[128,136,128]{2,1,0:T(8,128)(2,1)}, u32[]{:S(2)}, u32[]{:S(2)}) async-start(bf16[128,136,128]{2,1,0:T(8,128)(2,1)} %get-tuple-element.13), calls=%async_computation | async-start | bytes 8912896 | tf_op jit(solution)/shard_map/all_to_all | solution.py:575
  16.0 12.3 %copy-start.4 = (bf16[4,3,3,128,128]{4,3,2,1,0:T(8,128)(2,1)S(1)}, bf16[4,3,3,128,128]{4,3,2,1,0:T(8,128)(2,1)}, u32[]{:S(2)}) copy-start(bf16[4,3,3,128,128]{4,3,2,1,0:T(8,128)(2,1)} %param.12) | copy-start | bytes 3538948
  16.1 74.0 %collective-permute-start.8 = (bf16[4,128,256]{2,1,0:T(8,128)(2,1)S(1)}, bf16[4,128,256]{2,1,0:T(8,128)(2,1)S(1)}, u32[]{:S(2)}, u32[]{:S(2)}) collective-permute-start(bf16[4,128,256]{2,1,0:T(8,128)(2,1)S(1)} %slice.61), channel_id=1, source_target_pairs={{0,16},{16,32},{32,48},{48,64},{64,80},{80,96},{96,112},{1,17},{17... | collective-permute-start | bytes 786440 | tf_op jit(solution)/shard_map/ppermute | solution.py:580
  18.4 73.9 %collective-permute-start.9 = (bf16[4,128,256]{2,1,0:T(8,128)(2,1)S(1)}, bf16[4,128,256]{2,1,0:T(8,128)(2,1)S(1)}, u32[]{:S(2)}, u32[]{:S(2)}) collective-permute-start(bf16[4,128,256]{2,1,0:T(8,128)(2,1)S(1)} %slice.63), channel_id=1, source_target_pairs={{16,0},{32,16},{48,32},{64,48},{80,64},{96,80},{112,96},{17,1},{33... | collective-permute-start | bytes 786440 | tf_op jit(solution)/shard_map/ppermute | solution.py:581
  23.4 36.7 %collective-permute-start = (bf16[16,8,256]{2,1,0:T(8,128)(2,1)S(1)}, bf16[16,8,256]{2,1,0:T(8,128)(2,1)S(1)}, u32[]{:S(2)}, u32[]{:S(2)}) collective-permute-start(bf16[16,8,256]{2,1,0:T(8,128)(2,1)S(1)} %get-tuple-element.31), channel_id=1, source_target_pairs={{0,1},{1,2},{2,3},{3,4},{4,5},{5,6},{6,7},{7,8},{8,9},{9,10},{10,1... | collective-permute-start | bytes 196616 | tf_op jit(solution)/shard_map/ppermute | solution.py:582
  26.9 33.1 %collective-permute-start.1 = (bf16[16,8,256]{2,1,0:T(8,128)(2,1)S(1)}, bf16[16,8,256]{2,1,0:T(8,128)(2,1)S(1)}, u32[]{:S(2)}, u32[]{:S(2)}) collective-permute-start(bf16[16,8,256]{2,1,0:T(8,128)(2,1)S(1)} %get-tuple-element.32), channel_id=1, source_target_pairs={{1,0},{2,1},{3,2},{4,3},{5,4},{6,5},{7,6},{8,7},{9,8},{10,9},{11,1... | collective-permute-start | bytes 196616 | tf_op jit(solution)/shard_map/ppermute | solution.py:583
  34.8 1.9 copy-start.2
  60.1 18.9 %copy-start.3 = (bf16[16,144,256]{2,1,0:T(8,128)(2,1)}, bf16[16,144,256]{2,1,0:T(8,128)(2,1)S(1)}, u32[]{:S(2)}) copy-start(bf16[16,144,256]{2,1,0:T(8,128)(2,1)S(1)} %pad_maximum_fusion.cot_far) | copy-start | bytes 3538948
  77.8 6.7 %collective-permute-start.4 = (bf16[16,8,256]{2,1,0:T(8,128)(2,1)S(1)}, bf16[16,8,256]{2,1,0:T(8,128)(2,1)S(1)}, u32[]{:S(2)}, u32[]{:S(2)}) collective-permute-start(bf16[16,8,256]{2,1,0:T(8,128)(2,1)S(1)} %get-tuple-element.28), channel_id=1, source_target_pairs={{0,1},{1,2},{2,3},{3,4},{4,5},{5,6},{6,7},{7,8},{8,9},{9,10},{10,1... | collective-permute-start | bytes 196616 | tf_op jit(solution)/shard_map/ppermute | solution.py:599
  79.1 7.3 %collective-permute-start.5 = (bf16[16,8,256]{2,1,0:T(8,128)(2,1)S(1)}, bf16[16,8,256]{2,1,0:T(8,128)(2,1)S(1)}, u32[]{:S(2)}, u32[]{:S(2)}) collective-permute-start(bf16[16,8,256]{2,1,0:T(8,128)(2,1)S(1)} %get-tuple-element.27), channel_id=1, source_target_pairs={{1,0},{2,1},{3,2},{4,3},{5,4},{6,5},{7,6},{8,7},{9,8},{10,9},{11,1... | collective-permute-start | bytes 196616 | tf_op jit(solution)/shard_map/ppermute | solution.py:600
  80.4 15.7 %collective-permute-start.3 = (bf16[8,128,256]{2,1,0:T(8,128)(2,1)S(1)}, bf16[8,128,256]{2,1,0:T(8,128)(2,1)S(1)}, u32[]{:S(2)}, u32[]{:S(2)}) collective-permute-start(bf16[8,128,256]{2,1,0:T(8,128)(2,1)S(1)} %get-tuple-element.29), channel_id=1, source_target_pairs={{16,0},{32,16},{48,32},{64,48},{80,64},{96,80},{112,96},{17,1},{33... | collective-permute-start | bytes 1572872 | tf_op jit(solution)/shard_map/ppermute | solution.py:598
  84.5 11.6 %collective-permute-start.2 = (bf16[8,128,256]{2,1,0:T(8,128)(2,1)S(1)}, bf16[8,128,256]{2,1,0:T(8,128)(2,1)S(1)}, u32[]{:S(2)}, u32[]{:S(2)}) collective-permute-start(bf16[8,128,256]{2,1,0:T(8,128)(2,1)S(1)} %get-tuple-element.30), channel_id=1, source_target_pairs={{0,16},{16,32},{32,48},{48,64},{64,80},{80,96},{96,112},{1,17},{17... | collective-permute-start | bytes 1572872 | tf_op jit(solution)/shard_map/ppermute | solution.py:597
  86.5 5.9 %collective-permute-start.7 = (bf16[12,16,256]{2,1,0:T(8,128)(2,1)S(1)}, bf16[12,16,256]{2,1,0:T(8,128)(2,1)S(1)}, u32[]{:S(2)}, u32[]{:S(2)}) collective-permute-start(bf16[12,16,256]{2,1,0:T(8,128)(2,1)S(1)} %get-tuple-element.33), channel_id=1, source_target_pairs={{16,0},{32,16},{48,32},{64,48},{80,64},{96,80},{112,96},{17,1},{33... | collective-permute-start | bytes 294920 | tf_op jit(solution)/shard_map/ppermute | solution.py:606
  90.2 5.9 %collective-permute-start.6 = (bf16[12,16,256]{2,1,0:T(8,128)(2,1)S(1)}, bf16[12,16,256]{2,1,0:T(8,128)(2,1)S(1)}, u32[]{:S(2)}, u32[]{:S(2)}) collective-permute-start(bf16[12,16,256]{2,1,0:T(8,128)(2,1)S(1)} %get-tuple-element.34), channel_id=1, source_target_pairs={{0,16},{16,32},{32,48},{48,64},{64,80},{80,96},{96,112},{1,17},{17... | collective-permute-start | bytes 294920 | tf_op jit(solution)/shard_map/ppermute | solution.py:605
  132.2 65.6 %copy-start.1 = (bf16[4,16,64,128]{3,2,1,0:T(8,128)(2,1)S(1)}, bf16[4,16,64,128]{3,2,1,0:T(8,128)(2,1)}, u32[]{:S(2)}) copy-start(bf16[4,16,64,128]{3,2,1,0:T(8,128)(2,1)} %param.7) | copy-start | bytes 3145732
  132.2 65.6 %all-to-all-start.1 = ((bf16[128,128,128]{2,1,0:T(8,128)(2,1)}), bf16[128,128,128]{2,1,0:T(8,128)(2,1)}, u32[]{:S(2)}, u32[]{:S(2)}) async-start(bf16[128,128,128]{2,1,0:T(8,128)(2,1)} %get-tuple-element.20), calls=%async_computation.1 | async-start | bytes 8388608 | tf_op jit(solution)/shard_map/all_to_all | solution.py:612
  144.6 53.2 %copy-start = (bf16[4,16,128,128]{3,2,1,0:T(8,128)(2,1)S(1)}, bf16[4,16,128,128]{3,2,1,0:T(8,128)(2,1)}, u32[]{:S(2)}) copy-start(bf16[4,16,128,128]{3,2,1,0:T(8,128)(2,1)} %param.8) | copy-start | bytes 6291460

commit v9 on v8

--- a/solution.py
+++ b/solution.py
@@ -265,7 +265,7 @@
 def chunks_of(count):
     parts = -(-count // 7)
     size = -(-count // parts)
-    return size, [min(i * size, count - size) for i in range(parts)]
+    return size, parts, count - (parts - 1) * size
 
 
 def conv_kernel(
@@ -387,7 +387,7 @@
     source, target = ping, pong
     finish = None
     for index, count, epilogue in stages:
-        size, starts = chunks_of(count)
+        size, parts, last = chunks_of(count)
         arrivals[index].wait()
         if index == LAYERS - 1:
             cot_arrival.wait()
@@ -397,11 +397,14 @@
 
         def steady(k, carry, index=index, count=count, size=size, source=source, target=target, epilogue=epilogue):
             epilogue(target, (k - 1) * size, size)
-            matmul(source, index, jnp.minimum(k * size, count - size), size)
+            matmul(source, index, k * size, size)
             return carry
 
-        lax.fori_loop(1, len(starts), steady, 0)
-        finish = functools.partial(epilogue, target, starts[-1], size)
+        lax.fori_loop(1, parts if last == size else parts - 1, steady, 0)
+        if last < size:
+            epilogue(target, (parts - 2) * size, size)
+            matmul(source, index, (parts - 1) * size, last)
+        finish = functools.partial(epilogue, target, (parts - 1) * size, last)
         source, target = target, source
         if index == 2 * LAYERS - 1:
             bev_copy = pltpu.make_async_copy(

time: 205 us -> 207 us (level)
  Pallas kernels: 51.5 us -> 53.6 us
    pallas_call x1, Pallas kernels: 36.1 us -> 38.2 us  [convs(): pl.pallas_call(conv_kernel, out_shape=(pltpu.HBM(middle.shape, BF), pltpu...]
where the time goes in v9:
time: 207 us; the launch traced here: 206 us
  waiting for transfers between devices  86.9 us (42%)
  Pallas kernels  53.6 us (26%)
  starting transfers between devices  48.1 us (23%)
  local copies, waits for them, and re-layouts  10.3 us (5%)
  other arithmetic  5.7 us (3%)
    all_to_all x1, waiting for transfers between devices, per_device(): lax.all_to_all(rows_back, axes, split_axis=0, concat_axis=0, tiled=True)  50.9 us
    pallas_call x1, Pallas kernels, convs(): pl.pallas_call(conv_kernel, out_shape=(pltpu.HBM(middle.shape, BF), pltpu...  38.2 us
    ppermute x1, waiting for transfers between devices, per_device(): cot_left = lax.ppermute(cot[:, mid - PAIRS:], 'tile', east)  20.1 us
    all_to_all x1, starting transfers between devices, per_device(): lax.all_to_all(rows_back, axes, split_axis=0, concat_axis=0, tiled=True)  12.4 us
    all_to_all x1, waiting for transfers between devices, per_device(): lax.all_to_all(sent, axes, split_axis=0, concat_axis=0, tiled=True)  12.1 us
    all_to_all x1, starting transfers between devices, per_device(): lax.all_to_all(sent, axes, split_axis=0, concat_axis=0, tiled=True)  10.9 us
    pallas_call x1, Pallas kernels, final(): pl.pallas_call(final_kernel, out_shape=(jax.ShapeDtypeStruct(depth.shape,...  5.54 us
    pallas_call x1, Pallas kernels, splat(): pl.pallas_call(splat_kernel, out_shape=(jax.ShapeDtypeStruct(shape, BF),...  5.38 us
  transfers between devices with their start and end apart: 12, of which 4 were waited for; matrix products, arithmetic and copies ran while one was open for 7% of the time, Pallas kernels for 3%

profile of v9, /device:TPU:6, one launch (start us, length us, event | category | flops | bytes accessed | tf_op | source)
XLA Modules:
  0.0 205.7 jit_solution(11956435655655001823)
XLA Ops:
  0.6 4.4 %pack.1 = (bf16[128,136,128]{2,1,0:T(8,128)(2,1)}, s32[64]{0:T(128)S(1)}) custom-call(s32[4,1,16]{2,1,0:T(1,128)} %bitcast.21, s32[4,16]{1,0:T(4,128)} %local.1, s32[4,16,64]{2,1,0:T(8,128)} %cells.1, bf16[64,64,128]{2,1,0:T(8,128)(2,1)} %bitcast.17, bf16[64,128,128]{2,1,0:T(8,128)(2,1)} %bitcast.15), custom_call_target="tpu_custom_call" | custom-call | tf_op jit(solution)/shard_map/pack/pallas_call | solution.py:123
  5.1 10.9 %all-to-all-start = ((bf16[128,136,128]{2,1,0:T(8,128)(2,1)}), bf16[128,136,128]{2,1,0:T(8,128)(2,1)}, u32[]{:S(2)}, u32[]{:S(2)}) async-start(bf16[128,136,128]{2,1,0:T(8,128)(2,1)} %get-tuple-element.13), calls=%async_computation | async-start | bytes 8912896 | tf_op jit(solution)/shard_map/all_to_all | solution.py:578
  16.1 2.2 %collective-permute-start.8 = (bf16[4,128,256]{2,1,0:T(8,128)(2,1)S(1)}, bf16[4,128,256]{2,1,0:T(8,128)(2,1)S(1)}, u32[]{:S(2)}, u32[]{:S(2)}) collective-permute-start(bf16[4,128,256]{2,1,0:T(8,128)(2,1)S(1)} %slice.61), channel_id=1, source_target_pairs={{0,16},{16,32},{32,48},{48,64},{64,80},{80,96},{96,112},{1,17},{17... | collective-permute-start | bytes 786440 | tf_op jit(solution)/shard_map/ppermute | solution.py:583
  18.4 3.5 %collective-permute-start.9 = (bf16[4,128,256]{2,1,0:T(8,128)(2,1)S(1)}, bf16[4,128,256]{2,1,0:T(8,128)(2,1)S(1)}, u32[]{:S(2)}, u32[]{:S(2)}) collective-permute-start(bf16[4,128,256]{2,1,0:T(8,128)(2,1)S(1)} %slice.63), channel_id=1, source_target_pairs={{16,0},{32,16},{48,32},{64,48},{80,64},{96,80},{112,96},{17,1},{33... | collective-permute-start | bytes 786440 | tf_op jit(solution)/shard_map/ppermute | solution.py:584
  21.9 1.4 reshape.34
  23.4 3.5 %collective-permute-start = (bf16[16,8,256]{2,1,0:T(8,128)(2,1)S(1)}, bf16[16,8,256]{2,1,0:T(8,128)(2,1)S(1)}, u32[]{:S(2)}, u32[]{:S(2)}) collective-permute-start(bf16[16,8,256]{2,1,0:T(8,128)(2,1)S(1)} %get-tuple-element.31), channel_id=1, source_target_pairs={{0,1},{1,2},{2,3},{3,4},{4,5},{5,6},{6,7},{7,8},{8,9},{9,10},{10,1... | collective-permute-start | bytes 196616 | tf_op jit(solution)/shard_map/ppermute | solution.py:585
  28.3 1.8 fusion.4
  30.2 4.7 %copy.11 = bf16[4,3,4,128,256]{4,3,2,1,0:T(8,128)(2,1)} copy(bf16[4,3,4,128,256]{3,4,2,1,0:T(8,128)(2,1)} %fusion.4) | data formatting | bytes 6291456 | tf_op jit(solution)/shard_map/concatenate | solution.py:557
  35.3 1.4 copy-done.2
  36.7 3.2 %maximum_multiply_fusion.weights_far = bf16[8,1536,256]{2,1,0:T(8,128)(2,1)} fusion(bf16[4,1536,256]{2,1,0:T(8,128)(2,1)S(1)} %bitcast.19, bf16[4,1536,256]{2,1,0:T(8,128)(2,1)S(1)} %bitcast.20), kind=kLoop, calls=%fused_computation.4 | loop fusion | flops 6291456 | bytes 12582912 | tf_op jit(solution)/shard_map/mul | solution.py:590
  39.9 20.1 %collective-permute-done = bf16[16,8,256]{2,1,0:T(8,128)(2,1)S(1)} collective-permute-done((bf16[16,8,256]{2,1,0:T(8,128)(2,1)S(1)}, bf16[16,8,256]{2,1,0:T(8,128)(2,1)S(1)}, u32[]{:S(2)}, u32[]{:S(2)}) %collective-permute-start) | collective-permute-done | bytes 65568 | tf_op jit(solution)/shard_map/ppermute | solution.py:585
  60.2 12.1 %all-to-all-done.meta_all.message.meta_far = bf16[128,136,128]{2,1,0:T(8,128)(2,1)} async-done(((bf16[128,136,128]{2,1,0:T(8,128)(2,1)}), bf16[128,136,128]{2,1,0:T(8,128)(2,1)}, u32[]{:S(2)}, u32[]{:S(2)}) %all-to-all-start) | async-done | bytes 4456480 | tf_op jit(solution)/shard_map/all_to_all | solution.py:578
  72.3 5.4 %splat.1 = (bf16[16,128,256]{2,1,0:T(8,128)(2,1)S(1)}, s32[2,128]{1,0:T(2,128)S(1)}) custom-call(bf16[128,136,128]{2,1,0:T(8,128)(2,1)} %all-to-all-done.meta_all.message.meta_far, bf16[128,136,128]{2,1,0:T(8,128)(2,1)} %all-to-all-done.meta_all.message.meta_far), custom_call_target="tpu_custom_call" | custom-call | tf_op jit(solution)/shard_map/splat/pallas_call | solution.py:236
  77.8 1.3 collective-permute-start.4
  80.4 4.1 %collective-permute-start.3 = (bf16[8,128,256]{2,1,0:T(8,128)(2,1)S(1)}, bf16[8,128,256]{2,1,0:T(8,128)(2,1)S(1)}, u32[]{:S(2)}, u32[]{:S(2)}) collective-permute-start(bf16[8,128,256]{2,1,0:T(8,128)(2,1)S(1)} %get-tuple-element.29), channel_id=1, source_target_pairs={{16,0},{32,16},{48,32},{64,48},{80,64},{96,80},{112,96},{17,1},{33... | collective-permute-start | bytes 1572872 | tf_op jit(solution)/shard_map/ppermute | solution.py:601
  84.5 1.9 collective-permute-start.2
  86.5 3.6 %collective-permute-start.7 = (bf16[12,16,256]{2,1,0:T(8,128)(2,1)S(1)}, bf16[12,16,256]{2,1,0:T(8,128)(2,1)S(1)}, u32[]{:S(2)}, u32[]{:S(2)}) collective-permute-start(bf16[12,16,256]{2,1,0:T(8,128)(2,1)S(1)} %get-tuple-element.33), channel_id=1, source_target_pairs={{16,0},{32,16},{48,32},{64,48},{80,64},{96,80},{112,96},{17,1},{33... | collective-permute-start | bytes 294920 | tf_op jit(solution)/shard_map/ppermute | solution.py:609
  90.2 2.1 %collective-permute-start.6 = (bf16[12,16,256]{2,1,0:T(8,128)(2,1)S(1)}, bf16[12,16,256]{2,1,0:T(8,128)(2,1)S(1)}, u32[]{:S(2)}, u32[]{:S(2)}) collective-permute-start(bf16[12,16,256]{2,1,0:T(8,128)(2,1)S(1)} %get-tuple-element.34), channel_id=1, source_target_pairs={{0,16},{16,32},{32,48},{48,64},{64,80},{80,96},{96,112},{1,17},{17... | collective-permute-start | bytes 294920 | tf_op jit(solution)/shard_map/ppermute | solution.py:608
  92.3 3.7 %collective-permute-done.6.corner_above = bf16[12,16,256]{2,1,0:T(8,128)(2,1)S(1)} collective-permute-done((bf16[12,16,256]{2,1,0:T(8,128)(2,1)S(1)}, bf16[12,16,256]{2,1,0:T(8,128)(2,1)S(1)}, u32[]{:S(2)}, u32[]{:S(2)}) %collective-permute-start.6) | collective-permute-done | bytes 98336 | tf_op jit(solution)/shard_map/ppermute | solution.py:608
  96.1 38.2 %convs.1 = (bf16[16,128,256]{2,1,0:T(8,128)(2,1)}, bf16[128,128,128]{2,1,0:T(8,128)(2,1)}) custom-call(s32[4]{0:T(128)S(1)} %add_convert_fusion.edges, bf16[16,128,256]{2,1,0:T(8,128)(2,1)S(1)} %get-tuple-element.15.middle, bf16[8,128,256]{2,1,0:T(8,128)(2,1)S(1)} %collective-permute-done.2.above, bf16[8,128,256]{2,1,0:T(8,128)(2,1)S(1)} %collective-permute-done.3.below, ...), custom_call_target="tpu_custom_call" | custom-call | tf_op jit(solution)/shard_map/convs/pallas_call | solution.py:454
  134.3 12.4 %all-to-all-start.1 = ((bf16[128,128,128]{2,1,0:T(8,128)(2,1)}), bf16[128,128,128]{2,1,0:T(8,128)(2,1)}, u32[]{:S(2)}, u32[]{:S(2)}) async-start(bf16[128,128,128]{2,1,0:T(8,128)(2,1)} %get-tuple-element.20), calls=%async_computation.1 | async-start | bytes 8388608 | tf_op jit(solution)/shard_map/all_to_all | solution.py:615
  146.7 2.3 %reshape.37 = bf16[16,256,128]{2,1,0:T(8,128)(2,1)} reshape(bf16[16,128,256]{2,1,0:T(8,128)(2,1)} %get-tuple-element.18) | data formatting | bytes 2097152 | tf_op jit(solution)/shard_map/reshape | solution.py:618
  149.1 50.9 %all-to-all-done.1.returned = bf16[128,128,128]{2,1,0:T(8,128)(2,1)} async-done(((bf16[128,128,128]{2,1,0:T(8,128)(2,1)}), bf16[128,128,128]{2,1,0:T(8,128)(2,1)}, u32[]{:S(2)}, u32[]{:S(2)}) %all-to-all-start.1) | async-done | bytes 4194336 | tf_op jit(solution)/shard_map/all_to_all | solution.py:615
  200.0 5.5 %final.1 = (bf16[64,64,128]{2,1,0:T(8,128)(2,1)}, bf16[64,128,128]{2,1,0:T(8,128)(2,1)}) custom-call(s32[64]{0:T(128)S(1)} %get-tuple-element.19.slots, bf16[128,128,128]{2,1,0:T(8,128)(2,1)} %all-to-all-done.1.returned, bf16[64,64,128]{2,1,0:T(8,128)(2,1)S(1)} %bitcast.18, bf16[64,128,128]{2,1,0:T(8,128)(2,1)S(1)} %bitcast.16), custom_call_target="tpu_custom_call" | custom-call | tf_op jit(solution)/shard_map/final/pallas_call | solution.py:530
  (36 shorter events, 3.7 us)
Async XLA Ops:
  5.1 10.9 %copy-start.5 = (bf16[16,256,128]{2,1,0:T(8,128)(2,1)S(1)}, bf16[16,256,128]{2,1,0:T(8,128)(2,1)}, u32[]{:S(2)}) copy-start(bf16[16,256,128]{2,1,0:T(8,128)(2,1)} %param.13) | copy-start | bytes 3145732
  5.1 67.2 %all-to-all-start = ((bf16[128,136,128]{2,1,0:T(8,128)(2,1)}), bf16[128,136,128]{2,1,0:T(8,128)(2,1)}, u32[]{:S(2)}, u32[]{:S(2)}) async-start(bf16[128,136,128]{2,1,0:T(8,128)(2,1)} %get-tuple-element.13), calls=%async_computation | async-start | bytes 8912896 | tf_op jit(solution)/shard_map/all_to_all | solution.py:578
  16.0 12.3 %copy-start.4 = (bf16[4,3,3,128,128]{4,3,2,1,0:T(8,128)(2,1)S(1)}, bf16[4,3,3,128,128]{4,3,2,1,0:T(8,128)(2,1)}, u32[]{:S(2)}) copy-start(bf16[4,3,3,128,128]{4,3,2,1,0:T(8,128)(2,1)} %param.12) | copy-start | bytes 3538948
  16.1 74.0 %collective-permute-start.8 = (bf16[4,128,256]{2,1,0:T(8,128)(2,1)S(1)}, bf16[4,128,256]{2,1,0:T(8,128)(2,1)S(1)}, u32[]{:S(2)}, u32[]{:S(2)}) collective-permute-start(bf16[4,128,256]{2,1,0:T(8,128)(2,1)S(1)} %slice.61), channel_id=1, source_target_pairs={{0,16},{16,32},{32,48},{48,64},{64,80},{80,96},{96,112},{1,17},{17... | collective-permute-start | bytes 786440 | tf_op jit(solution)/shard_map/ppermute | solution.py:583
  18.4 73.9 %collective-permute-start.9 = (bf16[4,128,256]{2,1,0:T(8,128)(2,1)S(1)}, bf16[4,128,256]{2,1,0:T(8,128)(2,1)S(1)}, u32[]{:S(2)}, u32[]{:S(2)}) collective-permute-start(bf16[4,128,256]{2,1,0:T(8,128)(2,1)S(1)} %slice.63), channel_id=1, source_target_pairs={{16,0},{32,16},{48,32},{64,48},{80,64},{96,80},{112,96},{17,1},{33... | collective-permute-start | bytes 786440 | tf_op jit(solution)/shard_map/ppermute | solution.py:584
  23.4 36.7 %collective-permute-start = (bf16[16,8,256]{2,1,0:T(8,128)(2,1)S(1)}, bf16[16,8,256]{2,1,0:T(8,128)(2,1)S(1)}, u32[]{:S(2)}, u32[]{:S(2)}) collective-permute-start(bf16[16,8,256]{2,1,0:T(8,128)(2,1)S(1)} %get-tuple-element.31), channel_id=1, source_target_pairs={{0,1},{1,2},{2,3},{3,4},{4,5},{5,6},{6,7},{7,8},{8,9},{9,10},{10,1... | collective-permute-start | bytes 196616 | tf_op jit(solution)/shard_map/ppermute | solution.py:585
  26.9 33.1 %collective-permute-start.1 = (bf16[16,8,256]{2,1,0:T(8,128)(2,1)S(1)}, bf16[16,8,256]{2,1,0:T(8,128)(2,1)S(1)}, u32[]{:S(2)}, u32[]{:S(2)}) collective-permute-start(bf16[16,8,256]{2,1,0:T(8,128)(2,1)S(1)} %get-tuple-element.32), channel_id=1, source_target_pairs={{1,0},{2,1},{3,2},{4,3},{5,4},{6,5},{7,6},{8,7},{9,8},{10,9},{11,1... | collective-permute-start | bytes 196616 | tf_op jit(solution)/shard_map/ppermute | solution.py:586
  34.8 1.9 copy-start.2
  60.1 18.9 %copy-start.3 = (bf16[16,144,256]{2,1,0:T(8,128)(2,1)}, bf16[16,144,256]{2,1,0:T(8,128)(2,1)S(1)}, u32[]{:S(2)}) copy-start(bf16[16,144,256]{2,1,0:T(8,128)(2,1)S(1)} %pad_maximum_fusion.cot_far) | copy-start | bytes 3538948
  77.8 6.7 %collective-permute-start.4 = (bf16[16,8,256]{2,1,0:T(8,128)(2,1)S(1)}, bf16[16,8,256]{2,1,0:T(8,128)(2,1)S(1)}, u32[]{:S(2)}, u32[]{:S(2)}) collective-permute-start(bf16[16,8,256]{2,1,0:T(8,128)(2,1)S(1)} %get-tuple-element.28), channel_id=1, source_target_pairs={{0,1},{1,2},{2,3},{3,4},{4,5},{5,6},{6,7},{7,8},{8,9},{9,10},{10,1... | collective-permute-start | bytes 196616 | tf_op jit(solution)/shard_map/ppermute | solution.py:602
  79.1 7.3 %collective-permute-start.5 = (bf16[16,8,256]{2,1,0:T(8,128)(2,1)S(1)}, bf16[16,8,256]{2,1,0:T(8,128)(2,1)S(1)}, u32[]{:S(2)}, u32[]{:S(2)}) collective-permute-start(bf16[16,8,256]{2,1,0:T(8,128)(2,1)S(1)} %get-tuple-element.27), channel_id=1, source_target_pairs={{1,0},{2,1},{3,2},{4,3},{5,4},{6,5},{7,6},{8,7},{9,8},{10,9},{11,1... | collective-permute-start | bytes 196616 | tf_op jit(solution)/shard_map/ppermute | solution.py:603
  80.4 15.7 %collective-permute-start.3 = (bf16[8,128,256]{2,1,0:T(8,128)(2,1)S(1)}, bf16[8,128,256]{2,1,0:T(8,128)(2,1)S(1)}, u32[]{:S(2)}, u32[]{:S(2)}) collective-permute-start(bf16[8,128,256]{2,1,0:T(8,128)(2,1)S(1)} %get-tuple-element.29), channel_id=1, source_target_pairs={{16,0},{32,16},{48,32},{64,48},{80,64},{96,80},{112,96},{17,1},{33... | collective-permute-start | bytes 1572872 | tf_op jit(solution)/shard_map/ppermute | solution.py:601
  84.5 11.6 %collective-permute-start.2 = (bf16[8,128,256]{2,1,0:T(8,128)(2,1)S(1)}, bf16[8,128,256]{2,1,0:T(8,128)(2,1)S(1)}, u32[]{:S(2)}, u32[]{:S(2)}) collective-permute-start(bf16[8,128,256]{2,1,0:T(8,128)(2,1)S(1)} %get-tuple-element.30), channel_id=1, source_target_pairs={{0,16},{16,32},{32,48},{48,64},{64,80},{80,96},{96,112},{1,17},{17... | collective-permute-start | bytes 1572872 | tf_op jit(solution)/shard_map/ppermute | solution.py:600
  86.5 5.9 %collective-permute-start.7 = (bf16[12,16,256]{2,1,0:T(8,128)(2,1)S(1)}, bf16[12,16,256]{2,1,0:T(8,128)(2,1)S(1)}, u32[]{:S(2)}, u32[]{:S(2)}) collective-permute-start(bf16[12,16,256]{2,1,0:T(8,128)(2,1)S(1)} %get-tuple-element.33), channel_id=1, source_target_pairs={{16,0},{32,16},{48,32},{64,48},{80,64},{96,80},{112,96},{17,1},{33... | collective-permute-start | bytes 294920 | tf_op jit(solution)/shard_map/ppermute | solution.py:609
  90.2 5.9 %collective-permute-start.6 = (bf16[12,16,256]{2,1,0:T(8,128)(2,1)S(1)}, bf16[12,16,256]{2,1,0:T(8,128)(2,1)S(1)}, u32[]{:S(2)}, u32[]{:S(2)}) collective-permute-start(bf16[12,16,256]{2,1,0:T(8,128)(2,1)S(1)} %get-tuple-element.34), channel_id=1, source_target_pairs={{0,16},{16,32},{32,48},{48,64},{64,80},{80,96},{96,112},{1,17},{17... | collective-permute-start | bytes 294920 | tf_op jit(solution)/shard_map/ppermute | solution.py:608
  134.3 65.6 %copy-start.1 = (bf16[4,16,64,128]{3,2,1,0:T(8,128)(2,1)S(1)}, bf16[4,16,64,128]{3,2,1,0:T(8,128)(2,1)}, u32[]{:S(2)}) copy-start(bf16[4,16,64,128]{3,2,1,0:T(8,128)(2,1)} %param.7) | copy-start | bytes 3145732
  134.3 65.6 %all-to-all-start.1 = ((bf16[128,128,128]{2,1,0:T(8,128)(2,1)}), bf16[128,128,128]{2,1,0:T(8,128)(2,1)}, u32[]{:S(2)}, u32[]{:S(2)}) async-start(bf16[128,128,128]{2,1,0:T(8,128)(2,1)} %get-tuple-element.20), calls=%async_computation.1 | async-start | bytes 8388608 | tf_op jit(solution)/shard_map/all_to_all | solution.py:615
  146.7 53.2 %copy-start = (bf16[4,16,128,128]{3,2,1,0:T(8,128)(2,1)S(1)}, bf16[4,16,128,128]{3,2,1,0:T(8,128)(2,1)}, u32[]{:S(2)}) copy-start(bf16[4,16,128,128]{3,2,1,0:T(8,128)(2,1)} %param.8) | copy-start | bytes 6291460
